TPU v7x, 256 devices: a whole 4x4x8 slice. The times are simulated.
256 devices in a mesh: dp: 64 (over z, x, core), mp: 4 (over y).
Axes of the slice: x: 4, y: 4, z: 8, core: 2. Of those that a mesh axis runs over, the one named last changes fastest.
Arguments:
- hidden: bfloat16 [64, 512, 4608], P('dp', 'mp'), may hold values from -6 to 6
- lengths: int32 [64], P('dp'), may hold values from 64 to 512
- norm_gain: float32 [4608], replicated, may hold values from 0.25 to 1.75
- w_query: bfloat16 [4608, 2048], P('dp', 'mp'), may hold values from -0.09375 to 0.09375
- w_key: bfloat16 [4608, 1024], P('dp', 'mp'), may hold values from -0.09375 to 0.09375
- w_value: bfloat16 [4608, 1024], P('dp', 'mp'), may hold values from -0.09375 to 0.09375
- w_out: bfloat16 [2048, 4608], P('mp', 'dp'), may hold values from -0.125 to 0.125
- post_gain: float32 [4608], replicated, may hold values from 0.25 to 1.75
Outputs:
- mixed: bfloat16 [64, 512, 4608], P('dp', 'mp')
- key_cache: bfloat16 [64, 512, 1024], P('dp', None, 'mp')
- value_cache: bfloat16 [64, 512, 1024], P('dp', None, 'mp')
All inputs are finite; a program needn't handle non-finite values.
Results may differ from a plain program's by a relative error of at most 0.01.
Values may be sent and summed in bfloat16 or wider, within the bound.
No kernel may reach another device: no remote copies, remote signals or barrier semaphores. Data moves between devices by JAX's collectives and lax.ppermute only.
A program may use at most 128 MiB of HBM per device.

v0:
```python
import functools

import jax
import jax.numpy as jnp
from jax import lax
from jax.experimental import pallas as pl
from jax.experimental.pallas import tpu as pltpu
from jax.sharding import PartitionSpec as P


HD = 128
NZ, NX, NY = 8, 4, 4
F32 = jnp.float32
BF16 = jnp.bfloat16
ANY = pl.BlockSpec(memory_space=pl.ANY)
SMALL_LIMIT = 24 * 1024 * 1024


def spot(z, x, c):
    return ((z % NZ) * NX + (x % NX)) * 2 + c


def plane(array, dz=0, dx=0, dc=0):
    pairs = [
        (spot(z, x, c), spot(z + dz, x + dx, c ^ dc))
        for z in range(NZ)
        for x in range(NX)
        for c in range(2)
    ]
    return lax.ppermute(array, "dp", pairs)


def column(array, dy):
    return lax.ppermute(array, "mp", [(y, (y + dy) % NY) for y in range(NY)])


def norm_kernel(rows_ref, gain_ref, out_ref):
    rows = rows_ref[...].astype(F32)
    mean = jnp.mean(rows * rows, axis=-1, keepdims=True)
    out_ref[...] = (rows * lax.rsqrt(mean + 1e-06) * gain_ref[...]).astype(BF16)


def normed_rows(hidden, gain):
    rows, width = hidden.shape
    step = 64
    return pl.pallas_call(
        norm_kernel,
        grid=(rows // step,),
        in_specs=[
            pl.BlockSpec((step, width), lambda i: (i, 0)),
            pl.BlockSpec((width,), lambda i: (0,)),
        ],
        out_specs=pl.BlockSpec((step, width), lambda i: (i, 0)),
        out_shape=jax.ShapeDtypeStruct(hidden.shape, BF16),
        name="norm",
        cost_estimate=pl.CostEstimate(flops=2_000_000, bytes_accessed=2_400_000, transcendentals=128),
    )(hidden, gain)


def attended(scal, dy, q_ref, k_ref, v_ref, store):
    y, length = scal[3], scal[4]
    first = pl.multiple_of(lax.rem(y + dy, NY) * 128, 128)
    row = lax.broadcasted_iota(jnp.int32, (128, 512), 0) + first
    col = lax.broadcasted_iota(jnp.int32, (128, 512), 1)
    keep = (col <= row) & (col < length)
    for h in range(4):
        kv = slice((h // 2) * 128, (h // 2) * 128 + 128)
        score = lax.dot_general(
            q_ref[pl.ds(first, 128), h * 128 : h * 128 + 128],
            k_ref[:, kv],
            (((1,), (1,)), ((), ())),
            preferred_element_type=F32,
        )
        score = 50.0 * jnp.tanh(score * (1.0 / 50.0))
        score = jnp.where(keep, score, -1e30)
        top = jnp.max(score, axis=-1, keepdims=True)
        expo = jnp.exp(score - top)
        weights = (expo / jnp.sum(expo, axis=-1, keepdims=True)).astype(BF16)
        store(h, jnp.dot(weights, v_ref[:, kv], preferred_element_type=F32).astype(BF16))


def spread(att, wo, outs, width, chunk=1152):
    for at in range(0, width, chunk):
        partial = lax.dot_general(
            att[...], wo[at : at + chunk, :], (((1,), (1,)), ((), ())), preferred_element_type=F32
        )
        for ref, first in outs:
            ref[:, at : at + chunk] = partial[first : first + ref.shape[0]].astype(ref.dtype)


def start(pairs, sem):
    for src, dst in pairs:
        pltpu.make_async_copy(src, dst, sem).start()


def finished(target, rows, sem):
    part = target.at[pl.ds(0, rows)]
    pltpu.make_async_copy(part, part, sem).wait()


def rows_of(xbuf, y, dy, first, count):
    return xbuf.at[pl.ds(pl.multiple_of(lax.rem(y + dy, NY) * 128 + first, 64), count)]


def shards_of(ref, table, wbuf, base):
    for j in range(ref.shape[0]):
        yield ref.at[j], wbuf.at[pl.ds(pl.multiple_of(table[base + j], 8), 72)]


def fill_kernel(offsets, groups, n_old, scal, table, *refs):
    c, y = scal[2], scal[3]
    xs, refs = refs[: len(offsets)], refs[len(offsets) :]
    ws, refs = refs[: len(groups)], refs[len(groups) :]
    either, (xbuf, wbuf, sem) = refs[:-3][: -n_old or None], refs[-3:]

    for ref, at in zip(xs, offsets):
        pltpu.make_async_copy(ref, rows_of(xbuf, y, *at, ref.shape[0]), sem.at[0]).start()
    for ref, group in zip(ws, groups):
        start(shards_of(ref, table, wbuf, group * 4), sem.at[1])
    if either:
        for core, ref, base in ((0, either[0], 28), (1, either[1], 60)):

            @pl.when(c == core)
            def _():
                start(shards_of(ref, table, wbuf, base), sem.at[1])

    if xs:
        finished(xbuf, sum(ref.shape[0] for ref in xs), sem.at[0])
    finished(wbuf, 72 * 4 * (len(groups) + bool(either)), sem.at[1])


VMEM = pl.BlockSpec(memory_space=pltpu.VMEM)
SMEM = pl.BlockSpec(memory_space=pltpu.SMEM)


def fill(scal, table, xs, offsets, ws, groups, either, held, width):
    operands = [scal, table, *xs, *ws, *either, *held]
    n = len(operands)
    return pl.pallas_call(
        functools.partial(fill_kernel, offsets, groups, len(held)),
        in_specs=[SMEM] * 2 + [ANY] * (n - 2 - len(held)) + [VMEM] * len(held),
        out_specs=[VMEM] * 2,
        out_shape=[pltpu.VMEM((512, width), BF16), pltpu.VMEM((width, 1536), BF16)],
        scratch_shapes=[pltpu.SemaphoreType.DMA((2,))],
        input_output_aliases={n - 2: 0, n - 1: 1} if held else {},
        compiler_params=pltpu.CompilerParams(vmem_limit_bytes=SMALL_LIMIT),
        cost_estimate=pl.CostEstimate(flops=0, bytes_accessed=18_000_000, transcendentals=0),
    )(*operands)


def turned(raw, cos_ref, sin_ref, first, count):
    rows = pl.ds(first, count)
    return raw * cos_ref[rows, :] + pltpu.roll(raw, 64, 1) * sin_ref[rows, :]


def queries(scal, dy, xbuf, wbuf, cos_ref, sin_ref, q, slot):
    first = pl.multiple_of(lax.rem(scal[3] + dy, NY) * 128, 128)
    raw = jnp.dot(xbuf[pl.ds(first, 128), :], wbuf[:, 0:512], preferred_element_type=F32)
    for h in range(4):
        one = turned(raw[:, h * 128 : h * 128 + 128], cos_ref, sin_ref, first, 128)
        q[pl.ds(slot * 128, 128), h * 128 : h * 128 + 128] = (one * 144.0 ** (-0.5)).astype(BF16)


def attended(scal, dy, q, slot, k_ref, v_ref, att):
    y, length = scal[3], scal[4]
    first = lax.rem(y + dy, NY) * 128
    row = lax.broadcasted_iota(jnp.int32, (128, 512), 0) + first
    col = lax.broadcasted_iota(jnp.int32, (128, 512), 1)
    keep = (col <= row) & (col < length)
    mine = pl.ds(slot * 128, 128)
    for h in range(4):
        kv = slice((h // 2) * 128, (h // 2) * 128 + 128)
        head = slice(h * 128, h * 128 + 128)
        score = lax.dot_general(
            q[mine, head], k_ref[:, kv], (((1,), (1,)), ((), ())), preferred_element_type=F32
        )
        score = 50.0 * jnp.tanh(score * (1.0 / 50.0))
        score = jnp.where(keep, score, -1e30)
        top = jnp.max(score, axis=-1, keepdims=True)
        expo = jnp.exp(score - top)
        weights = (expo / jnp.sum(expo, axis=-1, keepdims=True)).astype(BF16)
        att[mine, head] = jnp.dot(weights, v_ref[:, kv], preferred_element_type=F32).astype(BF16)


def spread(att, wbuf, outs, chunk=1152):
    for at in range(0, wbuf.shape[0], chunk):
        partial = lax.dot_general(
            att[...], wbuf[at : at + chunk, 1024:1536], (((1,), (1,)), ((), ())), preferred_element_type=F32
        )
        for ref, first in outs:
            ref[:, at : at + chunk] = partial[first : first + ref.shape[0]].astype(ref.dtype)


def project_kernel(
    scal, table, cos_ref, sin_ref, up_own, down_own, up_other, down_other, xbuf, old,
    k_ref, v_ref, far0, far1, wbuf, q, att, sem,
):
    c, length = scal[2], scal[4]

    for core, halves, base in ((0, (up_other, down_other), 60), (1, (up_own, down_own), 28)):

        @pl.when(c == core)
        def _():
            for i, ref in enumerate(halves):
                start(shards_of(ref, table, wbuf, base + 2 * i), sem)

    finished(wbuf, 72 * 4, sem)
    live = lax.broadcasted_iota(jnp.int32, (512, 128), 0) < length
    raw = jnp.dot(xbuf[...], wbuf[:, 512:768], preferred_element_type=F32)
    for h in range(2):
        head = slice(h * 128, h * 128 + 128)
        k_ref[:, head] = jnp.where(live, turned(raw[:, head], cos_ref, sin_ref, 0, 512), 0.0).astype(BF16)
    raw = jnp.dot(xbuf[...], wbuf[:, 768:1024], preferred_element_type=F32)
    for h in range(2):
        head = slice(h * 128, h * 128 + 128)
        v_ref[:, head] = jnp.where(live, raw[:, head], 0.0).astype(BF16)
    queries(scal, 2, xbuf, wbuf, cos_ref, sin_ref, q, 0)
    attended(scal, 2, q, 0, k_ref, v_ref, att)
    spread(att, wbuf, ((far0, 0), (far1, 64)))


def project(scal, table, cosine, sine, arrays, xbuf, wbuf):
    width = wbuf.shape[0]
    outs = [(512, 256), (512, 256), (64, width), (64, width)]
    n = 4 + len(arrays)
    return pl.pallas_call(
        project_kernel,
        in_specs=[SMEM] * 2 + [VMEM] * 2 + [ANY] * len(arrays) + [VMEM] * 2,
        out_specs=[VMEM] * 5,
        out_shape=[jax.ShapeDtypeStruct(shape, BF16) for shape in outs] + [pltpu.VMEM(wbuf.shape, BF16)],
        scratch_shapes=[
            pltpu.VMEM((128, 512), BF16),
            pltpu.VMEM((128, 512), BF16),
            pltpu.SemaphoreType.DMA,
        ],
        input_output_aliases={n + 1: 4},
        compiler_params=pltpu.CompilerParams(vmem_limit_bytes=SMALL_LIMIT),
        name="project",
        cost_estimate=pl.CostEstimate(flops=4_000_000_000, bytes_accessed=10_000_000, transcendentals=524_288),
    )(scal, table, cosine, sine, *arrays, xbuf, wbuf)


def attend_kernel(blocks, outs, scal, cos_ref, sin_ref, k_ref, v_ref, xbuf, wbuf, *refs):
    out_refs, (q, att) = refs[:-2], refs[-2:]
    stride = blocks[-1] - blocks[0]

    def block(slot, carry):
        dy = blocks[0] + slot * stride
        queries(scal, dy, xbuf, wbuf, cos_ref, sin_ref, q, slot)
        attended(scal, dy, q, slot, k_ref, v_ref, att)
        return carry

    lax.fori_loop(0, len(blocks), block, 0)
    chunk = 1152

    def stretch(i, carry):
        at = pl.multiple_of(i * chunk, 128)
        partial = lax.dot_general(
            att[...], wbuf[pl.ds(at, chunk), 1024:1536], (((1,), (1,)), ((), ())), preferred_element_type=F32
        )
        for ref, first in zip(out_refs, outs):
            ref[:, pl.ds(at, chunk)] = partial[first : first + ref.shape[0]].astype(ref.dtype)
        return carry

    lax.fori_loop(0, wbuf.shape[0] // chunk, stretch, 0)


def attend(scal, cosine, sine, key, value, xbuf, wbuf, blocks, outs, count):
    width = wbuf.shape[0]
    n = len(blocks)
    return pl.pallas_call(
        functools.partial(attend_kernel, blocks, outs),
        in_specs=[SMEM] + [VMEM] * 6,
        out_specs=[VMEM] * len(outs),
        out_shape=[jax.ShapeDtypeStruct((count, width), BF16)] * len(outs),
        scratch_shapes=[pltpu.VMEM((n * 128, 512), BF16)] * 2,
        compiler_params=pltpu.CompilerParams(vmem_limit_bytes=SMALL_LIMIT),
        cost_estimate=pl.CostEstimate(
            flops=n * 1_400_000_000, bytes_accessed=1_000_000 + n * 1_200_000, transcendentals=n * 524_288
        ),
    )(scal, cosine, sine, key, value, xbuf, wbuf)


def finish_kernel(scal, rows_ref, own_ref, a1, b0, gain_ref, a0_hbm, b1_hbm, out_hbm, a0, b1, out, sem, osem):
    y, length = scal[3], scal[4]
    first = pltpu.make_async_copy(a0_hbm, a0, sem.at[0])
    second = pltpu.make_async_copy(b1_hbm, b1, sem.at[1])
    first.start()
    second.start()
    gain = gain_ref[...]
    count = 32
    for i in range(4):
        if i % 2 == 0:
            (first, second)[i // 2].wait()
        rows = slice(i * count, i * count + count)
        here = slice(i % 2 * count, i % 2 * count + count)
        before, after = ((a0, b0), (a1, b1))[i // 2]
        total = own_ref[rows, :].astype(F32) + before[here, :].astype(F32) + after[here, :].astype(F32)
        mean = jnp.mean(total * total, axis=-1, keepdims=True)
        post = total * lax.rsqrt(mean + 1e-06) * gain
        row = lax.broadcasted_iota(jnp.int32, (count, 1), 0) + y * 128 + i * count
        out[rows, :] = jnp.where(row < length, rows_ref[rows, :].astype(F32) + post, 0.0).astype(BF16)
        pltpu.make_async_copy(out.at[rows], out_hbm.at[rows], osem).start()
    pltpu.make_async_copy(out, out_hbm, osem).wait()


def finish(scal, hidden, own, a0, a1, b0, b1, gain):
    width = hidden.shape[-1]
    return pl.pallas_call(
        finish_kernel,
        in_specs=[SMEM] + [VMEM] * 5 + [ANY] * 2,
        out_specs=ANY,
        out_shape=jax.ShapeDtypeStruct(hidden.shape, BF16),
        scratch_shapes=[
            pltpu.VMEM((64, width), BF16),
            pltpu.VMEM((64, width), BF16),
            pltpu.VMEM(hidden.shape, BF16),
            pltpu.SemaphoreType.DMA((2,)),
            pltpu.SemaphoreType.DMA,
        ],
        compiler_params=pltpu.CompilerParams(vmem_limit_bytes=SMALL_LIMIT),
        name="finish",
        cost_estimate=pl.CostEstimate(flops=6_000_000, bytes_accessed=7_000_000, transcendentals=128),
    )(scal, hidden, own, a1, b0, gain, a0, b1)


def angle_tables(maxlen):
    half = HD // 2
    freqs = 10000.0 ** (-jnp.arange(half, dtype=F32) / half)
    angles = jnp.arange(maxlen, dtype=jnp.int32).astype(F32)[:, None] * freqs[None, :]
    cosine, sine = jnp.cos(angles), jnp.sin(angles)
    return jnp.concatenate([cosine, cosine], -1), jnp.concatenate([-sine, sine], -1)


def torus(array, d, cores=(0, 1)):
    pairs = [
        (spot(z, x, c), spot(z + d[c][0], x + d[c][1], c))
        for z in range(NZ)
        for x in range(NX)
        for c in cores
    ]
    return lax.ppermute(array, "dp", pairs)


def one_way(array, source):
    pairs = [(spot(z, x, source), spot(z, x, 1 - source)) for z in range(NZ) for x in range(NX)]
    return lax.ppermute(array, "dp", pairs)


def swapped(array):
    return plane(array, dc=1)


SMALL_UP, SMALL_DOWN = ((1, 0), (0, 1)), ((-1, 0), (0, -1))
LARGE_UP, LARGE_DOWN = ((0, 1), (1, 0)), ((0, -1), (-1, 0))
NEAR, FAR = (0, -1, 1, -2), (2, -3, 3, 4)


def wrapped(dz, dx):
    return dz % NZ, dx % NX


PLACES_A = tuple(
    tuple(wrapped(dz, dx) for dz in zs)
    for zs, dx in ((NEAR, 0), (NEAR, -1), (NEAR, 1), (FAR, -1), (FAR, 1), (FAR, -2), (NEAR, 2), (FAR, 0))
)
PLACES_B = tuple(
    tuple(wrapped(dz, dx) for dx in NEAR) for dz in (0, -1, 1, -2, 2, -3, 3, -4)
)


def row_table(z, x, core):
    places = jnp.array([PLACES_A, PLACES_B], jnp.int32)
    rows = []
    for dc in range(2):
        owner = (core + dc) % 2
        mine = jnp.where(owner == 0, places[0], places[1])
        rows.append((((z + mine[..., 0]) % NZ * NX + (x + mine[..., 1]) % NX) * 2 + owner) * 72)
    return jnp.stack(rows).reshape(-1).astype(jnp.int32)


def gathered_weights(shard, core, tables):
    first = core == 0
    s1 = torus(shard, SMALL_UP)
    s2 = torus(shard, SMALL_DOWN)
    s3 = torus(s1, SMALL_UP)
    s4 = torus(s2, SMALL_DOWN)
    s5 = torus(s3, SMALL_UP)
    s6 = torus(s4, SMALL_DOWN)
    s7 = torus(s6, SMALL_DOWN)
    near = jnp.stack([shard, s1, s2, s3])
    r1 = torus(near, LARGE_UP)
    r2 = torus(near, LARGE_DOWN)
    r2, *angles = lax.optimization_barrier((r2, *tables[2:]))
    tables = (*tables[:2], *angles)
    far = jnp.stack([s4, s5, s6, s7])
    r3 = torus(jnp.where(first, far, r1), LARGE_UP)
    r4 = torus(jnp.where(first, far, r2), LARGE_DOWN)
    r5 = torus(r3, LARGE_UP)
    r6 = torus(jnp.where(first, *lax.optimization_barrier((r2, r4))), LARGE_DOWN)
    r7 = torus(r5[:2], LARGE_UP, (1,))
    r8 = torus(r6[2:], LARGE_DOWN, (1,))
    arrays = [near, r1, r2, r3, r4, r5, r6]
    others = [swapped(a) for a in arrays]
    far = far, one_way(far, 0)
    up = r7, one_way(r7, 1)
    down = r8, one_way(r8, 1)
    return arrays, others, far, up, down, tables


def layer(hidden, lengths, norm_gain, w_query, w_key, w_value, w_out, post_gain):
    _, local_len, width = hidden.shape
    hidden = hidden.reshape(local_len, width)
    place = lax.axis_index("dp")
    core = place % 2
    scal = jnp.stack([place // 8, (place // 2) % 4, core, lax.axis_index("mp"), lengths[0]]).astype(jnp.int32)
    shard = jnp.concatenate([w_query, w_key, w_value, w_out.T], axis=1)
    normed = normed_rows(hidden, norm_gain)
    above, below = column(normed, -1), column(normed, 1)
    across0 = column(above[:64], -1)
    across1 = column(below[64:], 1)
    tables = (scal, row_table(scal[0], scal[1], core), *angle_tables(local_len * NY))
    arrays, others, far, up, down, tables = gathered_weights(shard, core, tables)
    scal, table, cosine, sine = tables
    held = fill(scal, table, [normed], ((0, 0),), arrays[:1], (0,), (), (), width)
    held = fill(
        scal, table, [above, below], ((1, 0), (3, 0)), arrays[1:5] + others[:3],
        (1, 2, 3, 4, 8, 9, 10), far, held, width,
    )
    held = fill(
        scal, table, [across0, across1], ((2, 0), (2, 64)), arrays[5:] + others[3:5],
        (5, 6, 11, 12), (), held, width,
    )
    xbuf, wbuf = fill(scal, table, [], (), others[5:], (13, 14), (), held, width)
    rest = [up[0], down[0], up[1], down[1]]
    key, value, far0, far1, wbuf = project(scal, table, cosine, sine, rest, xbuf, wbuf)
    rfar0, rfar1 = column(far0, 1), column(far1, -1)
    up0, up1, down0, down1 = attend(scal, cosine, sine, key, value, xbuf, wbuf, (1, 3), (0, 64, 128, 192), 64)
    a1, b0 = column(up1, 1), column(down0, -1)
    (own,) = attend(scal, cosine, sine, key, value, xbuf, wbuf, (0,), (0,), 128)
    a0 = column((up0.astype(F32) + rfar0.astype(F32)).astype(BF16), 1)
    b1 = column((down1.astype(F32) + rfar1.astype(F32)).astype(BF16), -1)
    mixed = finish(scal, hidden, own, a0, a1, b0, b1, post_gain)
    return mixed[None], key[None], value[None]


def solution(mesh):
    return jax.shard_map(
        layer,
        mesh=mesh,
        in_specs=(
            P("dp", "mp", None),
            P("dp"),
            P(),
            P("dp", "mp"),
            P("dp", "mp"),
            P("dp", "mp"),
            P("mp", "dp"),
            P(),
        ),
        out_specs=(P("dp", "mp", None), P("dp", None, "mp"), P("dp", None, "mp")),
        check_vma=False,
    )
```

profile of v0, /device:TPU:1, one launch (start us, length us, event | category | flops | bytes accessed | tf_op | source)
XLA Modules:
  0.0 220.9 jit_solution(7492318094475719893)
XLA Ops:
  1.6 2.1 collective-permute-start
  3.7 1.4 collective-permute-start.1
  5.1 3.2 %collective-permute-done = bf16[72,1536]{1,0:T(8,128)(2,1)S(1)} collective-permute-done((bf16[72,1536]{1,0:T(8,128)(2,1)S(1)}, bf16[72,1536]{1,0:T(8,128)(2,1)S(1)}, u32[]{:S(2)}, u32[]{:S(2)}) %collective-permute-start) | collective-permute-done | bytes 221216 | tf_op jit(solution)/shard_map/ppermute | solution.py:342
  8.8 5.5 %collective-permute-done.2 = bf16[72,1536]{1,0:T(8,128)(2,1)S(1)} collective-permute-done((bf16[72,1536]{1,0:T(8,128)(2,1)S(1)}, bf16[72,1536]{1,0:T(8,128)(2,1)S(1)}, u32[]{:S(2)}, u32[]{:S(2)}) %collective-permute-start.2) | collective-permute-done | bytes 221216 | tf_op jit(solution)/shard_map/ppermute | solution.py:342
  14.4 6.1 %collective-permute-start.3 = (bf16[4,72,1536]{2,1,0:T(8,128)(2,1)S(1)}, bf16[4,72,1536]{2,1,0:T(8,128)(2,1)S(1)}, u32[]{:S(2)}, u32[]{:S(2)}) collective-permute-start(bf16[4,72,1536]{2,1,0:T(8,128)(2,1)S(1)} %pad_maximum_fusion.refs_1_), channel_id=1, source_target_pairs={{0,24},{4,228},{8,0},{12,236},{16,8},{20,244},{24,16},{28,252},{32... | collective-permute-start | bytes 2654216 | tf_op jit(solution)/shard_map/ppermute | solution.py:342
  20.9 7.0 %collective-permute-done.4 = bf16[72,1536]{1,0:T(8,128)(2,1)S(1)} collective-permute-done((bf16[72,1536]{1,0:T(8,128)(2,1)S(1)}, bf16[72,1536]{1,0:T(8,128)(2,1)S(1)}, u32[]{:S(2)}, u32[]{:S(2)}) %collective-permute-start.4) | collective-permute-done | bytes 221216 | tf_op jit(solution)/shard_map/ppermute | solution.py:342
  28.0 1.5 collective-permute-start.5
  29.5 6.0 %collective-permute-done.6 = bf16[72,1536]{1,0:T(8,128)(2,1)} collective-permute-done((bf16[72,1536]{1,0:T(8,128)(2,1)S(1)}, bf16[72,1536]{1,0:T(8,128)(2,1)}, u32[]{:S(2)}, u32[]{:S(2)}) %collective-permute-start.6) | collective-permute-done | bytes 221216 | tf_op jit(solution)/shard_map/ppermute | solution.py:342
  37.9 3.0 %collective-permute-done.7 = bf16[72,1536]{1,0:T(8,128)(2,1)} collective-permute-done((bf16[72,1536]{1,0:T(8,128)(2,1)}, bf16[72,1536]{1,0:T(8,128)(2,1)}, u32[]{:S(2)}, u32[]{:S(2)}) %collective-permute-start.7) | collective-permute-done | bytes 221216 | tf_op jit(solution)/shard_map/ppermute | solution.py:342
  40.9 3.2 %pad_maximum_fusion.1 = (bf16[4,72,1536]{2,1,0:T(8,128)(2,1)}, bf16[4,72,1536]{2,1,0:T(8,128)(2,1)}, bf16[4,72,1536]{2,1,0:T(8,128)(2,1)}) fusion(bf16[1,72,1536]{2,1,0:T(8,128)(2,1)} %bitcast.19, bf16[1,72,1536]{2,1,0:T(8,128)(2,1)} %bitcast.18, bf16[1,72,1536]{2,1,0:T(8,128)(2,1)} %bitcast.17, bf16[1,72,1536]{2,1,0:T(8,128)(2,1)S(1)} %bitcast.54, ...), kind=kLoop, calls=%fused_computation.3 | loop fusion | flops 2211840 | bytes 5308417 | tf_op jit(solution)/shard_map/stack | solution.py:396
  44.1 3.2 %collective-permute-start.12 = (bf16[4,72,1536]{2,1,0:T(8,128)(2,1)}, bf16[4,72,1536]{2,1,0:T(8,128)(2,1)S(1)}, u32[]{:S(2)}, u32[]{:S(2)}) collective-permute-start(bf16[4,72,1536]{2,1,0:T(8,128)(2,1)} %get-tuple-element.49), channel_id=1, source_target_pairs={{0,24},{4,228},{8,0},{12,236},{16,8},{20,244},{24,16},{28,252},{32... | collective-permute-start | bytes 2654216 | tf_op jit(solution)/shard_map/ppermute | solution.py:342
  47.2 2.5 %norm.1.refs_0_ = bf16[128,4608]{1,0:T(8,128)(2,1)} custom-call(bf16[128,4608]{1,0:T(8,128)(2,1)} %bitcast.46, f32[4608]{0:T(1024)} %gain_ref.2), custom_call_target="tpu_custom_call" | custom-call | flops 2000000 | bytes 2400000 | tf_op jit(solution)/shard_map/norm/pallas_call | solution.py:46
  49.8 2.7 %collective-permute-start.19 = (bf16[128,4608]{1,0:T(8,128)(2,1)}, bf16[128,4608]{1,0:T(8,128)(2,1)S(1)}, u32[]{:S(2)}, u32[]{:S(2)}) collective-permute-start(bf16[128,4608]{1,0:T(8,128)(2,1)} %norm.1.refs_0_), channel_id=1, source_target_pairs={{0,3},{1,0},{2,1},{3,2},{4,7},{5,4},{6,5},{7,6},{8,11},{9,8},{10,9... | collective-permute-start | bytes 3538952 | tf_op jit(solution)/shard_map/ppermute | solution.py:34
  52.5 3.8 %collective-permute-start.25 = (bf16[4,72,1536]{2,1,0:T(8,128)(2,1)S(1)}, bf16[4,72,1536]{2,1,0:T(8,128)(2,1)S(1)}, u32[]{:S(2)}, u32[]{:S(2)}) collective-permute-start(bf16[4,72,1536]{2,1,0:T(8,128)(2,1)S(1)} %pad_maximum_fusion.refs_1_), channel_id=1, source_target_pairs={{0,4},{4,0},{8,12},{12,8},{16,20},{20,16},{24,28},{28,24},{32,36},... | collective-permute-start | bytes 2654216 | tf_op jit(solution)/shard_map/ppermute | solution.py:30
  56.3 1.2 collective-permute-done.12.refs_5_
  57.6 3.1 %collective-permute-start.13 = (bf16[4,72,1536]{2,1,0:T(8,128)(2,1)S(1)}, bf16[4,72,1536]{2,1,0:T(8,128)(2,1)}, u32[]{:S(2)}, u32[]{:S(2)}) collective-permute-start(bf16[4,72,1536]{2,1,0:T(8,128)(2,1)S(1)} %broadcast_select_fusion), channel_id=1, source_target_pairs={{0,24},{4,228},{8,0},{12,236},{16,8},{20,244},{24,16},{28,252},{32... | collective-permute-start | bytes 2654216 | tf_op jit(solution)/shard_map/ppermute | solution.py:342
  60.7 5.4 %collective-permute-done.9.refs_4_ = bf16[4,72,1536]{2,1,0:T(8,128)(2,1)S(1)} collective-permute-done((bf16[4,72,1536]{2,1,0:T(8,128)(2,1)}, bf16[4,72,1536]{2,1,0:T(8,128)(2,1)S(1)}, u32[]{:S(2)}, u32[]{:S(2)}) %collective-permute-start.9) | collective-permute-done | bytes 884768 | tf_op jit(solution)/shard_map/ppermute | solution.py:342
  66.1 8.8 %collective-permute-done.19.refs_0_ = bf16[128,4608]{1,0:T(8,128)(2,1)S(1)} collective-permute-done((bf16[128,4608]{1,0:T(8,128)(2,1)}, bf16[128,4608]{1,0:T(8,128)(2,1)S(1)}, u32[]{:S(2)}, u32[]{:S(2)}) %collective-permute-start.19) | collective-permute-done | bytes 1179680 | tf_op jit(solution)/shard_map/ppermute | solution.py:34
  75.0 3.5 %collective-permute-start.20 = (bf16[64,4608]{1,0:T(8,128)(2,1)S(1)}, bf16[64,4608]{1,0:T(8,128)(2,1)S(1)}, u32[]{:S(2)}, u32[]{:S(2)}) collective-permute-start(bf16[64,4608]{1,0:T(8,128)(2,1)S(1)} %slice.48), channel_id=1, source_target_pairs={{0,3},{1,0},{2,1},{3,2},{4,7},{5,4},{6,5},{7,6},{8,11},{9,8},{10,9... | collective-permute-start | bytes 1769480 | tf_op jit(solution)/shard_map/ppermute | solution.py:34
  78.5 1.3 collective-permute-start.28
  79.8 4.4 %collective-permute-start.27 = (bf16[4,72,1536]{2,1,0:T(8,128)(2,1)S(1)}, bf16[4,72,1536]{2,1,0:T(8,128)(2,1)S(1)}, u32[]{:S(2)}, u32[]{:S(2)}) collective-permute-start(bf16[4,72,1536]{2,1,0:T(8,128)(2,1)S(1)} %collective-permute-done.3.refs_3_), channel_id=1, source_target_pairs={{0,4},{4,0},{8,12},{12,8},{16,20},{20,16},{24,28},{28,24},{32,36},... | collective-permute-start | bytes 2654216 | tf_op jit(solution)/shard_map/ppermute | solution.py:30
  84.2 3.0 %collective-permute-done.20.refs_0_ = bf16[64,4608]{1,0:T(8,128)(2,1)S(1)} collective-permute-done((bf16[64,4608]{1,0:T(8,128)(2,1)S(1)}, bf16[64,4608]{1,0:T(8,128)(2,1)S(1)}, u32[]{:S(2)}, u32[]{:S(2)}) %collective-permute-start.20) | collective-permute-done | bytes 589856 | tf_op jit(solution)/shard_map/ppermute | solution.py:34
  88.0 4.8 %collective-permute-start.26 = (bf16[4,72,1536]{2,1,0:T(8,128)(2,1)}, bf16[4,72,1536]{2,1,0:T(8,128)(2,1)S(1)}, u32[]{:S(2)}, u32[]{:S(2)}) collective-permute-start(bf16[4,72,1536]{2,1,0:T(8,128)(2,1)} %collective-permute-done.8.refs_2_), channel_id=1, source_target_pairs={{0,4},{4,0},{8,12},{12,8},{16,20},{20,16},{24,28},{28,24},{32,36},... | collective-permute-start | bytes 2654216 | tf_op jit(solution)/shard_map/ppermute | solution.py:30
  93.4 1.8 slice.47
  95.2 1.8 slice.46
  97.0 12.7 %collective-permute-done.22.refs_1_ = bf16[64,4608]{1,0:T(8,128)(2,1)S(1)} collective-permute-done((bf16[64,4608]{1,0:T(8,128)(2,1)S(1)}, bf16[64,4608]{1,0:T(8,128)(2,1)S(1)}, u32[]{:S(2)}, u32[]{:S(2)}) %collective-permute-start.22) | collective-permute-done | bytes 589856 | tf_op jit(solution)/shard_map/ppermute | solution.py:34
  110.5 3.1 %collective-permute-start.14 = (bf16[2,72,1536]{2,1,0:T(8,128)(2,1)}, bf16[2,72,1536]{2,1,0:T(8,128)(2,1)}, u32[]{:S(2)}, u32[]{:S(2)}) collective-permute-start(bf16[2,72,1536]{2,1,0:T(8,128)(2,1)} %slice.47), channel_id=1, source_target_pairs={{4,228},{12,236},{20,244},{28,252},{36,4},{44,12},{52,20},{60,28},... | collective-permute-start | bytes 1327112 | tf_op jit(solution)/shard_map/ppermute | solution.py:342
  114.6 2.2 collective-permute-start.11
  120.1 3.2 %collective-permute-start.16 = (bf16[2,72,1536]{2,1,0:T(8,128)(2,1)}, bf16[2,72,1536]{2,1,0:T(8,128)(2,1)}, u32[]{:S(2)}, u32[]{:S(2)}) collective-permute-start(bf16[2,72,1536]{2,1,0:T(8,128)(2,1)} %collective-permute-done.14.down_own), channel_id=1, source_target_pairs={{4,0},{12,8},{20,16},{28,24},{36,32},{44,40},{52,48},{60,56},{68,6... | collective-permute-start | bytes 1327112 | tf_op jit(solution)/shard_map/ppermute | solution.py:347
  123.2 1.9 collective-permute-done.11.up_own
  125.1 2.1 collective-permute-start.15
  129.4 2.0 shard_map.112
  131.4 5.0 %copy-done = bf16[4608,1536]{1,0:T(8,128)(2,1)} copy-done((bf16[4608,1536]{1,0:T(8,128)(2,1)}, bf16[4608,1536]{1,0:T(8,128)(2,1)S(1)}, u32[]{:S(2)}) %copy-start) | copy-done | bytes 14155800
  136.4 5.0 %copy-done.1 = bf16[4608,1536]{1,0:T(8,128)(2,1)S(1)} copy-done((bf16[4608,1536]{1,0:T(8,128)(2,1)S(1)}, bf16[4608,1536]{1,0:T(8,128)(2,1)}, u32[]{:S(2)}) %copy-start.1) | copy-done | bytes 14155800
  141.4 1.3 copy-done.11
  147.4 9.8 %shard_map.113 = (bf16[512,4608]{1,0:T(8,128)(2,1)S(1)}, bf16[4608,1536]{1,0:T(8,128)(2,1)S(1)}) custom-call(s32[5]{0:T(128)S(1)} %stack.54.scal, s32[64]{0:T(128)S(1)} %reshape.237.table, bf16[128,4608]{1,0:T(8,128)(2,1)S(1)} %copy-done.9, bf16[128,4608]{1,0:T(8,128)(2,1)S(1)} %copy-done.11, ...), custom_call_target="tpu_custom_call", output_to_operand_aliasing={{0}: (13, {}), {1}: (14, {})} | custom-call | bytes 18000000 | tf_op jit(solution)/shard_map/pallas_call | solution.py:139
  157.3 3.2 %shard_map.114 = (bf16[512,4608]{1,0:T(8,128)(2,1)S(1)}, bf16[4608,1536]{1,0:T(8,128)(2,1)S(1)}) custom-call(s32[5]{0:T(128)S(1)} %stack.54.scal, s32[64]{0:T(128)S(1)} %reshape.237.table, bf16[64,4608]{1,0:T(8,128)(2,1)S(1)} %copy-done.29, bf16[64,4608]{1,0:T(8,128)(2,1)S(1)} %copy-done.31, ...), custom_call_target="tpu_custom_call", output_to_operand_aliasing={{0}: (8, {}), {1}: (9, {})} | custom-call | bytes 18000000 | tf_op jit(solution)/shard_map/pallas_call | solution.py:139
  160.5 2.1 shard_map.115
  162.6 8.3 %project.1 = (bf16[512,256]{1,0:T(8,128)(2,1)}, bf16[512,256]{1,0:T(8,128)(2,1)}, bf16[64,4608]{1,0:T(8,128)(2,1)S(1)}, bf16[64,4608]{1,0:T(8,128)(2,1)S(1)}, bf16[4608,1536]{1,0:T(8,128)(2,1)S(1)}) custom-call(s32[5]{0:T(128)S(1)} %stack.54.scal, s32[64]{0:T(128)S(1)} %reshape.237.table, ...), custom_call_target="tpu_custom_call", output_to_operand_aliasing={{4}: (9, {})} | custom-call | flops 4000000000 | bytes 10000000 | tf_op jit(solution)/shard_map/project/pallas_call | solution.py:226
  170.9 5.0 %copy-done.2 = bf16[4608,1536]{1,0:T(8,128)(2,1)} copy-done((bf16[4608,1536]{1,0:T(8,128)(2,1)}, bf16[4608,1536]{1,0:T(8,128)(2,1)S(1)}, u32[]{:S(2)}) %copy-start.2) | copy-done | bytes 14155800
  177.4 5.0 %copy-done.3 = bf16[4608,1536]{1,0:T(8,128)(2,1)S(1)} copy-done((bf16[4608,1536]{1,0:T(8,128)(2,1)S(1)}, bf16[4608,1536]{1,0:T(8,128)(2,1)}, u32[]{:S(2)}) %copy-start.3) | copy-done | bytes 14155800
  184.3 7.7 %shard_map.117 = (bf16[64,4608]{1,0:T(8,128)(2,1)S(1)}, bf16[64,4608]{1,0:T(8,128)(2,1)S(1)}, bf16[64,4608]{1,0:T(8,128)(2,1)S(1)}, bf16[64,4608]{1,0:T(8,128)(2,1)S(1)}) custom-call(s32[5]{0:T(128)S(1)} %stack.54.scal, f32[512,128]{1,0:T(8,128)S(1)} %get-tuple-element.25.cos_ref, f32[512,128]{1,0:T(8,128)S(1)} %get-tuple-element.26.sin_ref, ...), custom_call_target="tpu_custom_call" | custom-call | flops 2800000000 | bytes 3400000 | tf_op jit(solution)/shard_map/pallas_call | solution.py:271
  192.1 2.7 %collective-permute-start.30 = (bf16[64,4608]{1,0:T(8,128)(2,1)S(1)}, bf16[64,4608]{1,0:T(8,128)(2,1)S(1)}, u32[]{:S(2)}, u32[]{:S(2)}) collective-permute-start(bf16[64,4608]{1,0:T(8,128)(2,1)S(1)} %get-tuple-element.42), channel_id=1, source_target_pairs={{0,3},{1,0},{2,1},{3,2},{4,7},{5,4},{6,5},{7,6},{8,11},{9,8},{10,9... | collective-permute-start | bytes 1769480 | tf_op jit(solution)/shard_map/ppermute | solution.py:34
  195.0 1.3 collective-permute-start.34
  196.8 5.1 %shard_map.116.own_ref = bf16[128,4608]{1,0:T(8,128)(2,1)S(1)} custom-call(s32[5]{0:T(128)S(1)} %stack.54.scal, f32[512,128]{1,0:T(8,128)S(1)} %get-tuple-element.25.cos_ref, f32[512,128]{1,0:T(8,128)S(1)} %get-tuple-element.26.sin_ref, bf16[512,256]{1,0:T(8,128)(2,1)S(1)} %copy-done.13, bf16[512,256]{1,0:T(8,128)(2,1)S(1)} %copy-done.15, ...), custom_call_target="tpu_custom_call" | custom-call | flops 1400000000 | bytes 2200000 | tf_op jit(solution)/shard_map/pallas_call | solution.py:271
  201.9 6.8 %collective-permute-done.29.a1 = bf16[64,4608]{1,0:T(8,128)(2,1)S(1)} collective-permute-done((bf16[64,4608]{1,0:T(8,128)(2,1)S(1)}, bf16[64,4608]{1,0:T(8,128)(2,1)S(1)}, u32[]{:S(2)}, u32[]{:S(2)}) %collective-permute-start.29) | collective-permute-done | bytes 589856 | tf_op jit(solution)/shard_map/ppermute | solution.py:34
  208.7 9.1 %collective-permute-done.34.b1_hbm = bf16[64,4608]{1,0:T(8,128)(2,1)S(1)} collective-permute-done((bf16[64,4608]{1,0:T(8,128)(2,1)S(1)}, bf16[64,4608]{1,0:T(8,128)(2,1)S(1)}, u32[]{:S(2)}, u32[]{:S(2)}) %collective-permute-start.34) | collective-permute-done | bytes 589856 | tf_op jit(solution)/shard_map/ppermute | solution.py:34
  217.9 2.8 %finish.1 = bf16[128,4608]{1,0:T(8,128)(2,1)} custom-call(s32[5]{0:T(128)S(1)} %stack.54.scal, bf16[128,4608]{1,0:T(8,128)(2,1)S(1)} %bitcast.47, bf16[128,4608]{1,0:T(8,128)(2,1)S(1)} %shard_map.116.own_ref, bf16[64,4608]{1,0:T(8,128)(2,1)S(1)} %collective-permute-done.29.a1, bf16[64,4608]{1,0:T(8,128)(2,1)S(1)} %collective-permute-done.30.b0, ...), custom_call_target="tpu_custom_call" | custom-call | flops 6000000 | bytes 7000000 | tf_op jit(solution)/shard_map/finish/pallas_call | solution.py:309
  (125 shorter events, 21.3 us)
Async XLA Ops:
  1.6 6.7 %collective-permute-start = (bf16[72,1536]{1,0:T(8,128)(2,1)S(1)}, bf16[72,1536]{1,0:T(8,128)(2,1)S(1)}, u32[]{:S(2)}, u32[]{:S(2)}) collective-permute-start(bf16[72,1536]{1,0:T(8,128)(2,1)S(1)} %get-tuple-element.51), channel_id=1, source_target_pairs={{0,32},{4,12},{8,40},{12,20},{16,48},{20,28},{24,56},{28,4},{32,64... | collective-permute-start | bytes 663560 | tf_op jit(solution)/shard_map/ppermute | solution.py:342
  3.7 5.1 %collective-permute-start.1 = (bf16[72,1536]{1,0:T(8,128)(2,1)S(1)}, bf16[72,1536]{1,0:T(8,128)(2,1)S(1)}, u32[]{:S(2)}, u32[]{:S(2)}) collective-permute-start(bf16[72,1536]{1,0:T(8,128)(2,1)S(1)} %get-tuple-element.51), channel_id=1, source_target_pairs={{0,224},{4,28},{8,232},{12,4},{16,240},{20,12},{24,248},{28,20},{3... | collective-permute-start | bytes 663560 | tf_op jit(solution)/shard_map/ppermute | solution.py:342
  8.3 6.0 %collective-permute-start.2 = (bf16[72,1536]{1,0:T(8,128)(2,1)S(1)}, bf16[72,1536]{1,0:T(8,128)(2,1)S(1)}, u32[]{:S(2)}, u32[]{:S(2)}) collective-permute-start(bf16[72,1536]{1,0:T(8,128)(2,1)S(1)} %collective-permute-done), channel_id=1, source_target_pairs={{0,32},{4,12},{8,40},{12,20},{16,48},{20,28},{24,56},{28,4},{32,64... | collective-permute-start | bytes 663560 | tf_op jit(solution)/shard_map/ppermute | solution.py:342
  14.4 38.1 %copy-start.6 = (bf16[4,72,1536]{2,1,0:T(8,128)(2,1)}, bf16[4,72,1536]{2,1,0:T(8,128)(2,1)S(1)}, u32[]{:S(2)}) copy-start(bf16[4,72,1536]{2,1,0:T(8,128)(2,1)S(1)} %pad_maximum_fusion.refs_1_) | copy-start | bytes 2654212
  14.4 23.4 %collective-permute-start.3 = (bf16[4,72,1536]{2,1,0:T(8,128)(2,1)S(1)}, bf16[4,72,1536]{2,1,0:T(8,128)(2,1)S(1)}, u32[]{:S(2)}, u32[]{:S(2)}) collective-permute-start(bf16[4,72,1536]{2,1,0:T(8,128)(2,1)S(1)} %pad_maximum_fusion.refs_1_), channel_id=1, source_target_pairs={{0,24},{4,228},{8,0},{12,236},{16,8},{20,244},{24,16},{28,252},{32... | collective-permute-start | bytes 2654216 | tf_op jit(solution)/shard_map/ppermute | solution.py:342
  20.6 20.3 %collective-permute-start.8 = (bf16[4,72,1536]{2,1,0:T(8,128)(2,1)S(1)}, bf16[4,72,1536]{2,1,0:T(8,128)(2,1)}, u32[]{:S(2)}, u32[]{:S(2)}) collective-permute-start(bf16[4,72,1536]{2,1,0:T(8,128)(2,1)S(1)} %pad_maximum_fusion.refs_1_), channel_id=1, source_target_pairs={{0,8},{4,36},{8,16},{12,44},{16,24},{20,52},{24,0},{28,60},{32,40}... | collective-permute-start | bytes 2654216 | tf_op jit(solution)/shard_map/ppermute | solution.py:342
  20.6 7.4 %collective-permute-start.4 = (bf16[72,1536]{1,0:T(8,128)(2,1)S(1)}, bf16[72,1536]{1,0:T(8,128)(2,1)S(1)}, u32[]{:S(2)}, u32[]{:S(2)}) collective-permute-start(bf16[72,1536]{1,0:T(8,128)(2,1)S(1)} %collective-permute-done.1), channel_id=1, source_target_pairs={{0,224},{4,28},{8,232},{12,4},{16,240},{20,12},{24,248},{28,20},{3... | collective-permute-start | bytes 663560 | tf_op jit(solution)/shard_map/ppermute | solution.py:342
  28.0 7.6 %collective-permute-start.6 = (bf16[72,1536]{1,0:T(8,128)(2,1)S(1)}, bf16[72,1536]{1,0:T(8,128)(2,1)}, u32[]{:S(2)}, u32[]{:S(2)}) collective-permute-start(bf16[72,1536]{1,0:T(8,128)(2,1)S(1)} %collective-permute-done.4), channel_id=1, source_target_pairs={{0,224},{4,28},{8,232},{12,4},{16,240},{20,12},{24,248},{28,20},{3... | collective-permute-start | bytes 663560 | tf_op jit(solution)/shard_map/ppermute | solution.py:342
  28.0 9.9 %collective-permute-start.5 = (bf16[72,1536]{1,0:T(8,128)(2,1)S(1)}, bf16[72,1536]{1,0:T(8,128)(2,1)}, u32[]{:S(2)}, u32[]{:S(2)}) collective-permute-start(bf16[72,1536]{1,0:T(8,128)(2,1)S(1)} %collective-permute-done.2), channel_id=1, source_target_pairs={{0,32},{4,12},{8,40},{12,20},{16,48},{20,28},{24,56},{28,4},{32,64... | collective-permute-start | bytes 663560 | tf_op jit(solution)/shard_map/ppermute | solution.py:342
  35.5 5.4 %collective-permute-start.7 = (bf16[72,1536]{1,0:T(8,128)(2,1)}, bf16[72,1536]{1,0:T(8,128)(2,1)}, u32[]{:S(2)}, u32[]{:S(2)}) collective-permute-start(bf16[72,1536]{1,0:T(8,128)(2,1)} %collective-permute-done.6), channel_id=1, source_target_pairs={{0,224},{4,28},{8,232},{12,4},{16,240},{20,12},{24,248},{28,20},{3... | collective-permute-start | bytes 663560 | tf_op jit(solution)/shard_map/ppermute | solution.py:342
  44.1 13.5 %collective-permute-start.12 = (bf16[4,72,1536]{2,1,0:T(8,128)(2,1)}, bf16[4,72,1536]{2,1,0:T(8,128)(2,1)S(1)}, u32[]{:S(2)}, u32[]{:S(2)}) collective-permute-start(bf16[4,72,1536]{2,1,0:T(8,128)(2,1)} %get-tuple-element.49), channel_id=1, source_target_pairs={{0,24},{4,228},{8,0},{12,236},{16,8},{20,244},{24,16},{28,252},{32... | collective-permute-start | bytes 2654216 | tf_op jit(solution)/shard_map/ppermute | solution.py:342
  49.8 25.1 %collective-permute-start.19 = (bf16[128,4608]{1,0:T(8,128)(2,1)}, bf16[128,4608]{1,0:T(8,128)(2,1)S(1)}, u32[]{:S(2)}, u32[]{:S(2)}) collective-permute-start(bf16[128,4608]{1,0:T(8,128)(2,1)} %norm.1.refs_0_), channel_id=1, source_target_pairs={{0,3},{1,0},{2,1},{3,2},{4,7},{5,4},{6,5},{7,6},{8,11},{9,8},{10,9... | collective-permute-start | bytes 3538952 | tf_op jit(solution)/shard_map/ppermute | solution.py:34
  52.5 13.6 %collective-permute-start.9 = (bf16[4,72,1536]{2,1,0:T(8,128)(2,1)}, bf16[4,72,1536]{2,1,0:T(8,128)(2,1)S(1)}, u32[]{:S(2)}, u32[]{:S(2)}) collective-permute-start(bf16[4,72,1536]{2,1,0:T(8,128)(2,1)} %get-tuple-element.48), channel_id=1, source_target_pairs={{0,8},{4,36},{8,16},{12,44},{16,24},{20,52},{24,0},{28,60},{32,40}... | collective-permute-start | bytes 2654216 | tf_op jit(solution)/shard_map/ppermute | solution.py:342
  52.5 25.9 %collective-permute-start.21 = (bf16[128,4608]{1,0:T(8,128)(2,1)}, bf16[128,4608]{1,0:T(8,128)(2,1)S(1)}, u32[]{:S(2)}, u32[]{:S(2)}) collective-permute-start(bf16[128,4608]{1,0:T(8,128)(2,1)} %norm.1.refs_0_), channel_id=1, source_target_pairs={{0,1},{1,2},{2,3},{3,0},{4,5},{5,6},{6,7},{7,4},{8,9},{9,10},{10,1... | collective-permute-start | bytes 3538952 | tf_op jit(solution)/shard_map/ppermute | solution.py:34
  52.5 27.2 %collective-permute-start.25 = (bf16[4,72,1536]{2,1,0:T(8,128)(2,1)S(1)}, bf16[4,72,1536]{2,1,0:T(8,128)(2,1)S(1)}, u32[]{:S(2)}, u32[]{:S(2)}) collective-permute-start(bf16[4,72,1536]{2,1,0:T(8,128)(2,1)S(1)} %pad_maximum_fusion.refs_1_), channel_id=1, source_target_pairs={{0,4},{4,0},{8,12},{12,8},{16,20},{20,16},{24,28},{28,24},{32,36},... | collective-permute-start | bytes 2654216 | tf_op jit(solution)/shard_map/ppermute | solution.py:30
  57.6 35.2 %collective-permute-start.13 = (bf16[4,72,1536]{2,1,0:T(8,128)(2,1)S(1)}, bf16[4,72,1536]{2,1,0:T(8,128)(2,1)}, u32[]{:S(2)}, u32[]{:S(2)}) collective-permute-start(bf16[4,72,1536]{2,1,0:T(8,128)(2,1)S(1)} %broadcast_select_fusion), channel_id=1, source_target_pairs={{0,24},{4,228},{8,0},{12,236},{16,8},{20,244},{24,16},{28,252},{32... | collective-permute-start | bytes 2654216 | tf_op jit(solution)/shard_map/ppermute | solution.py:342
  66.1 26.8 %copy-start.16 = (bf16[4,72,1536]{2,1,0:T(8,128)(2,1)}, bf16[4,72,1536]{2,1,0:T(8,128)(2,1)S(1)}, u32[]{:S(2)}) copy-start(bf16[4,72,1536]{2,1,0:T(8,128)(2,1)S(1)} %collective-permute-done.9.refs_4_) | copy-start | bytes 2654212
  66.1 26.8 %collective-permute-start.10 = (bf16[4,72,1536]{2,1,0:T(8,128)(2,1)S(1)}, bf16[4,72,1536]{2,1,0:T(8,128)(2,1)}, u32[]{:S(2)}, u32[]{:S(2)}) collective-permute-start(bf16[4,72,1536]{2,1,0:T(8,128)(2,1)S(1)} %collective-permute-done.9.refs_4_), channel_id=1, source_target_pairs={{0,8},{4,36},{8,16},{12,44},{16,24},{20,52},{24,0},{28,60},{32,40}... | collective-permute-start | bytes 2654216 | tf_op jit(solution)/shard_map/ppermute | solution.py:342
  74.9 18.0 %copy-start.8 = (bf16[128,4608]{1,0:T(8,128)(2,1)}, bf16[128,4608]{1,0:T(8,128)(2,1)S(1)}, u32[]{:S(2)}) copy-start(bf16[128,4608]{1,0:T(8,128)(2,1)S(1)} %collective-permute-done.19.refs_0_) | copy-start | bytes 3538948
  75.0 12.2 %collective-permute-start.20 = (bf16[64,4608]{1,0:T(8,128)(2,1)S(1)}, bf16[64,4608]{1,0:T(8,128)(2,1)S(1)}, u32[]{:S(2)}, u32[]{:S(2)}) collective-permute-start(bf16[64,4608]{1,0:T(8,128)(2,1)S(1)} %slice.48), channel_id=1, source_target_pairs={{0,3},{1,0},{2,1},{3,2},{4,7},{5,4},{6,5},{7,6},{8,11},{9,8},{10,9... | collective-permute-start | bytes 1769480 | tf_op jit(solution)/shard_map/ppermute | solution.py:34
  78.5 18.5 %copy-start.10 = (bf16[128,4608]{1,0:T(8,128)(2,1)}, bf16[128,4608]{1,0:T(8,128)(2,1)S(1)}, u32[]{:S(2)}) copy-start(bf16[128,4608]{1,0:T(8,128)(2,1)S(1)} %collective-permute-done.21.refs_1_) | copy-start | bytes 3538948
  78.5 35.1 %collective-permute-start.28 = (bf16[4,72,1536]{2,1,0:T(8,128)(2,1)}, bf16[4,72,1536]{2,1,0:T(8,128)(2,1)S(1)}, u32[]{:S(2)}, u32[]{:S(2)}) collective-permute-start(bf16[4,72,1536]{2,1,0:T(8,128)(2,1)} %get-tuple-element.47.refs_9_), channel_id=1, source_target_pairs={{0,4},{8,12},{16,20},{24,28},{32,36},{40,44},{48,52},{56,60},{64,6... | collective-permute-start | bytes 2654216 | tf_op jit(solution)/shard_map/ppermute | solution.py:347
  79.8 17.2 %copy-start.18 = (bf16[4,72,1536]{2,1,0:T(8,128)(2,1)}, bf16[4,72,1536]{2,1,0:T(8,128)(2,1)S(1)}, u32[]{:S(2)}) copy-start(bf16[4,72,1536]{2,1,0:T(8,128)(2,1)S(1)} %collective-permute-done.25.refs_6_) | copy-start | bytes 2654212
  79.8 37.0 %collective-permute-start.27 = (bf16[4,72,1536]{2,1,0:T(8,128)(2,1)S(1)}, bf16[4,72,1536]{2,1,0:T(8,128)(2,1)S(1)}, u32[]{:S(2)}, u32[]{:S(2)}) collective-permute-start(bf16[4,72,1536]{2,1,0:T(8,128)(2,1)S(1)} %collective-permute-done.3.refs_3_), channel_id=1, source_target_pairs={{0,4},{4,0},{8,12},{12,8},{16,20},{20,16},{24,28},{28,24},{32,36},... | collective-permute-start | bytes 2654216 | tf_op jit(solution)/shard_map/ppermute | solution.py:30
  88.0 29.7 %collective-permute-start.26 = (bf16[4,72,1536]{2,1,0:T(8,128)(2,1)}, bf16[4,72,1536]{2,1,0:T(8,128)(2,1)S(1)}, u32[]{:S(2)}, u32[]{:S(2)}) collective-permute-start(bf16[4,72,1536]{2,1,0:T(8,128)(2,1)} %collective-permute-done.8.refs_2_), channel_id=1, source_target_pairs={{0,4},{4,0},{8,12},{12,8},{16,20},{20,16},{24,28},{28,24},{32,36},... | collective-permute-start | bytes 2654216 | tf_op jit(solution)/shard_map/ppermute | solution.py:30
  92.9 26.2 %collective-permute-start.23 = (bf16[4,72,1536]{2,1,0:T(8,128)(2,1)S(1)}, bf16[4,72,1536]{2,1,0:T(8,128)(2,1)S(1)}, u32[]{:S(2)}, u32[]{:S(2)}) collective-permute-start(bf16[4,72,1536]{2,1,0:T(8,128)(2,1)S(1)} %collective-permute-done.9.refs_4_), channel_id=1, source_target_pairs={{0,4},{4,0},{8,12},{12,8},{16,20},{20,16},{24,28},{28,24},{32,36},... | collective-permute-start | bytes 2654216 | tf_op jit(solution)/shard_map/ppermute | solution.py:30
  92.9 34.3 %copy-start.35 = (s32[1,8,4,2]{1,2,3,0:T(4,128)S(1)}, s32[1,8,4,2]{1,2,3,0:T(4,128)}, u32[]{:S(2)}) copy-start(s32[1,8,4,2]{1,2,3,0:T(4,128)} %constant.108) | copy-start | bytes 772
  92.9 34.2 %copy-start.36 = (s32[1,8,4,2]{1,2,3,0:T(4,128)S(1)}, s32[1,8,4,2]{1,2,3,0:T(4,128)}, u32[]{:S(2)}) copy-start(s32[1,8,4,2]{1,2,3,0:T(4,128)} %constant.109) | copy-start | bytes 772
  93.0 35.2 %copy-start.4 = (bf16[128,4608]{1,0:T(8,128)(2,1)S(1)}, bf16[128,4608]{1,0:T(8,128)(2,1)}, u32[]{:S(2)}) copy-start(bf16[128,4608]{1,0:T(8,128)(2,1)} %norm.1.refs_0_) | copy-start | bytes 3538948
  93.0 16.7 %collective-permute-start.22 = (bf16[64,4608]{1,0:T(8,128)(2,1)S(1)}, bf16[64,4608]{1,0:T(8,128)(2,1)S(1)}, u32[]{:S(2)}, u32[]{:S(2)}) collective-permute-start(bf16[64,4608]{1,0:T(8,128)(2,1)S(1)} %slice.49), channel_id=1, source_target_pairs={{0,1},{1,2},{2,3},{3,0},{4,5},{5,6},{6,7},{7,4},{8,9},{9,10},{10,1... | collective-permute-start | bytes 1769480 | tf_op jit(solution)/shard_map/ppermute | solution.py:34
  110.5 9.5 %collective-permute-start.14 = (bf16[2,72,1536]{2,1,0:T(8,128)(2,1)}, bf16[2,72,1536]{2,1,0:T(8,128)(2,1)}, u32[]{:S(2)}, u32[]{:S(2)}) collective-permute-start(bf16[2,72,1536]{2,1,0:T(8,128)(2,1)} %slice.47), channel_id=1, source_target_pairs={{4,228},{12,236},{20,244},{28,252},{36,4},{44,12},{52,20},{60,28},... | collective-permute-start | bytes 1327112 | tf_op jit(solution)/shard_map/ppermute | solution.py:342
  114.6 10.6 %collective-permute-start.11 = (bf16[2,72,1536]{2,1,0:T(8,128)(2,1)}, bf16[2,72,1536]{2,1,0:T(8,128)(2,1)}, u32[]{:S(2)}, u32[]{:S(2)}) collective-permute-start(bf16[2,72,1536]{2,1,0:T(8,128)(2,1)} %slice.46), channel_id=1, source_target_pairs={{4,36},{12,44},{20,52},{28,60},{36,68},{44,76},{52,84},{60,92},{68... | collective-permute-start | bytes 1327112 | tf_op jit(solution)/shard_map/ppermute | solution.py:342
  117.7 39.5 %collective-permute-start.24 = (bf16[4,72,1536]{2,1,0:T(8,128)(2,1)S(1)}, bf16[4,72,1536]{2,1,0:T(8,128)(2,1)}, u32[]{:S(2)}, u32[]{:S(2)}) collective-permute-start(bf16[4,72,1536]{2,1,0:T(8,128)(2,1)S(1)} %collective-permute-done.12.refs_5_), channel_id=1, source_target_pairs={{0,4},{4,0},{8,12},{12,8},{16,20},{20,16},{24,28},{28,24},{32,36},... | collective-permute-start | bytes 2654216 | tf_op jit(solution)/shard_map/ppermute | solution.py:30
  118.6 41.9 %collective-permute-start.18 = (bf16[4,72,1536]{2,1,0:T(8,128)(2,1)}, bf16[4,72,1536]{2,1,0:T(8,128)(2,1)}, u32[]{:S(2)}, u32[]{:S(2)}) collective-permute-start(bf16[4,72,1536]{2,1,0:T(8,128)(2,1)} %collective-permute-done.13.refs_3_), channel_id=1, source_target_pairs={{0,4},{4,0},{8,12},{12,8},{16,20},{20,16},{24,28},{28,24},{32,36},... | collective-permute-start | bytes 2654216 | tf_op jit(solution)/shard_map/ppermute | solution.py:30
  120.0 40.4 %collective-permute-start.17 = (bf16[4,72,1536]{2,1,0:T(8,128)(2,1)}, bf16[4,72,1536]{2,1,0:T(8,128)(2,1)}, u32[]{:S(2)}, u32[]{:S(2)}) collective-permute-start(bf16[4,72,1536]{2,1,0:T(8,128)(2,1)} %collective-permute-done.10.refs_2_), channel_id=1, source_target_pairs={{0,4},{4,0},{8,12},{12,8},{16,20},{20,16},{24,28},{28,24},{32,36},... | collective-permute-start | bytes 2654216 | tf_op jit(solution)/shard_map/ppermute | solution.py:30
  120.1 42.5 %collective-permute-start.16 = (bf16[2,72,1536]{2,1,0:T(8,128)(2,1)}, bf16[2,72,1536]{2,1,0:T(8,128)(2,1)}, u32[]{:S(2)}, u32[]{:S(2)}) collective-permute-start(bf16[2,72,1536]{2,1,0:T(8,128)(2,1)} %collective-permute-done.14.down_own), channel_id=1, source_target_pairs={{4,0},{12,8},{20,16},{28,24},{36,32},{44,40},{52,48},{60,56},{68,6... | collective-permute-start | bytes 1327112 | tf_op jit(solution)/shard_map/ppermute | solution.py:347
  125.1 37.5 %collective-permute-start.15 = (bf16[2,72,1536]{2,1,0:T(8,128)(2,1)}, bf16[2,72,1536]{2,1,0:T(8,128)(2,1)}, u32[]{:S(2)}, u32[]{:S(2)}) collective-permute-start(bf16[2,72,1536]{2,1,0:T(8,128)(2,1)} %collective-permute-done.11.up_own), channel_id=1, source_target_pairs={{4,0},{12,8},{20,16},{28,24},{36,32},{44,40},{52,48},{60,56},{68,6... | collective-permute-start | bytes 1327112 | tf_op jit(solution)/shard_map/ppermute | solution.py:347
  147.4 9.9 %copy-start.27 = (bf16[4,72,1536]{2,1,0:T(8,128)(2,1)S(1)}, bf16[4,72,1536]{2,1,0:T(8,128)(2,1)}, u32[]{:S(2)}) copy-start(bf16[4,72,1536]{2,1,0:T(8,128)(2,1)} %copy-done.26) | copy-start | bytes 2654212
  147.4 9.9 %copy-start.29 = (bf16[64,4608]{1,0:T(8,128)(2,1)S(1)}, bf16[64,4608]{1,0:T(8,128)(2,1)}, u32[]{:S(2)}) copy-start(bf16[64,4608]{1,0:T(8,128)(2,1)} %copy-done.28) | copy-start | bytes 1769476
  147.4 9.9 %copy-start.31 = (bf16[64,4608]{1,0:T(8,128)(2,1)S(1)}, bf16[64,4608]{1,0:T(8,128)(2,1)}, u32[]{:S(2)}) copy-start(bf16[64,4608]{1,0:T(8,128)(2,1)} %copy-done.30) | copy-start | bytes 1769476
  175.9 18.8 %collective-permute-start.33 = (bf16[64,4608]{1,0:T(8,128)(2,1)S(1)}, bf16[64,4608]{1,0:T(8,128)(2,1)S(1)}, u32[]{:S(2)}, u32[]{:S(2)}) collective-permute-start(bf16[64,4608]{1,0:T(8,128)(2,1)S(1)} %get-tuple-element.46), channel_id=1, source_target_pairs={{0,3},{1,0},{2,1},{3,2},{4,7},{5,4},{6,5},{7,6},{8,11},{9,8},{10,9... | collective-permute-start | bytes 1769480 | tf_op jit(solution)/shard_map/ppermute | solution.py:34
  177.1 19.1 %collective-permute-start.31 = (bf16[64,4608]{1,0:T(8,128)(2,1)S(1)}, bf16[64,4608]{1,0:T(8,128)(2,1)S(1)}, u32[]{:S(2)}, u32[]{:S(2)}) collective-permute-start(bf16[64,4608]{1,0:T(8,128)(2,1)S(1)} %get-tuple-element.44), channel_id=1, source_target_pairs={{0,1},{1,2},{2,3},{3,0},{4,5},{5,6},{6,7},{7,4},{8,9},{9,10},{10,1... | collective-permute-start | bytes 1769480 | tf_op jit(solution)/shard_map/ppermute | solution.py:34
  192.0 16.6 %collective-permute-start.29 = (bf16[64,4608]{1,0:T(8,128)(2,1)S(1)}, bf16[64,4608]{1,0:T(8,128)(2,1)S(1)}, u32[]{:S(2)}, u32[]{:S(2)}) collective-permute-start(bf16[64,4608]{1,0:T(8,128)(2,1)S(1)} %get-tuple-element.41), channel_id=1, source_target_pairs={{0,1},{1,2},{2,3},{3,0},{4,5},{5,6},{6,7},{7,4},{8,9},{9,10},{10,1... | collective-permute-start | bytes 1769480 | tf_op jit(solution)/shard_map/ppermute | solution.py:34
  192.1 16.5 %collective-permute-start.30 = (bf16[64,4608]{1,0:T(8,128)(2,1)S(1)}, bf16[64,4608]{1,0:T(8,128)(2,1)S(1)}, u32[]{:S(2)}, u32[]{:S(2)}) collective-permute-start(bf16[64,4608]{1,0:T(8,128)(2,1)S(1)} %get-tuple-element.42), channel_id=1, source_target_pairs={{0,3},{1,0},{2,1},{3,2},{4,7},{5,4},{6,5},{7,6},{8,11},{9,8},{10,9... | collective-permute-start | bytes 1769480 | tf_op jit(solution)/shard_map/ppermute | solution.py:34
  195.0 22.8 %collective-permute-start.34 = (bf16[64,4608]{1,0:T(8,128)(2,1)S(1)}, bf16[64,4608]{1,0:T(8,128)(2,1)S(1)}, u32[]{:S(2)}, u32[]{:S(2)}) collective-permute-start(bf16[64,4608]{1,0:T(8,128)(2,1)S(1)} %add_convert_fusion), channel_id=1, source_target_pairs={{0,3},{1,0},{2,1},{3,2},{4,7},{5,4},{6,5},{7,6},{8,11},{9,8},{10,9... | collective-permute-start | bytes 1769480 | tf_op jit(solution)/shard_map/ppermute | solution.py:34
  196.4 21.5 %copy-start.5 = (bf16[1,128,4608]{2,1,0:T(8,128)(2,1)S(1)}, bf16[1,128,4608]{2,1,0:T(8,128)(2,1)}, u32[]{:S(2)}) copy-start(bf16[1,128,4608]{2,1,0:T(8,128)(2,1)} %param.9) | copy-start | bytes 3538948
  196.4 21.5 %copy-start.32 = (f32[4608]{0:T(1024)S(1)}, f32[4608]{0:T(1024)}, u32[]{:S(2)}) copy-start(f32[4608]{0:T(1024)} %gain_ref.3) | copy-start | bytes 55300
  196.4 21.5 %collective-permute-start.32 = (bf16[64,4608]{1,0:T(8,128)(2,1)S(1)}, bf16[64,4608]{1,0:T(8,128)(2,1)S(1)}, u32[]{:S(2)}, u32[]{:S(2)}) collective-permute-start(bf16[64,4608]{1,0:T(8,128)(2,1)S(1)} %add_convert_fusion.1), channel_id=1, source_target_pairs={{0,1},{1,2},{2,3},{3,0},{4,5},{5,6},{6,7},{7,4},{8,9},{9,10},{10,1... | collective-permute-start | bytes 1769480 | tf_op jit(solution)/shard_map/ppermute | solution.py:34
  (24 other events, 65.2 us)
where the time goes:
time: 225 us; the launch traced here: 221 us
  waiting for transfers between devices  74.1 us (33%)
  starting transfers between devices  56.8 us (25%)
  Pallas kernels  43.5 us (19%)
  local copies, waits for them, and re-layouts  38.6 us (17%)
  other arithmetic  5.89 us (3%)
    ppermute x10, waiting for transfers between devices, column(): return lax.ppermute(array, 'mp', [(y, (y + dy) % NY) for y in range(NY)])  40.5 us
    unnamed x74, local copies, waits for them, and re-layouts  34.6 us
    ppermute x15, waiting for transfers between devices, torus(): return lax.ppermute(array, 'dp', pairs)  33.6 us
    ppermute x15, starting transfers between devices, torus(): return lax.ppermute(array, 'dp', pairs)  24.3 us
    pallas_call x4, Pallas kernels, fill(): pl.pallas_call(functools.partial(fill_kernel, offsets, groups, len(held))...  17.1 us
    ppermute x7, starting transfers between devices, plane(): return lax.ppermute(array, 'dp', pairs)  13.5 us
    pallas_call x2, Pallas kernels, attend(): pl.pallas_call(functools.partial(attend_kernel, blocks, outs), in_specs=[...  12.8 us
    ppermute x10, starting transfers between devices, column(): return lax.ppermute(array, 'mp', [(y, (y + dy) % NY) for y in range(NY)])  12.5 us
  transfers between devices with their start and end apart: 35, of which 15 were waited for; matrix products, arithmetic and copies ran while one was open for 3% of the time, Pallas kernels for 15%

commit v1 on v0

--- a/solution.py
+++ b/solution.py
@@ -391,8 +391,7 @@
     near = jnp.stack([shard, s1, s2, s3])
     r1 = torus(near, LARGE_UP)
     r2 = torus(near, LARGE_DOWN)
-    r2, *angles = lax.optimization_barrier((r2, *tables[2:]))
-    tables = (*tables[:2], *angles)
+    r2, tables = lax.optimization_barrier((r2, tables))
     far = jnp.stack([s4, s5, s6, s7])
     r3 = torus(jnp.where(first, far, r1), LARGE_UP)
     r4 = torus(jnp.where(first, far, r2), LARGE_DOWN)
@@ -422,10 +421,9 @@
     tables = (scal, row_table(scal[0], scal[1], core), *angle_tables(local_len * NY))
     arrays, others, far, up, down, tables = gathered_weights(shard, core, tables)
     scal, table, cosine, sine = tables
-    held = fill(scal, table, [normed], ((0, 0),), arrays[:1], (0,), (), (), width)
     held = fill(
-        scal, table, [above, below], ((1, 0), (3, 0)), arrays[1:5] + others[:3],
-        (1, 2, 3, 4, 8, 9, 10), far, held, width,
+        scal, table, [normed, above, below], ((0, 0), (1, 0), (3, 0)), arrays[:5] + others[:3],
+        (0, 1, 2, 3, 4, 8, 9, 10), far, (), width,
     )
     held = fill(
         scal, table, [across0, across1], ((2, 0), (2, 64)), arrays[5:] + others[3:5],

time: 225 us -> 186 us (0.83); the launches traced: 221 us -> 185 us
  local copies, waits for them, and re-layouts: 38.6 us -> 3.04 us
  waiting for transfers between devices: 74.1 us -> 59.8 us
  starting transfers between devices: 56.8 us -> 65.1 us
  Pallas kernels: 43.5 us -> 46.6 us
  other arithmetic: 5.89 us -> 8.84 us
    unnamed x74 -> x28, local copies, waits for them, and re-layouts: 34.6 us -> 2.64 us
    ppermute x10, waiting for transfers between devices: 40.5 us -> 29 us  [column(): return lax.ppermute(array, 'mp', [(y, (y + dy) % NY) for y in range(NY)])]
    ppermute x7, starting transfers between devices: 13.5 us -> 17.9 us  [plane(): return lax.ppermute(array, 'dp', pairs)]
    ppermute x10, starting transfers between devices: 12.5 us -> 15.8 us  [column(): return lax.ppermute(array, 'mp', [(y, (y + dy) % NY) for y in range(NY)])]
    ppermute x15, starting transfers between devices: 24.3 us -> 27.5 us  [torus(): return lax.ppermute(array, 'dp', pairs)]
    pallas_call x4 -> x3, Pallas kernels: 17.1 us -> 20.3 us  [fill(): pl.pallas_call(functools.partial(fill_kernel, offsets, groups, len(held))...]
    ppermute x15, waiting for transfers between devices: 33.6 us -> 30.7 us  [torus(): return lax.ppermute(array, 'dp', pairs)]
    ppermute x3, starting transfers between devices: 6.53 us -> 3.89 us  [one_way(): return lax.ppermute(array, 'dp', pairs)]
  transfers between devices with their start and end apart: 35 -> 35, of which waited for: 15 -> 15; matrix products, arithmetic and copies ran while one was open for 3% -> 2% of each run, Pallas kernels for 15% -> 19%
where the time goes in v1:
time: 186 us; the launch traced here: 185 us
  starting transfers between devices  65.1 us (35%)
  waiting for transfers between devices  59.8 us (32%)
  Pallas kernels  46.6 us (25%)
  other arithmetic  8.84 us (5%)
  local copies, waits for them, and re-layouts  3.04 us (2%)
    ppermute x15, waiting for transfers between devices, torus(): return lax.ppermute(array, 'dp', pairs)  30.7 us
    ppermute x10, waiting for transfers between devices, column(): return lax.ppermute(array, 'mp', [(y, (y + dy) % NY) for y in range(NY)])  29 us
    ppermute x15, starting transfers between devices, torus(): return lax.ppermute(array, 'dp', pairs)  27.5 us
    pallas_call x3, Pallas kernels, fill(): pl.pallas_call(functools.partial(fill_kernel, offsets, groups, len(held))...  20.3 us
    ppermute x7, starting transfers between devices, plane(): return lax.ppermute(array, 'dp', pairs)  17.9 us
    ppermute x10, starting transfers between devices, column(): return lax.ppermute(array, 'mp', [(y, (y + dy) % NY) for y in range(NY)])  15.8 us
    pallas_call x2, Pallas kernels, attend(): pl.pallas_call(functools.partial(attend_kernel, blocks, outs), in_specs=[...  12.8 us
    pallas_call x1, Pallas kernels, project(): pl.pallas_call(project_kernel, in_specs=[SMEM] * 2 + [VMEM] * 2 + [ANY] *...  8.24 us
  transfers between devices with their start and end apart: 35, of which 15 were waited for; matrix products, arithmetic and copies ran while one was open for 2% of the time, Pallas kernels for 19%

profile of v1, /device:TPU:1, one launch (start us, length us, event | category | flops | bytes accessed | tf_op | source)
XLA Modules:
  0.0 185.1 jit_solution(8357348612324925678)
XLA Ops:
  0.6 1.0 fusion.19
  1.6 2.1 %collective-permute-start = (bf16[72,1536]{1,0:T(8,128)(2,1)S(1)}, bf16[72,1536]{1,0:T(8,128)(2,1)S(1)}, u32[]{:S(2)}, u32[]{:S(2)}) collective-permute-start(bf16[72,1536]{1,0:T(8,128)(2,1)S(1)} %get-tuple-element.51), channel_id=1, source_target_pairs={{0,32},{4,12},{8,40},{12,20},{16,48},{20,28},{24,56},{28,4},{32,64... | collective-permute-start | bytes 663560 | tf_op jit(solution)/shard_map/ppermute | solution.py:342
  3.7 1.4 collective-permute-start.1
  5.1 3.2 %collective-permute-done = bf16[72,1536]{1,0:T(8,128)(2,1)S(1)} collective-permute-done((bf16[72,1536]{1,0:T(8,128)(2,1)S(1)}, bf16[72,1536]{1,0:T(8,128)(2,1)S(1)}, u32[]{:S(2)}, u32[]{:S(2)}) %collective-permute-start) | collective-permute-done | bytes 221216 | tf_op jit(solution)/shard_map/ppermute | solution.py:342
  8.8 5.6 %collective-permute-done.2 = bf16[72,1536]{1,0:T(8,128)(2,1)} collective-permute-done((bf16[72,1536]{1,0:T(8,128)(2,1)S(1)}, bf16[72,1536]{1,0:T(8,128)(2,1)}, u32[]{:S(2)}, u32[]{:S(2)}) %collective-permute-start.2) | collective-permute-done | bytes 221216 | tf_op jit(solution)/shard_map/ppermute | solution.py:342
  14.4 1.1 pad_maximum_fusion.refs_3_
  15.5 6.1 %collective-permute-start.3 = (bf16[4,72,1536]{2,1,0:T(8,128)(2,1)S(1)}, bf16[4,72,1536]{2,1,0:T(8,128)(2,1)S(1)}, u32[]{:S(2)}, u32[]{:S(2)}) collective-permute-start(bf16[4,72,1536]{2,1,0:T(8,128)(2,1)S(1)} %pad_maximum_fusion.refs_3_), channel_id=1, source_target_pairs={{0,24},{4,228},{8,0},{12,236},{16,8},{20,244},{24,16},{28,252},{32... | collective-permute-start | bytes 2654216 | tf_op jit(solution)/shard_map/ppermute | solution.py:342
  21.7 1.8 fusion
  23.8 7.1 %collective-permute-done.4 = bf16[72,1536]{1,0:T(8,128)(2,1)S(1)} collective-permute-done((bf16[72,1536]{1,0:T(8,128)(2,1)S(1)}, bf16[72,1536]{1,0:T(8,128)(2,1)S(1)}, u32[]{:S(2)}, u32[]{:S(2)}) %collective-permute-start.4) | collective-permute-done | bytes 221216 | tf_op jit(solution)/shard_map/ppermute | solution.py:342
  31.6 1.0 collective-permute-start.6
  33.1 5.7 %collective-permute-done.6 = bf16[72,1536]{1,0:T(8,128)(2,1)} collective-permute-done((bf16[72,1536]{1,0:T(8,128)(2,1)S(1)}, bf16[72,1536]{1,0:T(8,128)(2,1)}, u32[]{:S(2)}, u32[]{:S(2)}) %collective-permute-start.6) | collective-permute-done | bytes 221216 | tf_op jit(solution)/shard_map/ppermute | solution.py:342
  38.9 2.4 %collective-permute-start.7 = (bf16[72,1536]{1,0:T(8,128)(2,1)}, bf16[72,1536]{1,0:T(8,128)(2,1)}, u32[]{:S(2)}, u32[]{:S(2)}) collective-permute-start(bf16[72,1536]{1,0:T(8,128)(2,1)} %collective-permute-done.6), channel_id=1, source_target_pairs={{0,224},{4,28},{8,232},{12,4},{16,240},{20,12},{24,248},{28,20},{3... | collective-permute-start | bytes 663560 | tf_op jit(solution)/shard_map/ppermute | solution.py:342
  42.2 1.4 pad_maximum_fusion.2
  43.6 0.9 collective-permute-done.7
  44.5 3.2 %pad_maximum_fusion.1 = (bf16[4,72,1536]{2,1,0:T(8,128)(2,1)}, bf16[4,72,1536]{2,1,0:T(8,128)(2,1)}, bf16[4,72,1536]{2,1,0:T(8,128)(2,1)}) fusion(bf16[1,72,1536]{2,1,0:T(8,128)(2,1)} %bitcast.19, bf16[1,72,1536]{2,1,0:T(8,128)(2,1)} %bitcast.18, bf16[1,72,1536]{2,1,0:T(8,128)(2,1)} %bitcast.17, bf16[1,72,1536]{2,1,0:T(8,128)(2,1)S(1)} %bitcast.53, ...), kind=kLoop, calls=%fused_computation.3 | loop fusion | flops 2211840 | bytes 5308417 | tf_op jit(solution)/shard_map/stack | solution.py:395
  47.7 1.5 collective-permute-start.12
  49.2 2.5 %norm.1.refs_0_ = bf16[128,4608]{1,0:T(8,128)(2,1)} custom-call(bf16[128,4608]{1,0:T(8,128)(2,1)} %bitcast.46, f32[4608]{0:T(1024)} %gain_ref.2), custom_call_target="tpu_custom_call" | custom-call | flops 2000000 | bytes 2400000 | tf_op jit(solution)/shard_map/norm/pallas_call | solution.py:46
  51.7 2.7 %collective-permute-start.19 = (bf16[128,4608]{1,0:T(8,128)(2,1)}, bf16[128,4608]{1,0:T(8,128)(2,1)S(1)}, u32[]{:S(2)}, u32[]{:S(2)}) collective-permute-start(bf16[128,4608]{1,0:T(8,128)(2,1)} %norm.1.refs_0_), channel_id=1, source_target_pairs={{0,3},{1,0},{2,1},{3,2},{4,7},{5,4},{6,5},{7,6},{8,11},{9,8},{10,9... | collective-permute-start | bytes 3538952 | tf_op jit(solution)/shard_map/ppermute | solution.py:34
  54.5 4.7 %collective-permute-start.25 = (bf16[4,72,1536]{2,1,0:T(8,128)(2,1)S(1)}, bf16[4,72,1536]{2,1,0:T(8,128)(2,1)S(1)}, u32[]{:S(2)}, u32[]{:S(2)}) collective-permute-start(bf16[4,72,1536]{2,1,0:T(8,128)(2,1)S(1)} %pad_maximum_fusion.refs_3_), channel_id=1, source_target_pairs={{0,4},{4,0},{8,12},{12,8},{16,20},{20,16},{24,28},{28,24},{32,36},... | collective-permute-start | bytes 2654216 | tf_op jit(solution)/shard_map/ppermute | solution.py:30
  60.2 2.6 %collective-permute-start.13 = (bf16[4,72,1536]{2,1,0:T(8,128)(2,1)S(1)}, bf16[4,72,1536]{2,1,0:T(8,128)(2,1)S(1)}, u32[]{:S(2)}, u32[]{:S(2)}) collective-permute-start(bf16[4,72,1536]{2,1,0:T(8,128)(2,1)S(1)} %broadcast_select_fusion), channel_id=1, source_target_pairs={{0,24},{4,228},{8,0},{12,236},{16,8},{20,244},{24,16},{28,252},{32... | collective-permute-start | bytes 2654216 | tf_op jit(solution)/shard_map/ppermute | solution.py:342
  62.8 12.8 %collective-permute-done.19.refs_1_ = bf16[128,4608]{1,0:T(8,128)(2,1)S(1)} collective-permute-done((bf16[128,4608]{1,0:T(8,128)(2,1)}, bf16[128,4608]{1,0:T(8,128)(2,1)S(1)}, u32[]{:S(2)}, u32[]{:S(2)}) %collective-permute-start.19) | collective-permute-done | bytes 1179680 | tf_op jit(solution)/shard_map/ppermute | solution.py:34
  75.7 3.4 %collective-permute-start.20 = (bf16[64,4608]{1,0:T(8,128)(2,1)S(1)}, bf16[64,4608]{1,0:T(8,128)(2,1)S(1)}, u32[]{:S(2)}, u32[]{:S(2)}) collective-permute-start(bf16[64,4608]{1,0:T(8,128)(2,1)S(1)} %slice.48), channel_id=1, source_target_pairs={{0,3},{1,0},{2,1},{3,2},{4,7},{5,4},{6,5},{7,6},{8,11},{9,8},{10,9... | collective-permute-start | bytes 1769480 | tf_op jit(solution)/shard_map/ppermute | solution.py:34
  79.3 2.0 %collective-permute-start.10 = (bf16[4,72,1536]{2,1,0:T(8,128)(2,1)S(1)}, bf16[4,72,1536]{2,1,0:T(8,128)(2,1)S(1)}, u32[]{:S(2)}, u32[]{:S(2)}) collective-permute-start(bf16[4,72,1536]{2,1,0:T(8,128)(2,1)S(1)} %collective-permute-done.9.refs_6_), channel_id=1, source_target_pairs={{0,8},{4,36},{8,16},{12,44},{16,24},{20,52},{24,0},{28,60},{32,40}... | collective-permute-start | bytes 2654216 | tf_op jit(solution)/shard_map/ppermute | solution.py:342
  81.3 1.3 collective-permute-start.28
  82.6 4.8 %collective-permute-done.20.refs_0_ = bf16[64,4608]{1,0:T(8,128)(2,1)S(1)} collective-permute-done((bf16[64,4608]{1,0:T(8,128)(2,1)S(1)}, bf16[64,4608]{1,0:T(8,128)(2,1)S(1)}, u32[]{:S(2)}, u32[]{:S(2)}) %collective-permute-start.20) | collective-permute-done | bytes 589856 | tf_op jit(solution)/shard_map/ppermute | solution.py:34
  87.3 6.1 %collective-permute-start.27 = (bf16[4,72,1536]{2,1,0:T(8,128)(2,1)S(1)}, bf16[4,72,1536]{2,1,0:T(8,128)(2,1)S(1)}, u32[]{:S(2)}, u32[]{:S(2)}) collective-permute-start(bf16[4,72,1536]{2,1,0:T(8,128)(2,1)S(1)} %collective-permute-done.3.refs_5_), channel_id=1, source_target_pairs={{0,4},{4,0},{8,12},{12,8},{16,20},{20,16},{24,28},{28,24},{32,36},... | collective-permute-start | bytes 2654216 | tf_op jit(solution)/shard_map/ppermute | solution.py:30
  93.5 3.4 %collective-permute-start.26 = (bf16[4,72,1536]{2,1,0:T(8,128)(2,1)S(1)}, bf16[4,72,1536]{2,1,0:T(8,128)(2,1)S(1)}, u32[]{:S(2)}, u32[]{:S(2)}) collective-permute-start(bf16[4,72,1536]{2,1,0:T(8,128)(2,1)S(1)} %copy-done.3), channel_id=1, source_target_pairs={{0,4},{4,0},{8,12},{12,8},{16,20},{20,16},{24,28},{28,24},{32,36},... | collective-permute-start | bytes 2654216 | tf_op jit(solution)/shard_map/ppermute | solution.py:30
  97.1 3.0 %collective-permute-start.24 = (bf16[4,72,1536]{2,1,0:T(8,128)(2,1)S(1)}, bf16[4,72,1536]{2,1,0:T(8,128)(2,1)S(1)}, u32[]{:S(2)}, u32[]{:S(2)}) collective-permute-start(bf16[4,72,1536]{2,1,0:T(8,128)(2,1)S(1)} %collective-permute-done.12.refs_7_), channel_id=1, source_target_pairs={{0,4},{4,0},{8,12},{12,8},{16,20},{20,16},{24,28},{28,24},{32,36},... | collective-permute-start | bytes 2654216 | tf_op jit(solution)/shard_map/ppermute | solution.py:30
  100.7 5.3 %collective-permute-start.14 = (bf16[2,72,1536]{2,1,0:T(8,128)(2,1)S(1)}, bf16[2,72,1536]{2,1,0:T(8,128)(2,1)S(1)}, u32[]{:S(2)}, u32[]{:S(2)}) collective-permute-start(bf16[2,72,1536]{2,1,0:T(8,128)(2,1)S(1)} %slice.47), channel_id=1, source_target_pairs={{4,228},{12,236},{20,244},{28,252},{36,4},{44,12},{52,20},{60,28},... | collective-permute-start | bytes 1327112 | tf_op jit(solution)/shard_map/ppermute | solution.py:342
  106.0 1.9 %collective-permute-start.11 = (bf16[2,72,1536]{2,1,0:T(8,128)(2,1)S(1)}, bf16[2,72,1536]{2,1,0:T(8,128)(2,1)S(1)}, u32[]{:S(2)}, u32[]{:S(2)}) collective-permute-start(bf16[2,72,1536]{2,1,0:T(8,128)(2,1)S(1)} %slice.46), channel_id=1, source_target_pairs={{4,36},{12,44},{20,52},{28,60},{36,68},{44,76},{52,84},{60,92},{68... | collective-permute-start | bytes 1327112 | tf_op jit(solution)/shard_map/ppermute | solution.py:342
  107.9 3.3 %collective-permute-done.14.down_own = bf16[2,72,1536]{2,1,0:T(8,128)(2,1)S(1)} collective-permute-done((bf16[2,72,1536]{2,1,0:T(8,128)(2,1)S(1)}, bf16[2,72,1536]{2,1,0:T(8,128)(2,1)S(1)}, u32[]{:S(2)}, u32[]{:S(2)}) %collective-permute-start.14) | collective-permute-done | bytes 442400 | tf_op jit(solution)/shard_map/ppermute | solution.py:342
  111.2 1.3 collective-permute-start.16
  112.5 3.7 %collective-permute-done.11.up_own = bf16[2,72,1536]{2,1,0:T(8,128)(2,1)S(1)} collective-permute-done((bf16[2,72,1536]{2,1,0:T(8,128)(2,1)S(1)}, bf16[2,72,1536]{2,1,0:T(8,128)(2,1)S(1)}, u32[]{:S(2)}, u32[]{:S(2)}) %collective-permute-start.11) | collective-permute-done | bytes 442400 | tf_op jit(solution)/shard_map/ppermute | solution.py:342
  116.3 1.3 collective-permute-start.15
  117.6 11.9 %shard_map.112 = (bf16[512,4608]{1,0:T(8,128)(2,1)S(1)}, bf16[4608,1536]{1,0:T(8,128)(2,1)S(1)}) custom-call(s32[5]{0:T(128)S(1)} %stack.59.scal, s32[64]{0:T(128)S(1)} %reshape.236.table, bf16[128,4608]{1,0:T(8,128)(2,1)S(1)} %copy-done, bf16[128,4608]{1,0:T(8,128)(2,1)S(1)} %collective-permute-done.19.refs_1_, ...), custom_call_target="tpu_custom_call" | custom-call | bytes 18000000 | tf_op jit(solution)/shard_map/pallas_call | solution.py:139
  129.5 5.4 %shard_map.113 = (bf16[512,4608]{1,0:T(8,128)(2,1)S(1)}, bf16[4608,1536]{1,0:T(8,128)(2,1)S(1)}) custom-call(s32[5]{0:T(128)S(1)} %stack.59.scal, s32[64]{0:T(128)S(1)} %reshape.236.table, bf16[64,4608]{1,0:T(8,128)(2,1)S(1)} %collective-permute-done.20.refs_0_, ...), custom_call_target="tpu_custom_call", output_to_operand_aliasing={{0}: (8, {}), {1}: (9, {})} | custom-call | bytes 18000000 | tf_op jit(solution)/shard_map/pallas_call | solution.py:139
  135.0 2.9 %shard_map.114 = (bf16[512,4608]{1,0:T(8,128)(2,1)S(1)}, bf16[4608,1536]{1,0:T(8,128)(2,1)S(1)}) custom-call(s32[5]{0:T(128)S(1)} %stack.59.scal, s32[64]{0:T(128)S(1)} %reshape.236.table, bf16[4,72,1536]{2,1,0:T(8,128)(2,1)S(1)} %collective-permute-done.17.refs_0_, ...), custom_call_target="tpu_custom_call", output_to_operand_aliasing={{0}: (4, {}), {1}: (5, {})} | custom-call | bytes 18000000 | tf_op jit(solution)/shard_map/pallas_call | solution.py:139
  137.9 8.2 %project.1 = (bf16[512,256]{1,0:T(8,128)(2,1)}, bf16[512,256]{1,0:T(8,128)(2,1)}, bf16[64,4608]{1,0:T(8,128)(2,1)S(1)}, bf16[64,4608]{1,0:T(8,128)(2,1)S(1)}, bf16[4608,1536]{1,0:T(8,128)(2,1)S(1)}) custom-call(s32[5]{0:T(128)S(1)} %stack.59.scal, s32[64]{0:T(128)S(1)} %reshape.236.table, ...), custom_call_target="tpu_custom_call", output_to_operand_aliasing={{4}: (9, {})} | custom-call | flops 4000000000 | bytes 10000000 | tf_op jit(solution)/shard_map/project/pallas_call | solution.py:226
  146.2 3.2 %collective-permute-start.33 = (bf16[64,4608]{1,0:T(8,128)(2,1)S(1)}, bf16[64,4608]{1,0:T(8,128)(2,1)S(1)}, u32[]{:S(2)}, u32[]{:S(2)}) collective-permute-start(bf16[64,4608]{1,0:T(8,128)(2,1)S(1)} %get-tuple-element.46), channel_id=1, source_target_pairs={{0,3},{1,0},{2,1},{3,2},{4,7},{5,4},{6,5},{7,6},{8,11},{9,8},{10,9... | collective-permute-start | bytes 1769480 | tf_op jit(solution)/shard_map/ppermute | solution.py:34
  149.3 0.9 copy-done.5
  150.3 0.9 copy-done.7
  151.2 7.7 %shard_map.116 = (bf16[64,4608]{1,0:T(8,128)(2,1)S(1)}, bf16[64,4608]{1,0:T(8,128)(2,1)S(1)}, bf16[64,4608]{1,0:T(8,128)(2,1)S(1)}, bf16[64,4608]{1,0:T(8,128)(2,1)S(1)}) custom-call(s32[5]{0:T(128)S(1)} %stack.59.scal, f32[512,128]{1,0:T(8,128)S(1)} %get-tuple-element.26.cos_ref, f32[512,128]{1,0:T(8,128)S(1)} %get-tuple-element.27.sin_ref, ...), custom_call_target="tpu_custom_call" | custom-call | flops 2800000000 | bytes 3400000 | tf_op jit(solution)/shard_map/pallas_call | solution.py:271
  159.0 2.8 %collective-permute-start.30 = (bf16[64,4608]{1,0:T(8,128)(2,1)S(1)}, bf16[64,4608]{1,0:T(8,128)(2,1)S(1)}, u32[]{:S(2)}, u32[]{:S(2)}) collective-permute-start(bf16[64,4608]{1,0:T(8,128)(2,1)S(1)} %get-tuple-element.42), channel_id=1, source_target_pairs={{0,3},{1,0},{2,1},{3,2},{4,7},{5,4},{6,5},{7,6},{8,11},{9,8},{10,9... | collective-permute-start | bytes 1769480 | tf_op jit(solution)/shard_map/ppermute | solution.py:34
  161.9 3.5 %collective-permute-start.34 = (bf16[64,4608]{1,0:T(8,128)(2,1)S(1)}, bf16[64,4608]{1,0:T(8,128)(2,1)S(1)}, u32[]{:S(2)}, u32[]{:S(2)}) collective-permute-start(bf16[64,4608]{1,0:T(8,128)(2,1)S(1)} %add_convert_fusion), channel_id=1, source_target_pairs={{0,3},{1,0},{2,1},{3,2},{4,7},{5,4},{6,5},{7,6},{8,11},{9,8},{10,9... | collective-permute-start | bytes 1769480 | tf_op jit(solution)/shard_map/ppermute | solution.py:34
  166.1 5.1 %shard_map.115.own_ref = bf16[128,4608]{1,0:T(8,128)(2,1)S(1)} custom-call(s32[5]{0:T(128)S(1)} %stack.59.scal, f32[512,128]{1,0:T(8,128)S(1)} %get-tuple-element.26.cos_ref, f32[512,128]{1,0:T(8,128)S(1)} %get-tuple-element.27.sin_ref, bf16[512,256]{1,0:T(8,128)(2,1)S(1)} %copy-done.6, bf16[512,256]{1,0:T(8,128)(2,1)S(1)} %copy-done.8, ...), custom_call_target="tpu_custom_call" | custom-call | flops 1400000000 | bytes 2200000 | tf_op jit(solution)/shard_map/pallas_call | solution.py:271
  171.3 4.6 %collective-permute-done.29.a1 = bf16[64,4608]{1,0:T(8,128)(2,1)S(1)} collective-permute-done((bf16[64,4608]{1,0:T(8,128)(2,1)S(1)}, bf16[64,4608]{1,0:T(8,128)(2,1)S(1)}, u32[]{:S(2)}, u32[]{:S(2)}) %collective-permute-start.29) | collective-permute-done | bytes 589856 | tf_op jit(solution)/shard_map/ppermute | solution.py:34
  175.9 5.5 %collective-permute-done.34.b1_hbm = bf16[64,4608]{1,0:T(8,128)(2,1)S(1)} collective-permute-done((bf16[64,4608]{1,0:T(8,128)(2,1)S(1)}, bf16[64,4608]{1,0:T(8,128)(2,1)S(1)}, u32[]{:S(2)}, u32[]{:S(2)}) %collective-permute-start.34) | collective-permute-done | bytes 589856 | tf_op jit(solution)/shard_map/ppermute | solution.py:34
  182.2 2.8 %finish.1 = bf16[128,4608]{1,0:T(8,128)(2,1)} custom-call(s32[5]{0:T(128)S(1)} %stack.59.scal, bf16[128,4608]{1,0:T(8,128)(2,1)S(1)} %bitcast.47, bf16[128,4608]{1,0:T(8,128)(2,1)S(1)} %shard_map.115.own_ref, bf16[64,4608]{1,0:T(8,128)(2,1)S(1)} %collective-permute-done.29.a1, bf16[64,4608]{1,0:T(8,128)(2,1)S(1)} %collective-permute-done.30.b0, ...), custom_call_target="tpu_custom_call" | custom-call | flops 6000000 | bytes 7000000 | tf_op jit(solution)/shard_map/finish/pallas_call | solution.py:309
  (78 shorter events, 6.0 us)
Async XLA Ops:
  1.6 6.7 %collective-permute-start = (bf16[72,1536]{1,0:T(8,128)(2,1)S(1)}, bf16[72,1536]{1,0:T(8,128)(2,1)S(1)}, u32[]{:S(2)}, u32[]{:S(2)}) collective-permute-start(bf16[72,1536]{1,0:T(8,128)(2,1)S(1)} %get-tuple-element.51), channel_id=1, source_target_pairs={{0,32},{4,12},{8,40},{12,20},{16,48},{20,28},{24,56},{28,4},{32,64... | collective-permute-start | bytes 663560 | tf_op jit(solution)/shard_map/ppermute | solution.py:342
  3.7 5.1 %collective-permute-start.1 = (bf16[72,1536]{1,0:T(8,128)(2,1)S(1)}, bf16[72,1536]{1,0:T(8,128)(2,1)S(1)}, u32[]{:S(2)}, u32[]{:S(2)}) collective-permute-start(bf16[72,1536]{1,0:T(8,128)(2,1)S(1)} %get-tuple-element.51), channel_id=1, source_target_pairs={{0,224},{4,28},{8,232},{12,4},{16,240},{20,12},{24,248},{28,20},{3... | collective-permute-start | bytes 663560 | tf_op jit(solution)/shard_map/ppermute | solution.py:342
  8.3 6.1 %collective-permute-start.2 = (bf16[72,1536]{1,0:T(8,128)(2,1)S(1)}, bf16[72,1536]{1,0:T(8,128)(2,1)}, u32[]{:S(2)}, u32[]{:S(2)}) collective-permute-start(bf16[72,1536]{1,0:T(8,128)(2,1)S(1)} %collective-permute-done), channel_id=1, source_target_pairs={{0,32},{4,12},{8,40},{12,20},{16,48},{20,28},{24,56},{28,4},{32,64... | collective-permute-start | bytes 663560 | tf_op jit(solution)/shard_map/ppermute | solution.py:342
  14.4 9.4 %copy-start.12 = (s32[1,8,4,2]{1,2,3,0:T(4,128)S(1)}, s32[1,8,4,2]{1,2,3,0:T(4,128)}, u32[]{:S(2)}) copy-start(s32[1,8,4,2]{1,2,3,0:T(4,128)} %constant.108) | copy-start | bytes 772
  14.4 9.4 %copy-start.13 = (s32[1,8,4,2]{1,2,3,0:T(4,128)S(1)}, s32[1,8,4,2]{1,2,3,0:T(4,128)}, u32[]{:S(2)}) copy-start(s32[1,8,4,2]{1,2,3,0:T(4,128)} %constant.109) | copy-start | bytes 772
  15.5 28.1 %collective-permute-start.3 = (bf16[4,72,1536]{2,1,0:T(8,128)(2,1)S(1)}, bf16[4,72,1536]{2,1,0:T(8,128)(2,1)S(1)}, u32[]{:S(2)}, u32[]{:S(2)}) collective-permute-start(bf16[4,72,1536]{2,1,0:T(8,128)(2,1)S(1)} %pad_maximum_fusion.refs_3_), channel_id=1, source_target_pairs={{0,24},{4,228},{8,0},{12,236},{16,8},{20,244},{24,16},{28,252},{32... | collective-permute-start | bytes 2654216 | tf_op jit(solution)/shard_map/ppermute | solution.py:342
  21.6 22.8 %collective-permute-start.8 = (bf16[4,72,1536]{2,1,0:T(8,128)(2,1)S(1)}, bf16[4,72,1536]{2,1,0:T(8,128)(2,1)S(1)}, u32[]{:S(2)}, u32[]{:S(2)}) collective-permute-start(bf16[4,72,1536]{2,1,0:T(8,128)(2,1)S(1)} %pad_maximum_fusion.refs_3_), channel_id=1, source_target_pairs={{0,8},{4,36},{8,16},{12,44},{16,24},{20,52},{24,0},{28,60},{32,40}... | collective-permute-start | bytes 2654216 | tf_op jit(solution)/shard_map/ppermute | solution.py:342
  23.4 7.4 %collective-permute-start.4 = (bf16[72,1536]{1,0:T(8,128)(2,1)S(1)}, bf16[72,1536]{1,0:T(8,128)(2,1)S(1)}, u32[]{:S(2)}, u32[]{:S(2)}) collective-permute-start(bf16[72,1536]{1,0:T(8,128)(2,1)S(1)} %collective-permute-done.1), channel_id=1, source_target_pairs={{0,224},{4,28},{8,232},{12,4},{16,240},{20,12},{24,248},{28,20},{3... | collective-permute-start | bytes 663560 | tf_op jit(solution)/shard_map/ppermute | solution.py:342
  31.6 7.3 %collective-permute-start.6 = (bf16[72,1536]{1,0:T(8,128)(2,1)S(1)}, bf16[72,1536]{1,0:T(8,128)(2,1)}, u32[]{:S(2)}, u32[]{:S(2)}) collective-permute-start(bf16[72,1536]{1,0:T(8,128)(2,1)S(1)} %collective-permute-done.4), channel_id=1, source_target_pairs={{0,224},{4,28},{8,232},{12,4},{16,240},{20,12},{24,248},{28,20},{3... | collective-permute-start | bytes 663560 | tf_op jit(solution)/shard_map/ppermute | solution.py:342
  32.6 10.9 %collective-permute-start.5 = (bf16[72,1536]{1,0:T(8,128)(2,1)}, bf16[72,1536]{1,0:T(8,128)(2,1)}, u32[]{:S(2)}, u32[]{:S(2)}) collective-permute-start(bf16[72,1536]{1,0:T(8,128)(2,1)} %collective-permute-done.2), channel_id=1, source_target_pairs={{0,32},{4,12},{8,40},{12,20},{16,48},{20,28},{24,56},{28,4},{32,64... | collective-permute-start | bytes 663560 | tf_op jit(solution)/shard_map/ppermute | solution.py:342
  38.9 5.6 %collective-permute-start.7 = (bf16[72,1536]{1,0:T(8,128)(2,1)}, bf16[72,1536]{1,0:T(8,128)(2,1)}, u32[]{:S(2)}, u32[]{:S(2)}) collective-permute-start(bf16[72,1536]{1,0:T(8,128)(2,1)} %collective-permute-done.6), channel_id=1, source_target_pairs={{0,224},{4,28},{8,232},{12,4},{16,240},{20,12},{24,248},{28,20},{3... | collective-permute-start | bytes 663560 | tf_op jit(solution)/shard_map/ppermute | solution.py:342
  42.2 2.3 %copy-start.11 = (bf16[72,1536]{1,0:T(8,128)(2,1)S(1)}, bf16[72,1536]{1,0:T(8,128)(2,1)}, u32[]{:S(2)}) copy-start(bf16[72,1536]{1,0:T(8,128)(2,1)} %copy-done.10) | copy-start | bytes 663556
  44.5 3.2 %copy-start.2 = (bf16[4,72,1536]{2,1,0:T(8,128)(2,1)}, bf16[4,72,1536]{2,1,0:T(8,128)(2,1)S(1)}, u32[]{:S(2)}) copy-start(bf16[4,72,1536]{2,1,0:T(8,128)(2,1)S(1)} %collective-permute-done.8.refs_4_) | copy-start | bytes 2654212
  47.7 12.4 %collective-permute-start.12 = (bf16[4,72,1536]{2,1,0:T(8,128)(2,1)}, bf16[4,72,1536]{2,1,0:T(8,128)(2,1)S(1)}, u32[]{:S(2)}, u32[]{:S(2)}) collective-permute-start(bf16[4,72,1536]{2,1,0:T(8,128)(2,1)} %get-tuple-element.49), channel_id=1, source_target_pairs={{0,24},{4,228},{8,0},{12,236},{16,8},{20,244},{24,16},{28,252},{32... | collective-permute-start | bytes 2654216 | tf_op jit(solution)/shard_map/ppermute | solution.py:342
  51.7 23.9 %collective-permute-start.19 = (bf16[128,4608]{1,0:T(8,128)(2,1)}, bf16[128,4608]{1,0:T(8,128)(2,1)S(1)}, u32[]{:S(2)}, u32[]{:S(2)}) collective-permute-start(bf16[128,4608]{1,0:T(8,128)(2,1)} %norm.1.refs_0_), channel_id=1, source_target_pairs={{0,3},{1,0},{2,1},{3,2},{4,7},{5,4},{6,5},{7,6},{8,11},{9,8},{10,9... | collective-permute-start | bytes 3538952 | tf_op jit(solution)/shard_map/ppermute | solution.py:34
  54.5 24.6 %collective-permute-start.21 = (bf16[128,4608]{1,0:T(8,128)(2,1)}, bf16[128,4608]{1,0:T(8,128)(2,1)S(1)}, u32[]{:S(2)}, u32[]{:S(2)}) collective-permute-start(bf16[128,4608]{1,0:T(8,128)(2,1)} %norm.1.refs_0_), channel_id=1, source_target_pairs={{0,1},{1,2},{2,3},{3,0},{4,5},{5,6},{6,7},{7,4},{8,9},{9,10},{10,1... | collective-permute-start | bytes 3538952 | tf_op jit(solution)/shard_map/ppermute | solution.py:34
  54.5 26.8 %collective-permute-start.25 = (bf16[4,72,1536]{2,1,0:T(8,128)(2,1)S(1)}, bf16[4,72,1536]{2,1,0:T(8,128)(2,1)S(1)}, u32[]{:S(2)}, u32[]{:S(2)}) collective-permute-start(bf16[4,72,1536]{2,1,0:T(8,128)(2,1)S(1)} %pad_maximum_fusion.refs_3_), channel_id=1, source_target_pairs={{0,4},{4,0},{8,12},{12,8},{16,20},{20,16},{24,28},{28,24},{32,36},... | collective-permute-start | bytes 2654216 | tf_op jit(solution)/shard_map/ppermute | solution.py:30
  59.2 20.1 %collective-permute-start.9 = (bf16[4,72,1536]{2,1,0:T(8,128)(2,1)}, bf16[4,72,1536]{2,1,0:T(8,128)(2,1)S(1)}, u32[]{:S(2)}, u32[]{:S(2)}) collective-permute-start(bf16[4,72,1536]{2,1,0:T(8,128)(2,1)} %get-tuple-element.48), channel_id=1, source_target_pairs={{0,8},{4,36},{8,16},{12,44},{16,24},{20,52},{24,0},{28,60},{32,40}... | collective-permute-start | bytes 2654216 | tf_op jit(solution)/shard_map/ppermute | solution.py:342
  60.2 21.1 %copy-start.4 = (bf16[4,72,1536]{2,1,0:T(8,128)(2,1)S(1)}, bf16[4,72,1536]{2,1,0:T(8,128)(2,1)}, u32[]{:S(2)}) copy-start(bf16[4,72,1536]{2,1,0:T(8,128)(2,1)} %get-tuple-element.47.refs_11_) | copy-start | bytes 2654212
  60.2 33.3 %copy-start.3 = (bf16[4,72,1536]{2,1,0:T(8,128)(2,1)S(1)}, bf16[4,72,1536]{2,1,0:T(8,128)(2,1)}, u32[]{:S(2)}) copy-start(bf16[4,72,1536]{2,1,0:T(8,128)(2,1)} %copy-done.2) | copy-start | bytes 2654212
  60.2 36.7 %collective-permute-start.13 = (bf16[4,72,1536]{2,1,0:T(8,128)(2,1)S(1)}, bf16[4,72,1536]{2,1,0:T(8,128)(2,1)S(1)}, u32[]{:S(2)}, u32[]{:S(2)}) collective-permute-start(bf16[4,72,1536]{2,1,0:T(8,128)(2,1)S(1)} %broadcast_select_fusion), channel_id=1, source_target_pairs={{0,24},{4,228},{8,0},{12,236},{16,8},{20,244},{24,16},{28,252},{32... | collective-permute-start | bytes 2654216 | tf_op jit(solution)/shard_map/ppermute | solution.py:342
  75.7 11.6 %collective-permute-start.20 = (bf16[64,4608]{1,0:T(8,128)(2,1)S(1)}, bf16[64,4608]{1,0:T(8,128)(2,1)S(1)}, u32[]{:S(2)}, u32[]{:S(2)}) collective-permute-start(bf16[64,4608]{1,0:T(8,128)(2,1)S(1)} %slice.48), channel_id=1, source_target_pairs={{0,3},{1,0},{2,1},{3,2},{4,7},{5,4},{6,5},{7,6},{8,11},{9,8},{10,9... | collective-permute-start | bytes 1769480 | tf_op jit(solution)/shard_map/ppermute | solution.py:34
  79.1 38.4 %copy-start = (bf16[128,4608]{1,0:T(8,128)(2,1)S(1)}, bf16[128,4608]{1,0:T(8,128)(2,1)}, u32[]{:S(2)}) copy-start(bf16[128,4608]{1,0:T(8,128)(2,1)} %norm.1.refs_0_) | copy-start | bytes 3538948
  79.2 14.3 %collective-permute-start.22 = (bf16[64,4608]{1,0:T(8,128)(2,1)S(1)}, bf16[64,4608]{1,0:T(8,128)(2,1)S(1)}, u32[]{:S(2)}, u32[]{:S(2)}) collective-permute-start(bf16[64,4608]{1,0:T(8,128)(2,1)S(1)} %slice.49), channel_id=1, source_target_pairs={{0,1},{1,2},{2,3},{3,0},{4,5},{5,6},{6,7},{7,4},{8,9},{9,10},{10,1... | collective-permute-start | bytes 1769480 | tf_op jit(solution)/shard_map/ppermute | solution.py:34
  79.3 17.8 %collective-permute-start.10 = (bf16[4,72,1536]{2,1,0:T(8,128)(2,1)S(1)}, bf16[4,72,1536]{2,1,0:T(8,128)(2,1)S(1)}, u32[]{:S(2)}, u32[]{:S(2)}) collective-permute-start(bf16[4,72,1536]{2,1,0:T(8,128)(2,1)S(1)} %collective-permute-done.9.refs_6_), channel_id=1, source_target_pairs={{0,8},{4,36},{8,16},{12,44},{16,24},{20,52},{24,0},{28,60},{32,40}... | collective-permute-start | bytes 2654216 | tf_op jit(solution)/shard_map/ppermute | solution.py:342
  81.3 18.8 %collective-permute-start.28 = (bf16[4,72,1536]{2,1,0:T(8,128)(2,1)S(1)}, bf16[4,72,1536]{2,1,0:T(8,128)(2,1)S(1)}, u32[]{:S(2)}, u32[]{:S(2)}) collective-permute-start(bf16[4,72,1536]{2,1,0:T(8,128)(2,1)S(1)} %copy-done.4), channel_id=1, source_target_pairs={{0,4},{8,12},{16,20},{24,28},{32,36},{40,44},{48,52},{56,60},{64,6... | collective-permute-start | bytes 2654216 | tf_op jit(solution)/shard_map/ppermute | solution.py:347
  87.3 12.8 %collective-permute-start.27 = (bf16[4,72,1536]{2,1,0:T(8,128)(2,1)S(1)}, bf16[4,72,1536]{2,1,0:T(8,128)(2,1)S(1)}, u32[]{:S(2)}, u32[]{:S(2)}) collective-permute-start(bf16[4,72,1536]{2,1,0:T(8,128)(2,1)S(1)} %collective-permute-done.3.refs_5_), channel_id=1, source_target_pairs={{0,4},{4,0},{8,12},{12,8},{16,20},{20,16},{24,28},{28,24},{32,36},... | collective-permute-start | bytes 2654216 | tf_op jit(solution)/shard_map/ppermute | solution.py:30
  93.5 7.2 %collective-permute-start.26 = (bf16[4,72,1536]{2,1,0:T(8,128)(2,1)S(1)}, bf16[4,72,1536]{2,1,0:T(8,128)(2,1)S(1)}, u32[]{:S(2)}, u32[]{:S(2)}) collective-permute-start(bf16[4,72,1536]{2,1,0:T(8,128)(2,1)S(1)} %copy-done.3), channel_id=1, source_target_pairs={{0,4},{4,0},{8,12},{12,8},{16,20},{20,16},{24,28},{28,24},{32,36},... | collective-permute-start | bytes 2654216 | tf_op jit(solution)/shard_map/ppermute | solution.py:30
  96.9 9.1 %collective-permute-start.23 = (bf16[4,72,1536]{2,1,0:T(8,128)(2,1)S(1)}, bf16[4,72,1536]{2,1,0:T(8,128)(2,1)S(1)}, u32[]{:S(2)}, u32[]{:S(2)}) collective-permute-start(bf16[4,72,1536]{2,1,0:T(8,128)(2,1)S(1)} %collective-permute-done.9.refs_6_), channel_id=1, source_target_pairs={{0,4},{4,0},{8,12},{12,8},{16,20},{20,16},{24,28},{28,24},{32,36},... | collective-permute-start | bytes 2654216 | tf_op jit(solution)/shard_map/ppermute | solution.py:30
  97.1 32.5 %collective-permute-start.24 = (bf16[4,72,1536]{2,1,0:T(8,128)(2,1)S(1)}, bf16[4,72,1536]{2,1,0:T(8,128)(2,1)S(1)}, u32[]{:S(2)}, u32[]{:S(2)}) collective-permute-start(bf16[4,72,1536]{2,1,0:T(8,128)(2,1)S(1)} %collective-permute-done.12.refs_7_), channel_id=1, source_target_pairs={{0,4},{4,0},{8,12},{12,8},{16,20},{20,16},{24,28},{28,24},{32,36},... | collective-permute-start | bytes 2654216 | tf_op jit(solution)/shard_map/ppermute | solution.py:30
  100.1 34.9 %collective-permute-start.18 = (bf16[4,72,1536]{2,1,0:T(8,128)(2,1)S(1)}, bf16[4,72,1536]{2,1,0:T(8,128)(2,1)S(1)}, u32[]{:S(2)}, u32[]{:S(2)}) collective-permute-start(bf16[4,72,1536]{2,1,0:T(8,128)(2,1)S(1)} %collective-permute-done.13.refs_3_), channel_id=1, source_target_pairs={{0,4},{4,0},{8,12},{12,8},{16,20},{20,16},{24,28},{28,24},{32,36},... | collective-permute-start | bytes 2654216 | tf_op jit(solution)/shard_map/ppermute | solution.py:30
  100.2 34.8 %collective-permute-start.17 = (bf16[4,72,1536]{2,1,0:T(8,128)(2,1)S(1)}, bf16[4,72,1536]{2,1,0:T(8,128)(2,1)S(1)}, u32[]{:S(2)}, u32[]{:S(2)}) collective-permute-start(bf16[4,72,1536]{2,1,0:T(8,128)(2,1)S(1)} %collective-permute-done.10.refs_2_), channel_id=1, source_target_pairs={{0,4},{4,0},{8,12},{12,8},{16,20},{20,16},{24,28},{28,24},{32,36},... | collective-permute-start | bytes 2654216 | tf_op jit(solution)/shard_map/ppermute | solution.py:30
  100.7 10.6 %collective-permute-start.14 = (bf16[2,72,1536]{2,1,0:T(8,128)(2,1)S(1)}, bf16[2,72,1536]{2,1,0:T(8,128)(2,1)S(1)}, u32[]{:S(2)}, u32[]{:S(2)}) collective-permute-start(bf16[2,72,1536]{2,1,0:T(8,128)(2,1)S(1)} %slice.47), channel_id=1, source_target_pairs={{4,228},{12,236},{20,244},{28,252},{36,4},{44,12},{52,20},{60,28},... | collective-permute-start | bytes 1327112 | tf_op jit(solution)/shard_map/ppermute | solution.py:342
  106.0 10.3 %collective-permute-start.11 = (bf16[2,72,1536]{2,1,0:T(8,128)(2,1)S(1)}, bf16[2,72,1536]{2,1,0:T(8,128)(2,1)S(1)}, u32[]{:S(2)}, u32[]{:S(2)}) collective-permute-start(bf16[2,72,1536]{2,1,0:T(8,128)(2,1)S(1)} %slice.46), channel_id=1, source_target_pairs={{4,36},{12,44},{20,52},{28,60},{36,68},{44,76},{52,84},{60,92},{68... | collective-permute-start | bytes 1327112 | tf_op jit(solution)/shard_map/ppermute | solution.py:342
  111.2 26.7 %collective-permute-start.16 = (bf16[2,72,1536]{2,1,0:T(8,128)(2,1)S(1)}, bf16[2,72,1536]{2,1,0:T(8,128)(2,1)S(1)}, u32[]{:S(2)}, u32[]{:S(2)}) collective-permute-start(bf16[2,72,1536]{2,1,0:T(8,128)(2,1)S(1)} %collective-permute-done.14.down_own), channel_id=1, source_target_pairs={{4,0},{12,8},{20,16},{28,24},{36,32},{44,40},{52,48},{60,56},{68,6... | collective-permute-start | bytes 1327112 | tf_op jit(solution)/shard_map/ppermute | solution.py:347
  116.3 21.6 %collective-permute-start.15 = (bf16[2,72,1536]{2,1,0:T(8,128)(2,1)S(1)}, bf16[2,72,1536]{2,1,0:T(8,128)(2,1)S(1)}, u32[]{:S(2)}, u32[]{:S(2)}) collective-permute-start(bf16[2,72,1536]{2,1,0:T(8,128)(2,1)S(1)} %collective-permute-done.11.up_own), channel_id=1, source_target_pairs={{4,0},{12,8},{20,16},{28,24},{36,32},{44,40},{52,48},{60,56},{68,6... | collective-permute-start | bytes 1327112 | tf_op jit(solution)/shard_map/ppermute | solution.py:347
  146.2 15.6 %collective-permute-start.33 = (bf16[64,4608]{1,0:T(8,128)(2,1)S(1)}, bf16[64,4608]{1,0:T(8,128)(2,1)S(1)}, u32[]{:S(2)}, u32[]{:S(2)}) collective-permute-start(bf16[64,4608]{1,0:T(8,128)(2,1)S(1)} %get-tuple-element.46), channel_id=1, source_target_pairs={{0,3},{1,0},{2,1},{3,2},{4,7},{5,4},{6,5},{7,6},{8,11},{9,8},{10,9... | collective-permute-start | bytes 1769480 | tf_op jit(solution)/shard_map/ppermute | solution.py:34
  149.3 16.6 %collective-permute-start.31 = (bf16[64,4608]{1,0:T(8,128)(2,1)S(1)}, bf16[64,4608]{1,0:T(8,128)(2,1)S(1)}, u32[]{:S(2)}, u32[]{:S(2)}) collective-permute-start(bf16[64,4608]{1,0:T(8,128)(2,1)S(1)} %get-tuple-element.44), channel_id=1, source_target_pairs={{0,1},{1,2},{2,3},{3,0},{4,5},{5,6},{6,7},{7,4},{8,9},{9,10},{10,1... | collective-permute-start | bytes 1769480 | tf_op jit(solution)/shard_map/ppermute | solution.py:34
  149.3 1.0 copy-start.5
  150.3 0.9 copy-start.7
  158.9 16.9 %collective-permute-start.29 = (bf16[64,4608]{1,0:T(8,128)(2,1)S(1)}, bf16[64,4608]{1,0:T(8,128)(2,1)S(1)}, u32[]{:S(2)}, u32[]{:S(2)}) collective-permute-start(bf16[64,4608]{1,0:T(8,128)(2,1)S(1)} %get-tuple-element.41), channel_id=1, source_target_pairs={{0,1},{1,2},{2,3},{3,0},{4,5},{5,6},{6,7},{7,4},{8,9},{9,10},{10,1... | collective-permute-start | bytes 1769480 | tf_op jit(solution)/shard_map/ppermute | solution.py:34
  159.0 16.9 %collective-permute-start.30 = (bf16[64,4608]{1,0:T(8,128)(2,1)S(1)}, bf16[64,4608]{1,0:T(8,128)(2,1)S(1)}, u32[]{:S(2)}, u32[]{:S(2)}) collective-permute-start(bf16[64,4608]{1,0:T(8,128)(2,1)S(1)} %get-tuple-element.42), channel_id=1, source_target_pairs={{0,3},{1,0},{2,1},{3,2},{4,7},{5,4},{6,5},{7,6},{8,11},{9,8},{10,9... | collective-permute-start | bytes 1769480 | tf_op jit(solution)/shard_map/ppermute | solution.py:34
  161.9 4.2 %copy-start.6 = (bf16[512,256]{1,0:T(8,128)(2,1)S(1)}, bf16[512,256]{1,0:T(8,128)(2,1)}, u32[]{:S(2)}) copy-start(bf16[512,256]{1,0:T(8,128)(2,1)} %get-tuple-element.38.k_ref) | copy-start | bytes 786436
  161.9 4.2 %copy-start.8 = (bf16[512,256]{1,0:T(8,128)(2,1)S(1)}, bf16[512,256]{1,0:T(8,128)(2,1)}, u32[]{:S(2)}) copy-start(bf16[512,256]{1,0:T(8,128)(2,1)} %get-tuple-element.39.v_ref) | copy-start | bytes 786436
  161.9 19.5 %collective-permute-start.34 = (bf16[64,4608]{1,0:T(8,128)(2,1)S(1)}, bf16[64,4608]{1,0:T(8,128)(2,1)S(1)}, u32[]{:S(2)}, u32[]{:S(2)}) collective-permute-start(bf16[64,4608]{1,0:T(8,128)(2,1)S(1)} %add_convert_fusion), channel_id=1, source_target_pairs={{0,3},{1,0},{2,1},{3,2},{4,7},{5,4},{6,5},{7,6},{8,11},{9,8},{10,9... | collective-permute-start | bytes 1769480 | tf_op jit(solution)/shard_map/ppermute | solution.py:34
  166.0 16.2 %copy-start.1 = (bf16[1,128,4608]{2,1,0:T(8,128)(2,1)S(1)}, bf16[1,128,4608]{2,1,0:T(8,128)(2,1)}, u32[]{:S(2)}) copy-start(bf16[1,128,4608]{2,1,0:T(8,128)(2,1)} %param.9) | copy-start | bytes 3538948
  166.0 16.2 %copy-start.9 = (f32[4608]{0:T(1024)S(1)}, f32[4608]{0:T(1024)}, u32[]{:S(2)}) copy-start(f32[4608]{0:T(1024)} %gain_ref.3) | copy-start | bytes 55300
  166.0 16.2 %collective-permute-start.32 = (bf16[64,4608]{1,0:T(8,128)(2,1)S(1)}, bf16[64,4608]{1,0:T(8,128)(2,1)S(1)}, u32[]{:S(2)}, u32[]{:S(2)}) collective-permute-start(bf16[64,4608]{1,0:T(8,128)(2,1)S(1)} %add_convert_fusion.1), channel_id=1, source_target_pairs={{0,1},{1,2},{2,3},{3,0},{4,5},{5,6},{6,7},{7,4},{8,9},{9,10},{10,1... | collective-permute-start | bytes 1769480 | tf_op jit(solution)/shard_map/ppermute | solution.py:34
  (1 other events, 0.7 us)

commit v2 on v1

--- a/solution.py
+++ b/solution.py
@@ -90,7 +90,10 @@
 
 def start(pairs, sem):
     for src, dst in pairs:
-        pltpu.make_async_copy(src, dst, sem).start()
+        half = src.shape[-1] // 2
+        for part in range(2):
+            cols = pl.ds(part * half, half)
+            pltpu.make_async_copy(src.at[:, cols], dst.at[:, cols], sem).start()
 
 
 def finished(target, rows, sem):
@@ -113,8 +116,7 @@
     ws, refs = refs[: len(groups)], refs[len(groups) :]
     either, (xbuf, wbuf, sem) = refs[:-3][: -n_old or None], refs[-3:]
 
-    for ref, at in zip(xs, offsets):
-        pltpu.make_async_copy(ref, rows_of(xbuf, y, *at, ref.shape[0]), sem.at[0]).start()
+    start([(ref, rows_of(xbuf, y, *at, ref.shape[0])) for ref, at in zip(xs, offsets)], sem.at[0])
     for ref, group in zip(ws, groups):
         start(shards_of(ref, table, wbuf, group * 4), sem.at[1])
     if either:
@@ -285,8 +287,8 @@
     y, length = scal[3], scal[4]
     first = pltpu.make_async_copy(a0_hbm, a0, sem.at[0])
     second = pltpu.make_async_copy(b1_hbm, b1, sem.at[1])
-    first.start()
-    second.start()
+    start([(a0_hbm, a0)], sem.at[0])
+    start([(b1_hbm, b1)], sem.at[1])
     gain = gain_ref[...]
     count = 32
     for i in range(4):
@@ -300,7 +302,7 @@
         post = total * lax.rsqrt(mean + 1e-06) * gain
         row = lax.broadcasted_iota(jnp.int32, (count, 1), 0) + y * 128 + i * count
         out[rows, :] = jnp.where(row < length, rows_ref[rows, :].astype(F32) + post, 0.0).astype(BF16)
-        pltpu.make_async_copy(out.at[rows], out_hbm.at[rows], osem).start()
+        start([(out.at[rows], out_hbm.at[rows])], osem)
     pltpu.make_async_copy(out, out_hbm, osem).wait()
 
 

time: 186 us -> 175 us (0.941)
  Pallas kernels: 46.6 us -> 29.7 us
  waiting for transfers between devices: 59.8 us -> 68.1 us
    pallas_call x3, Pallas kernels: 20.3 us -> 4.29 us  [fill(): pl.pallas_call(functools.partial(fill_kernel, offsets, groups, len(held))...]
    ppermute x10, waiting for transfers between devices: 29 us -> 37.3 us  [column(): return lax.ppermute(array, 'mp', [(y, (y + dy) % NY) for y in range(NY)])]
  transfers between devices with their start and end apart: 35 -> 35, of which waited for: 15 -> 15; matrix products, arithmetic and copies ran while one was open for 2% -> 2% of each run, Pallas kernels for 19% -> 11%
where the time goes in v2:
time: 175 us
  waiting for transfers between devices  68.1 us (39%)
  starting transfers between devices  63.3 us (36%)
  Pallas kernels  29.7 us (17%)
  other arithmetic  8.84 us (5%)
  local copies, waits for them, and re-layouts  3.04 us (2%)
  between operations  1.86 us (1%)
    ppermute x10, waiting for transfers between devices, column(): return lax.ppermute(array, 'mp', [(y, (y + dy) % NY) for y in range(NY)])  37.3 us
    ppermute x15, waiting for transfers between devices, torus(): return lax.ppermute(array, 'dp', pairs)  30.7 us
    ppermute x15, starting transfers between devices, torus(): return lax.ppermute(array, 'dp', pairs)  27.5 us
    ppermute x7, starting transfers between devices, plane(): return lax.ppermute(array, 'dp', pairs)  17.9 us
    ppermute x10, starting transfers between devices, column(): return lax.ppermute(array, 'mp', [(y, (y + dy) % NY) for y in range(NY)])  14 us
    pallas_call x2, Pallas kernels, attend(): pl.pallas_call(functools.partial(attend_kernel, blocks, outs), in_specs=[...  12.8 us
    pallas_call x1, Pallas kernels, project(): pl.pallas_call(project_kernel, in_specs=[SMEM] * 2 + [VMEM] * 2 + [ANY] *...  7.44 us
    pallas_call x3, Pallas kernels, fill(): pl.pallas_call(functools.partial(fill_kernel, offsets, groups, len(held))...  4.29 us
  transfers between devices with their start and end apart: 35, of which 15 were waited for; matrix products, arithmetic and copies ran while one was open for 2% of the time, Pallas kernels for 11%

profile of v2, /device:TPU:1, one launch (start us, length us, event | category | flops | bytes accessed | tf_op | source)
XLA Modules:
  0.0 174.8 jit_solution(2926603685013992500)
XLA Ops:
  0.6 1.0 fusion.19
  1.6 2.1 %collective-permute-start = (bf16[72,1536]{1,0:T(8,128)(2,1)S(1)}, bf16[72,1536]{1,0:T(8,128)(2,1)S(1)}, u32[]{:S(2)}, u32[]{:S(2)}) collective-permute-start(bf16[72,1536]{1,0:T(8,128)(2,1)S(1)} %get-tuple-element.51), channel_id=1, source_target_pairs={{0,32},{4,12},{8,40},{12,20},{16,48},{20,28},{24,56},{28,4},{32,64... | collective-permute-start | bytes 663560 | tf_op jit(solution)/shard_map/ppermute | solution.py:344
  3.7 1.4 collective-permute-start.1
  5.1 3.2 %collective-permute-done = bf16[72,1536]{1,0:T(8,128)(2,1)S(1)} collective-permute-done((bf16[72,1536]{1,0:T(8,128)(2,1)S(1)}, bf16[72,1536]{1,0:T(8,128)(2,1)S(1)}, u32[]{:S(2)}, u32[]{:S(2)}) %collective-permute-start) | collective-permute-done | bytes 221216 | tf_op jit(solution)/shard_map/ppermute | solution.py:344
  8.8 5.6 %collective-permute-done.2 = bf16[72,1536]{1,0:T(8,128)(2,1)} collective-permute-done((bf16[72,1536]{1,0:T(8,128)(2,1)S(1)}, bf16[72,1536]{1,0:T(8,128)(2,1)}, u32[]{:S(2)}, u32[]{:S(2)}) %collective-permute-start.2) | collective-permute-done | bytes 221216 | tf_op jit(solution)/shard_map/ppermute | solution.py:344
  14.4 1.1 pad_maximum_fusion.refs_3_
  15.5 6.1 %collective-permute-start.3 = (bf16[4,72,1536]{2,1,0:T(8,128)(2,1)S(1)}, bf16[4,72,1536]{2,1,0:T(8,128)(2,1)S(1)}, u32[]{:S(2)}, u32[]{:S(2)}) collective-permute-start(bf16[4,72,1536]{2,1,0:T(8,128)(2,1)S(1)} %pad_maximum_fusion.refs_3_), channel_id=1, source_target_pairs={{0,24},{4,228},{8,0},{12,236},{16,8},{20,244},{24,16},{28,252},{32... | collective-permute-start | bytes 2654216 | tf_op jit(solution)/shard_map/ppermute | solution.py:344
  21.7 1.8 %fusion = (f32[512,64]{1,0:T(8,128)S(1)}, f32[512,64]{1,0:T(8,128)}, f32[512,64]{1,0:T(8,128)}) fusion(f32[64]{0:T(128)S(1)} %multiply_power_fusion, f32[512]{0:T(512)S(1)} %iota_convert_fusion), kind=kLoop, calls=%fused_computation.12 | loop fusion | flops 65536 | bytes 395520 | tf_op jit(solution)/shard_map/neg | solution.py:334
  23.8 7.1 %collective-permute-done.4 = bf16[72,1536]{1,0:T(8,128)(2,1)S(1)} collective-permute-done((bf16[72,1536]{1,0:T(8,128)(2,1)S(1)}, bf16[72,1536]{1,0:T(8,128)(2,1)S(1)}, u32[]{:S(2)}, u32[]{:S(2)}) %collective-permute-start.4) | collective-permute-done | bytes 221216 | tf_op jit(solution)/shard_map/ppermute | solution.py:344
  31.6 1.0 collective-permute-start.6
  33.1 5.7 %collective-permute-done.6 = bf16[72,1536]{1,0:T(8,128)(2,1)} collective-permute-done((bf16[72,1536]{1,0:T(8,128)(2,1)S(1)}, bf16[72,1536]{1,0:T(8,128)(2,1)}, u32[]{:S(2)}, u32[]{:S(2)}) %collective-permute-start.6) | collective-permute-done | bytes 221216 | tf_op jit(solution)/shard_map/ppermute | solution.py:344
  38.9 2.4 %collective-permute-start.7 = (bf16[72,1536]{1,0:T(8,128)(2,1)}, bf16[72,1536]{1,0:T(8,128)(2,1)}, u32[]{:S(2)}, u32[]{:S(2)}) collective-permute-start(bf16[72,1536]{1,0:T(8,128)(2,1)} %collective-permute-done.6), channel_id=1, source_target_pairs={{0,224},{4,28},{8,232},{12,4},{16,240},{20,12},{24,248},{28,20},{3... | collective-permute-start | bytes 663560 | tf_op jit(solution)/shard_map/ppermute | solution.py:344
  42.2 1.4 pad_maximum_fusion.2
  44.5 3.2 %pad_maximum_fusion.1 = (bf16[4,72,1536]{2,1,0:T(8,128)(2,1)}, bf16[4,72,1536]{2,1,0:T(8,128)(2,1)}, bf16[4,72,1536]{2,1,0:T(8,128)(2,1)}) fusion(bf16[1,72,1536]{2,1,0:T(8,128)(2,1)} %bitcast.19, bf16[1,72,1536]{2,1,0:T(8,128)(2,1)} %bitcast.18, bf16[1,72,1536]{2,1,0:T(8,128)(2,1)} %bitcast.17, bf16[1,72,1536]{2,1,0:T(8,128)(2,1)S(1)} %bitcast.53, ...), kind=kLoop, calls=%fused_computation.3 | loop fusion | flops 2211840 | bytes 5308417 | tf_op jit(solution)/shard_map/stack | solution.py:397
  47.7 1.5 collective-permute-start.12
  49.2 2.5 %norm.1.refs_0_ = bf16[128,4608]{1,0:T(8,128)(2,1)} custom-call(bf16[128,4608]{1,0:T(8,128)(2,1)} %bitcast.46, f32[4608]{0:T(1024)} %gain_ref.2), custom_call_target="tpu_custom_call" | custom-call | flops 2000000 | bytes 2400000 | tf_op jit(solution)/shard_map/norm/pallas_call | solution.py:46
  51.7 2.7 %collective-permute-start.19 = (bf16[128,4608]{1,0:T(8,128)(2,1)}, bf16[128,4608]{1,0:T(8,128)(2,1)S(1)}, u32[]{:S(2)}, u32[]{:S(2)}) collective-permute-start(bf16[128,4608]{1,0:T(8,128)(2,1)} %norm.1.refs_0_), channel_id=1, source_target_pairs={{0,3},{1,0},{2,1},{3,2},{4,7},{5,4},{6,5},{7,6},{8,11},{9,8},{10,9... | collective-permute-start | bytes 3538952 | tf_op jit(solution)/shard_map/ppermute | solution.py:34
  54.5 4.7 %collective-permute-start.25 = (bf16[4,72,1536]{2,1,0:T(8,128)(2,1)S(1)}, bf16[4,72,1536]{2,1,0:T(8,128)(2,1)S(1)}, u32[]{:S(2)}, u32[]{:S(2)}) collective-permute-start(bf16[4,72,1536]{2,1,0:T(8,128)(2,1)S(1)} %pad_maximum_fusion.refs_3_), channel_id=1, source_target_pairs={{0,4},{4,0},{8,12},{12,8},{16,20},{20,16},{24,28},{28,24},{32,36},... | collective-permute-start | bytes 2654216 | tf_op jit(solution)/shard_map/ppermute | solution.py:30
  60.2 2.6 %collective-permute-start.13 = (bf16[4,72,1536]{2,1,0:T(8,128)(2,1)S(1)}, bf16[4,72,1536]{2,1,0:T(8,128)(2,1)S(1)}, u32[]{:S(2)}, u32[]{:S(2)}) collective-permute-start(bf16[4,72,1536]{2,1,0:T(8,128)(2,1)S(1)} %broadcast_select_fusion), channel_id=1, source_target_pairs={{0,24},{4,228},{8,0},{12,236},{16,8},{20,244},{24,16},{28,252},{32... | collective-permute-start | bytes 2654216 | tf_op jit(solution)/shard_map/ppermute | solution.py:344
  62.8 12.8 %collective-permute-done.19.refs_1_ = bf16[128,4608]{1,0:T(8,128)(2,1)S(1)} collective-permute-done((bf16[128,4608]{1,0:T(8,128)(2,1)}, bf16[128,4608]{1,0:T(8,128)(2,1)S(1)}, u32[]{:S(2)}, u32[]{:S(2)}) %collective-permute-start.19) | collective-permute-done | bytes 1179680 | tf_op jit(solution)/shard_map/ppermute | solution.py:34
  75.7 3.4 %collective-permute-start.20 = (bf16[64,4608]{1,0:T(8,128)(2,1)S(1)}, bf16[64,4608]{1,0:T(8,128)(2,1)S(1)}, u32[]{:S(2)}, u32[]{:S(2)}) collective-permute-start(bf16[64,4608]{1,0:T(8,128)(2,1)S(1)} %slice.48), channel_id=1, source_target_pairs={{0,3},{1,0},{2,1},{3,2},{4,7},{5,4},{6,5},{7,6},{8,11},{9,8},{10,9... | collective-permute-start | bytes 1769480 | tf_op jit(solution)/shard_map/ppermute | solution.py:34
  79.3 2.0 %collective-permute-start.10 = (bf16[4,72,1536]{2,1,0:T(8,128)(2,1)S(1)}, bf16[4,72,1536]{2,1,0:T(8,128)(2,1)S(1)}, u32[]{:S(2)}, u32[]{:S(2)}) collective-permute-start(bf16[4,72,1536]{2,1,0:T(8,128)(2,1)S(1)} %collective-permute-done.9.refs_6_), channel_id=1, source_target_pairs={{0,8},{4,36},{8,16},{12,44},{16,24},{20,52},{24,0},{28,60},{32,40}... | collective-permute-start | bytes 2654216 | tf_op jit(solution)/shard_map/ppermute | solution.py:344
  81.3 1.3 collective-permute-start.28
  82.6 4.8 %collective-permute-done.20.refs_0_ = bf16[64,4608]{1,0:T(8,128)(2,1)S(1)} collective-permute-done((bf16[64,4608]{1,0:T(8,128)(2,1)S(1)}, bf16[64,4608]{1,0:T(8,128)(2,1)S(1)}, u32[]{:S(2)}, u32[]{:S(2)}) %collective-permute-start.20) | collective-permute-done | bytes 589856 | tf_op jit(solution)/shard_map/ppermute | solution.py:34
  87.3 6.1 %collective-permute-start.27 = (bf16[4,72,1536]{2,1,0:T(8,128)(2,1)S(1)}, bf16[4,72,1536]{2,1,0:T(8,128)(2,1)S(1)}, u32[]{:S(2)}, u32[]{:S(2)}) collective-permute-start(bf16[4,72,1536]{2,1,0:T(8,128)(2,1)S(1)} %collective-permute-done.3.refs_5_), channel_id=1, source_target_pairs={{0,4},{4,0},{8,12},{12,8},{16,20},{20,16},{24,28},{28,24},{32,36},... | collective-permute-start | bytes 2654216 | tf_op jit(solution)/shard_map/ppermute | solution.py:30
  93.5 3.4 %collective-permute-start.26 = (bf16[4,72,1536]{2,1,0:T(8,128)(2,1)S(1)}, bf16[4,72,1536]{2,1,0:T(8,128)(2,1)S(1)}, u32[]{:S(2)}, u32[]{:S(2)}) collective-permute-start(bf16[4,72,1536]{2,1,0:T(8,128)(2,1)S(1)} %copy-done.3), channel_id=1, source_target_pairs={{0,4},{4,0},{8,12},{12,8},{16,20},{20,16},{24,28},{28,24},{32,36},... | collective-permute-start | bytes 2654216 | tf_op jit(solution)/shard_map/ppermute | solution.py:30
  97.1 3.0 %collective-permute-start.24 = (bf16[4,72,1536]{2,1,0:T(8,128)(2,1)S(1)}, bf16[4,72,1536]{2,1,0:T(8,128)(2,1)S(1)}, u32[]{:S(2)}, u32[]{:S(2)}) collective-permute-start(bf16[4,72,1536]{2,1,0:T(8,128)(2,1)S(1)} %collective-permute-done.12.refs_7_), channel_id=1, source_target_pairs={{0,4},{4,0},{8,12},{12,8},{16,20},{20,16},{24,28},{28,24},{32,36},... | collective-permute-start | bytes 2654216 | tf_op jit(solution)/shard_map/ppermute | solution.py:30
  100.7 5.3 %collective-permute-start.14 = (bf16[2,72,1536]{2,1,0:T(8,128)(2,1)S(1)}, bf16[2,72,1536]{2,1,0:T(8,128)(2,1)S(1)}, u32[]{:S(2)}, u32[]{:S(2)}) collective-permute-start(bf16[2,72,1536]{2,1,0:T(8,128)(2,1)S(1)} %slice.47), channel_id=1, source_target_pairs={{4,228},{12,236},{20,244},{28,252},{36,4},{44,12},{52,20},{60,28},... | collective-permute-start | bytes 1327112 | tf_op jit(solution)/shard_map/ppermute | solution.py:344
  106.0 1.9 %collective-permute-start.11 = (bf16[2,72,1536]{2,1,0:T(8,128)(2,1)S(1)}, bf16[2,72,1536]{2,1,0:T(8,128)(2,1)S(1)}, u32[]{:S(2)}, u32[]{:S(2)}) collective-permute-start(bf16[2,72,1536]{2,1,0:T(8,128)(2,1)S(1)} %slice.46), channel_id=1, source_target_pairs={{4,36},{12,44},{20,52},{28,60},{36,68},{44,76},{52,84},{60,92},{68... | collective-permute-start | bytes 1327112 | tf_op jit(solution)/shard_map/ppermute | solution.py:344
  107.9 3.3 %collective-permute-done.14.down_own = bf16[2,72,1536]{2,1,0:T(8,128)(2,1)S(1)} collective-permute-done((bf16[2,72,1536]{2,1,0:T(8,128)(2,1)S(1)}, bf16[2,72,1536]{2,1,0:T(8,128)(2,1)S(1)}, u32[]{:S(2)}, u32[]{:S(2)}) %collective-permute-start.14) | collective-permute-done | bytes 442400 | tf_op jit(solution)/shard_map/ppermute | solution.py:344
  111.2 1.3 collective-permute-start.16
  112.5 3.7 %collective-permute-done.11.up_own = bf16[2,72,1536]{2,1,0:T(8,128)(2,1)S(1)} collective-permute-done((bf16[2,72,1536]{2,1,0:T(8,128)(2,1)S(1)}, bf16[2,72,1536]{2,1,0:T(8,128)(2,1)S(1)}, u32[]{:S(2)}, u32[]{:S(2)}) %collective-permute-start.11) | collective-permute-done | bytes 442400 | tf_op jit(solution)/shard_map/ppermute | solution.py:344
  116.3 1.3 collective-permute-start.15
  117.6 2.2 %shard_map.112 = (bf16[512,4608]{1,0:T(8,128)(2,1)S(1)}, bf16[4608,1536]{1,0:T(8,128)(2,1)S(1)}) custom-call(s32[5]{0:T(128)S(1)} %stack.59.scal, s32[64]{0:T(128)S(1)} %reshape.236.table, bf16[128,4608]{1,0:T(8,128)(2,1)S(1)} %copy-done, bf16[128,4608]{1,0:T(8,128)(2,1)S(1)} %collective-permute-done.19.refs_1_, ...), custom_call_target="tpu_custom_call" | custom-call | bytes 18000000 | tf_op jit(solution)/shard_map/pallas_call | solution.py:141
  119.8 1.2 shard_map.113
  122.0 7.4 %project.1 = (bf16[512,256]{1,0:T(8,128)(2,1)}, bf16[512,256]{1,0:T(8,128)(2,1)}, bf16[64,4608]{1,0:T(8,128)(2,1)S(1)}, bf16[64,4608]{1,0:T(8,128)(2,1)S(1)}, bf16[4608,1536]{1,0:T(8,128)(2,1)S(1)}) custom-call(s32[5]{0:T(128)S(1)} %stack.59.scal, s32[64]{0:T(128)S(1)} %reshape.236.table, ...), custom_call_target="tpu_custom_call", output_to_operand_aliasing={{4}: (9, {})} | custom-call | flops 4000000000 | bytes 10000000 | tf_op jit(solution)/shard_map/project/pallas_call | solution.py:228
  129.4 2.9 %collective-permute-start.33 = (bf16[64,4608]{1,0:T(8,128)(2,1)S(1)}, bf16[64,4608]{1,0:T(8,128)(2,1)S(1)}, u32[]{:S(2)}, u32[]{:S(2)}) collective-permute-start(bf16[64,4608]{1,0:T(8,128)(2,1)S(1)} %get-tuple-element.46), channel_id=1, source_target_pairs={{0,3},{1,0},{2,1},{3,2},{4,7},{5,4},{6,5},{7,6},{8,11},{9,8},{10,9... | collective-permute-start | bytes 1769480 | tf_op jit(solution)/shard_map/ppermute | solution.py:34
  132.3 0.9 copy-done.5
  133.3 0.9 copy-done.7
  134.2 7.7 %shard_map.116 = (bf16[64,4608]{1,0:T(8,128)(2,1)S(1)}, bf16[64,4608]{1,0:T(8,128)(2,1)S(1)}, bf16[64,4608]{1,0:T(8,128)(2,1)S(1)}, bf16[64,4608]{1,0:T(8,128)(2,1)S(1)}) custom-call(s32[5]{0:T(128)S(1)} %stack.59.scal, f32[512,128]{1,0:T(8,128)S(1)} %get-tuple-element.26.cos_ref, f32[512,128]{1,0:T(8,128)S(1)} %get-tuple-element.27.sin_ref, ...), custom_call_target="tpu_custom_call" | custom-call | flops 2800000000 | bytes 3400000 | tf_op jit(solution)/shard_map/pallas_call | solution.py:273
  142.0 2.8 %collective-permute-start.30 = (bf16[64,4608]{1,0:T(8,128)(2,1)S(1)}, bf16[64,4608]{1,0:T(8,128)(2,1)S(1)}, u32[]{:S(2)}, u32[]{:S(2)}) collective-permute-start(bf16[64,4608]{1,0:T(8,128)(2,1)S(1)} %get-tuple-element.42), channel_id=1, source_target_pairs={{0,3},{1,0},{2,1},{3,2},{4,7},{5,4},{6,5},{7,6},{8,11},{9,8},{10,9... | collective-permute-start | bytes 1769480 | tf_op jit(solution)/shard_map/ppermute | solution.py:34
  145.0 1.7 collective-permute-start.34
  146.7 2.2 %collective-permute-done.31 = bf16[64,4608]{1,0:T(8,128)(2,1)S(1)} collective-permute-done((bf16[64,4608]{1,0:T(8,128)(2,1)S(1)}, bf16[64,4608]{1,0:T(8,128)(2,1)S(1)}, u32[]{:S(2)}, u32[]{:S(2)}) %collective-permute-start.31) | collective-permute-done | bytes 589856 | tf_op jit(solution)/shard_map/ppermute | solution.py:34
  149.4 5.1 %shard_map.115.own_ref = bf16[128,4608]{1,0:T(8,128)(2,1)S(1)} custom-call(s32[5]{0:T(128)S(1)} %stack.59.scal, f32[512,128]{1,0:T(8,128)S(1)} %get-tuple-element.26.cos_ref, f32[512,128]{1,0:T(8,128)S(1)} %get-tuple-element.27.sin_ref, bf16[512,256]{1,0:T(8,128)(2,1)S(1)} %copy-done.6, bf16[512,256]{1,0:T(8,128)(2,1)S(1)} %copy-done.8, ...), custom_call_target="tpu_custom_call" | custom-call | flops 1400000000 | bytes 2200000 | tf_op jit(solution)/shard_map/pallas_call | solution.py:273
  154.5 7.0 %collective-permute-done.29.a1 = bf16[64,4608]{1,0:T(8,128)(2,1)S(1)} collective-permute-done((bf16[64,4608]{1,0:T(8,128)(2,1)S(1)}, bf16[64,4608]{1,0:T(8,128)(2,1)S(1)}, u32[]{:S(2)}, u32[]{:S(2)}) %collective-permute-start.29) | collective-permute-done | bytes 589856 | tf_op jit(solution)/shard_map/ppermute | solution.py:34
  161.5 7.4 %collective-permute-done.34.b1_hbm = bf16[64,4608]{1,0:T(8,128)(2,1)S(1)} collective-permute-done((bf16[64,4608]{1,0:T(8,128)(2,1)S(1)}, bf16[64,4608]{1,0:T(8,128)(2,1)S(1)}, u32[]{:S(2)}, u32[]{:S(2)}) %collective-permute-start.34) | collective-permute-done | bytes 589856 | tf_op jit(solution)/shard_map/ppermute | solution.py:34
  169.0 3.0 %collective-permute-done.32.a0_hbm = bf16[64,4608]{1,0:T(8,128)(2,1)S(1)} collective-permute-done((bf16[64,4608]{1,0:T(8,128)(2,1)S(1)}, bf16[64,4608]{1,0:T(8,128)(2,1)S(1)}, u32[]{:S(2)}, u32[]{:S(2)}) %collective-permute-start.32) | collective-permute-done | bytes 589856 | tf_op jit(solution)/shard_map/ppermute | solution.py:34
  172.0 2.6 %finish.1 = bf16[128,4608]{1,0:T(8,128)(2,1)} custom-call(s32[5]{0:T(128)S(1)} %stack.59.scal, bf16[128,4608]{1,0:T(8,128)(2,1)S(1)} %bitcast.47, bf16[128,4608]{1,0:T(8,128)(2,1)S(1)} %shard_map.115.own_ref, bf16[64,4608]{1,0:T(8,128)(2,1)S(1)} %collective-permute-done.29.a1, bf16[64,4608]{1,0:T(8,128)(2,1)S(1)} %collective-permute-done.30.b0, ...), custom_call_target="tpu_custom_call" | custom-call | flops 6000000 | bytes 7000000 | tf_op jit(solution)/shard_map/finish/pallas_call | solution.py:311
  (78 shorter events, 6.8 us)
Async XLA Ops:
  1.6 6.7 %collective-permute-start = (bf16[72,1536]{1,0:T(8,128)(2,1)S(1)}, bf16[72,1536]{1,0:T(8,128)(2,1)S(1)}, u32[]{:S(2)}, u32[]{:S(2)}) collective-permute-start(bf16[72,1536]{1,0:T(8,128)(2,1)S(1)} %get-tuple-element.51), channel_id=1, source_target_pairs={{0,32},{4,12},{8,40},{12,20},{16,48},{20,28},{24,56},{28,4},{32,64... | collective-permute-start | bytes 663560 | tf_op jit(solution)/shard_map/ppermute | solution.py:344
  3.7 5.1 %collective-permute-start.1 = (bf16[72,1536]{1,0:T(8,128)(2,1)S(1)}, bf16[72,1536]{1,0:T(8,128)(2,1)S(1)}, u32[]{:S(2)}, u32[]{:S(2)}) collective-permute-start(bf16[72,1536]{1,0:T(8,128)(2,1)S(1)} %get-tuple-element.51), channel_id=1, source_target_pairs={{0,224},{4,28},{8,232},{12,4},{16,240},{20,12},{24,248},{28,20},{3... | collective-permute-start | bytes 663560 | tf_op jit(solution)/shard_map/ppermute | solution.py:344
  8.3 6.1 %collective-permute-start.2 = (bf16[72,1536]{1,0:T(8,128)(2,1)S(1)}, bf16[72,1536]{1,0:T(8,128)(2,1)}, u32[]{:S(2)}, u32[]{:S(2)}) collective-permute-start(bf16[72,1536]{1,0:T(8,128)(2,1)S(1)} %collective-permute-done), channel_id=1, source_target_pairs={{0,32},{4,12},{8,40},{12,20},{16,48},{20,28},{24,56},{28,4},{32,64... | collective-permute-start | bytes 663560 | tf_op jit(solution)/shard_map/ppermute | solution.py:344
  14.4 9.4 %copy-start.12 = (s32[1,8,4,2]{1,2,3,0:T(4,128)S(1)}, s32[1,8,4,2]{1,2,3,0:T(4,128)}, u32[]{:S(2)}) copy-start(s32[1,8,4,2]{1,2,3,0:T(4,128)} %constant.108) | copy-start | bytes 772
  14.4 9.4 %copy-start.13 = (s32[1,8,4,2]{1,2,3,0:T(4,128)S(1)}, s32[1,8,4,2]{1,2,3,0:T(4,128)}, u32[]{:S(2)}) copy-start(s32[1,8,4,2]{1,2,3,0:T(4,128)} %constant.109) | copy-start | bytes 772
  15.5 28.1 %collective-permute-start.3 = (bf16[4,72,1536]{2,1,0:T(8,128)(2,1)S(1)}, bf16[4,72,1536]{2,1,0:T(8,128)(2,1)S(1)}, u32[]{:S(2)}, u32[]{:S(2)}) collective-permute-start(bf16[4,72,1536]{2,1,0:T(8,128)(2,1)S(1)} %pad_maximum_fusion.refs_3_), channel_id=1, source_target_pairs={{0,24},{4,228},{8,0},{12,236},{16,8},{20,244},{24,16},{28,252},{32... | collective-permute-start | bytes 2654216 | tf_op jit(solution)/shard_map/ppermute | solution.py:344
  21.6 22.8 %collective-permute-start.8 = (bf16[4,72,1536]{2,1,0:T(8,128)(2,1)S(1)}, bf16[4,72,1536]{2,1,0:T(8,128)(2,1)S(1)}, u32[]{:S(2)}, u32[]{:S(2)}) collective-permute-start(bf16[4,72,1536]{2,1,0:T(8,128)(2,1)S(1)} %pad_maximum_fusion.refs_3_), channel_id=1, source_target_pairs={{0,8},{4,36},{8,16},{12,44},{16,24},{20,52},{24,0},{28,60},{32,40}... | collective-permute-start | bytes 2654216 | tf_op jit(solution)/shard_map/ppermute | solution.py:344
  23.4 7.4 %collective-permute-start.4 = (bf16[72,1536]{1,0:T(8,128)(2,1)S(1)}, bf16[72,1536]{1,0:T(8,128)(2,1)S(1)}, u32[]{:S(2)}, u32[]{:S(2)}) collective-permute-start(bf16[72,1536]{1,0:T(8,128)(2,1)S(1)} %collective-permute-done.1), channel_id=1, source_target_pairs={{0,224},{4,28},{8,232},{12,4},{16,240},{20,12},{24,248},{28,20},{3... | collective-permute-start | bytes 663560 | tf_op jit(solution)/shard_map/ppermute | solution.py:344
  31.6 7.3 %collective-permute-start.6 = (bf16[72,1536]{1,0:T(8,128)(2,1)S(1)}, bf16[72,1536]{1,0:T(8,128)(2,1)}, u32[]{:S(2)}, u32[]{:S(2)}) collective-permute-start(bf16[72,1536]{1,0:T(8,128)(2,1)S(1)} %collective-permute-done.4), channel_id=1, source_target_pairs={{0,224},{4,28},{8,232},{12,4},{16,240},{20,12},{24,248},{28,20},{3... | collective-permute-start | bytes 663560 | tf_op jit(solution)/shard_map/ppermute | solution.py:344
  32.6 10.9 %collective-permute-start.5 = (bf16[72,1536]{1,0:T(8,128)(2,1)}, bf16[72,1536]{1,0:T(8,128)(2,1)}, u32[]{:S(2)}, u32[]{:S(2)}) collective-permute-start(bf16[72,1536]{1,0:T(8,128)(2,1)} %collective-permute-done.2), channel_id=1, source_target_pairs={{0,32},{4,12},{8,40},{12,20},{16,48},{20,28},{24,56},{28,4},{32,64... | collective-permute-start | bytes 663560 | tf_op jit(solution)/shard_map/ppermute | solution.py:344
  38.9 5.6 %collective-permute-start.7 = (bf16[72,1536]{1,0:T(8,128)(2,1)}, bf16[72,1536]{1,0:T(8,128)(2,1)}, u32[]{:S(2)}, u32[]{:S(2)}) collective-permute-start(bf16[72,1536]{1,0:T(8,128)(2,1)} %collective-permute-done.6), channel_id=1, source_target_pairs={{0,224},{4,28},{8,232},{12,4},{16,240},{20,12},{24,248},{28,20},{3... | collective-permute-start | bytes 663560 | tf_op jit(solution)/shard_map/ppermute | solution.py:344
  42.2 2.3 %copy-start.11 = (bf16[72,1536]{1,0:T(8,128)(2,1)S(1)}, bf16[72,1536]{1,0:T(8,128)(2,1)}, u32[]{:S(2)}) copy-start(bf16[72,1536]{1,0:T(8,128)(2,1)} %copy-done.10) | copy-start | bytes 663556
  44.5 3.2 %copy-start.2 = (bf16[4,72,1536]{2,1,0:T(8,128)(2,1)}, bf16[4,72,1536]{2,1,0:T(8,128)(2,1)S(1)}, u32[]{:S(2)}) copy-start(bf16[4,72,1536]{2,1,0:T(8,128)(2,1)S(1)} %collective-permute-done.8.refs_4_) | copy-start | bytes 2654212
  47.7 12.4 %collective-permute-start.12 = (bf16[4,72,1536]{2,1,0:T(8,128)(2,1)}, bf16[4,72,1536]{2,1,0:T(8,128)(2,1)S(1)}, u32[]{:S(2)}, u32[]{:S(2)}) collective-permute-start(bf16[4,72,1536]{2,1,0:T(8,128)(2,1)} %get-tuple-element.49), channel_id=1, source_target_pairs={{0,24},{4,228},{8,0},{12,236},{16,8},{20,244},{24,16},{28,252},{32... | collective-permute-start | bytes 2654216 | tf_op jit(solution)/shard_map/ppermute | solution.py:344
  51.7 23.9 %collective-permute-start.19 = (bf16[128,4608]{1,0:T(8,128)(2,1)}, bf16[128,4608]{1,0:T(8,128)(2,1)S(1)}, u32[]{:S(2)}, u32[]{:S(2)}) collective-permute-start(bf16[128,4608]{1,0:T(8,128)(2,1)} %norm.1.refs_0_), channel_id=1, source_target_pairs={{0,3},{1,0},{2,1},{3,2},{4,7},{5,4},{6,5},{7,6},{8,11},{9,8},{10,9... | collective-permute-start | bytes 3538952 | tf_op jit(solution)/shard_map/ppermute | solution.py:34
  54.5 24.6 %collective-permute-start.21 = (bf16[128,4608]{1,0:T(8,128)(2,1)}, bf16[128,4608]{1,0:T(8,128)(2,1)S(1)}, u32[]{:S(2)}, u32[]{:S(2)}) collective-permute-start(bf16[128,4608]{1,0:T(8,128)(2,1)} %norm.1.refs_0_), channel_id=1, source_target_pairs={{0,1},{1,2},{2,3},{3,0},{4,5},{5,6},{6,7},{7,4},{8,9},{9,10},{10,1... | collective-permute-start | bytes 3538952 | tf_op jit(solution)/shard_map/ppermute | solution.py:34
  54.5 26.8 %collective-permute-start.25 = (bf16[4,72,1536]{2,1,0:T(8,128)(2,1)S(1)}, bf16[4,72,1536]{2,1,0:T(8,128)(2,1)S(1)}, u32[]{:S(2)}, u32[]{:S(2)}) collective-permute-start(bf16[4,72,1536]{2,1,0:T(8,128)(2,1)S(1)} %pad_maximum_fusion.refs_3_), channel_id=1, source_target_pairs={{0,4},{4,0},{8,12},{12,8},{16,20},{20,16},{24,28},{28,24},{32,36},... | collective-permute-start | bytes 2654216 | tf_op jit(solution)/shard_map/ppermute | solution.py:30
  59.2 20.1 %collective-permute-start.9 = (bf16[4,72,1536]{2,1,0:T(8,128)(2,1)}, bf16[4,72,1536]{2,1,0:T(8,128)(2,1)S(1)}, u32[]{:S(2)}, u32[]{:S(2)}) collective-permute-start(bf16[4,72,1536]{2,1,0:T(8,128)(2,1)} %get-tuple-element.48), channel_id=1, source_target_pairs={{0,8},{4,36},{8,16},{12,44},{16,24},{20,52},{24,0},{28,60},{32,40}... | collective-permute-start | bytes 2654216 | tf_op jit(solution)/shard_map/ppermute | solution.py:344
  60.2 21.1 %copy-start.4 = (bf16[4,72,1536]{2,1,0:T(8,128)(2,1)S(1)}, bf16[4,72,1536]{2,1,0:T(8,128)(2,1)}, u32[]{:S(2)}) copy-start(bf16[4,72,1536]{2,1,0:T(8,128)(2,1)} %get-tuple-element.47.refs_11_) | copy-start | bytes 2654212
  60.2 33.3 %copy-start.3 = (bf16[4,72,1536]{2,1,0:T(8,128)(2,1)S(1)}, bf16[4,72,1536]{2,1,0:T(8,128)(2,1)}, u32[]{:S(2)}) copy-start(bf16[4,72,1536]{2,1,0:T(8,128)(2,1)} %copy-done.2) | copy-start | bytes 2654212
  60.2 36.7 %collective-permute-start.13 = (bf16[4,72,1536]{2,1,0:T(8,128)(2,1)S(1)}, bf16[4,72,1536]{2,1,0:T(8,128)(2,1)S(1)}, u32[]{:S(2)}, u32[]{:S(2)}) collective-permute-start(bf16[4,72,1536]{2,1,0:T(8,128)(2,1)S(1)} %broadcast_select_fusion), channel_id=1, source_target_pairs={{0,24},{4,228},{8,0},{12,236},{16,8},{20,244},{24,16},{28,252},{32... | collective-permute-start | bytes 2654216 | tf_op jit(solution)/shard_map/ppermute | solution.py:344
  75.7 11.6 %collective-permute-start.20 = (bf16[64,4608]{1,0:T(8,128)(2,1)S(1)}, bf16[64,4608]{1,0:T(8,128)(2,1)S(1)}, u32[]{:S(2)}, u32[]{:S(2)}) collective-permute-start(bf16[64,4608]{1,0:T(8,128)(2,1)S(1)} %slice.48), channel_id=1, source_target_pairs={{0,3},{1,0},{2,1},{3,2},{4,7},{5,4},{6,5},{7,6},{8,11},{9,8},{10,9... | collective-permute-start | bytes 1769480 | tf_op jit(solution)/shard_map/ppermute | solution.py:34
  79.1 38.4 %copy-start = (bf16[128,4608]{1,0:T(8,128)(2,1)S(1)}, bf16[128,4608]{1,0:T(8,128)(2,1)}, u32[]{:S(2)}) copy-start(bf16[128,4608]{1,0:T(8,128)(2,1)} %norm.1.refs_0_) | copy-start | bytes 3538948
  79.2 14.3 %collective-permute-start.22 = (bf16[64,4608]{1,0:T(8,128)(2,1)S(1)}, bf16[64,4608]{1,0:T(8,128)(2,1)S(1)}, u32[]{:S(2)}, u32[]{:S(2)}) collective-permute-start(bf16[64,4608]{1,0:T(8,128)(2,1)S(1)} %slice.49), channel_id=1, source_target_pairs={{0,1},{1,2},{2,3},{3,0},{4,5},{5,6},{6,7},{7,4},{8,9},{9,10},{10,1... | collective-permute-start | bytes 1769480 | tf_op jit(solution)/shard_map/ppermute | solution.py:34
  79.3 17.8 %collective-permute-start.10 = (bf16[4,72,1536]{2,1,0:T(8,128)(2,1)S(1)}, bf16[4,72,1536]{2,1,0:T(8,128)(2,1)S(1)}, u32[]{:S(2)}, u32[]{:S(2)}) collective-permute-start(bf16[4,72,1536]{2,1,0:T(8,128)(2,1)S(1)} %collective-permute-done.9.refs_6_), channel_id=1, source_target_pairs={{0,8},{4,36},{8,16},{12,44},{16,24},{20,52},{24,0},{28,60},{32,40}... | collective-permute-start | bytes 2654216 | tf_op jit(solution)/shard_map/ppermute | solution.py:344
  81.3 18.8 %collective-permute-start.28 = (bf16[4,72,1536]{2,1,0:T(8,128)(2,1)S(1)}, bf16[4,72,1536]{2,1,0:T(8,128)(2,1)S(1)}, u32[]{:S(2)}, u32[]{:S(2)}) collective-permute-start(bf16[4,72,1536]{2,1,0:T(8,128)(2,1)S(1)} %copy-done.4), channel_id=1, source_target_pairs={{0,4},{8,12},{16,20},{24,28},{32,36},{40,44},{48,52},{56,60},{64,6... | collective-permute-start | bytes 2654216 | tf_op jit(solution)/shard_map/ppermute | solution.py:349
  87.3 12.8 %collective-permute-start.27 = (bf16[4,72,1536]{2,1,0:T(8,128)(2,1)S(1)}, bf16[4,72,1536]{2,1,0:T(8,128)(2,1)S(1)}, u32[]{:S(2)}, u32[]{:S(2)}) collective-permute-start(bf16[4,72,1536]{2,1,0:T(8,128)(2,1)S(1)} %collective-permute-done.3.refs_5_), channel_id=1, source_target_pairs={{0,4},{4,0},{8,12},{12,8},{16,20},{20,16},{24,28},{28,24},{32,36},... | collective-permute-start | bytes 2654216 | tf_op jit(solution)/shard_map/ppermute | solution.py:30
  93.5 7.2 %collective-permute-start.26 = (bf16[4,72,1536]{2,1,0:T(8,128)(2,1)S(1)}, bf16[4,72,1536]{2,1,0:T(8,128)(2,1)S(1)}, u32[]{:S(2)}, u32[]{:S(2)}) collective-permute-start(bf16[4,72,1536]{2,1,0:T(8,128)(2,1)S(1)} %copy-done.3), channel_id=1, source_target_pairs={{0,4},{4,0},{8,12},{12,8},{16,20},{20,16},{24,28},{28,24},{32,36},... | collective-permute-start | bytes 2654216 | tf_op jit(solution)/shard_map/ppermute | solution.py:30
  96.9 9.1 %collective-permute-start.23 = (bf16[4,72,1536]{2,1,0:T(8,128)(2,1)S(1)}, bf16[4,72,1536]{2,1,0:T(8,128)(2,1)S(1)}, u32[]{:S(2)}, u32[]{:S(2)}) collective-permute-start(bf16[4,72,1536]{2,1,0:T(8,128)(2,1)S(1)} %collective-permute-done.9.refs_6_), channel_id=1, source_target_pairs={{0,4},{4,0},{8,12},{12,8},{16,20},{20,16},{24,28},{28,24},{32,36},... | collective-permute-start | bytes 2654216 | tf_op jit(solution)/shard_map/ppermute | solution.py:30
  97.1 22.7 %collective-permute-start.24 = (bf16[4,72,1536]{2,1,0:T(8,128)(2,1)S(1)}, bf16[4,72,1536]{2,1,0:T(8,128)(2,1)S(1)}, u32[]{:S(2)}, u32[]{:S(2)}) collective-permute-start(bf16[4,72,1536]{2,1,0:T(8,128)(2,1)S(1)} %collective-permute-done.12.refs_7_), channel_id=1, source_target_pairs={{0,4},{4,0},{8,12},{12,8},{16,20},{20,16},{24,28},{28,24},{32,36},... | collective-permute-start | bytes 2654216 | tf_op jit(solution)/shard_map/ppermute | solution.py:30
  100.1 21.0 %collective-permute-start.18 = (bf16[4,72,1536]{2,1,0:T(8,128)(2,1)S(1)}, bf16[4,72,1536]{2,1,0:T(8,128)(2,1)S(1)}, u32[]{:S(2)}, u32[]{:S(2)}) collective-permute-start(bf16[4,72,1536]{2,1,0:T(8,128)(2,1)S(1)} %collective-permute-done.13.refs_3_), channel_id=1, source_target_pairs={{0,4},{4,0},{8,12},{12,8},{16,20},{20,16},{24,28},{28,24},{32,36},... | collective-permute-start | bytes 2654216 | tf_op jit(solution)/shard_map/ppermute | solution.py:30
  100.2 20.9 %collective-permute-start.17 = (bf16[4,72,1536]{2,1,0:T(8,128)(2,1)S(1)}, bf16[4,72,1536]{2,1,0:T(8,128)(2,1)S(1)}, u32[]{:S(2)}, u32[]{:S(2)}) collective-permute-start(bf16[4,72,1536]{2,1,0:T(8,128)(2,1)S(1)} %collective-permute-done.10.refs_2_), channel_id=1, source_target_pairs={{0,4},{4,0},{8,12},{12,8},{16,20},{20,16},{24,28},{28,24},{32,36},... | collective-permute-start | bytes 2654216 | tf_op jit(solution)/shard_map/ppermute | solution.py:30
  100.7 10.6 %collective-permute-start.14 = (bf16[2,72,1536]{2,1,0:T(8,128)(2,1)S(1)}, bf16[2,72,1536]{2,1,0:T(8,128)(2,1)S(1)}, u32[]{:S(2)}, u32[]{:S(2)}) collective-permute-start(bf16[2,72,1536]{2,1,0:T(8,128)(2,1)S(1)} %slice.47), channel_id=1, source_target_pairs={{4,228},{12,236},{20,244},{28,252},{36,4},{44,12},{52,20},{60,28},... | collective-permute-start | bytes 1327112 | tf_op jit(solution)/shard_map/ppermute | solution.py:344
  106.0 10.3 %collective-permute-start.11 = (bf16[2,72,1536]{2,1,0:T(8,128)(2,1)S(1)}, bf16[2,72,1536]{2,1,0:T(8,128)(2,1)S(1)}, u32[]{:S(2)}, u32[]{:S(2)}) collective-permute-start(bf16[2,72,1536]{2,1,0:T(8,128)(2,1)S(1)} %slice.46), channel_id=1, source_target_pairs={{4,36},{12,44},{20,52},{28,60},{36,68},{44,76},{52,84},{60,92},{68... | collective-permute-start | bytes 1327112 | tf_op jit(solution)/shard_map/ppermute | solution.py:344
  111.2 10.7 %collective-permute-start.16 = (bf16[2,72,1536]{2,1,0:T(8,128)(2,1)S(1)}, bf16[2,72,1536]{2,1,0:T(8,128)(2,1)S(1)}, u32[]{:S(2)}, u32[]{:S(2)}) collective-permute-start(bf16[2,72,1536]{2,1,0:T(8,128)(2,1)S(1)} %collective-permute-done.14.down_own), channel_id=1, source_target_pairs={{4,0},{12,8},{20,16},{28,24},{36,32},{44,40},{52,48},{60,56},{68,6... | collective-permute-start | bytes 1327112 | tf_op jit(solution)/shard_map/ppermute | solution.py:349
  116.3 5.7 %collective-permute-start.15 = (bf16[2,72,1536]{2,1,0:T(8,128)(2,1)S(1)}, bf16[2,72,1536]{2,1,0:T(8,128)(2,1)S(1)}, u32[]{:S(2)}, u32[]{:S(2)}) collective-permute-start(bf16[2,72,1536]{2,1,0:T(8,128)(2,1)S(1)} %collective-permute-done.11.up_own), channel_id=1, source_target_pairs={{4,0},{12,8},{20,16},{28,24},{36,32},{44,40},{52,48},{60,56},{68,6... | collective-permute-start | bytes 1327112 | tf_op jit(solution)/shard_map/ppermute | solution.py:349
  129.4 15.4 %collective-permute-start.33 = (bf16[64,4608]{1,0:T(8,128)(2,1)S(1)}, bf16[64,4608]{1,0:T(8,128)(2,1)S(1)}, u32[]{:S(2)}, u32[]{:S(2)}) collective-permute-start(bf16[64,4608]{1,0:T(8,128)(2,1)S(1)} %get-tuple-element.46), channel_id=1, source_target_pairs={{0,3},{1,0},{2,1},{3,2},{4,7},{5,4},{6,5},{7,6},{8,11},{9,8},{10,9... | collective-permute-start | bytes 1769480 | tf_op jit(solution)/shard_map/ppermute | solution.py:34
  132.3 16.6 %collective-permute-start.31 = (bf16[64,4608]{1,0:T(8,128)(2,1)S(1)}, bf16[64,4608]{1,0:T(8,128)(2,1)S(1)}, u32[]{:S(2)}, u32[]{:S(2)}) collective-permute-start(bf16[64,4608]{1,0:T(8,128)(2,1)S(1)} %get-tuple-element.44), channel_id=1, source_target_pairs={{0,1},{1,2},{2,3},{3,0},{4,5},{5,6},{6,7},{7,4},{8,9},{9,10},{10,1... | collective-permute-start | bytes 1769480 | tf_op jit(solution)/shard_map/ppermute | solution.py:34
  132.3 1.0 copy-start.5
  133.3 0.9 copy-start.7
  142.0 19.6 %collective-permute-start.29 = (bf16[64,4608]{1,0:T(8,128)(2,1)S(1)}, bf16[64,4608]{1,0:T(8,128)(2,1)S(1)}, u32[]{:S(2)}, u32[]{:S(2)}) collective-permute-start(bf16[64,4608]{1,0:T(8,128)(2,1)S(1)} %get-tuple-element.41), channel_id=1, source_target_pairs={{0,1},{1,2},{2,3},{3,0},{4,5},{5,6},{6,7},{7,4},{8,9},{9,10},{10,1... | collective-permute-start | bytes 1769480 | tf_op jit(solution)/shard_map/ppermute | solution.py:34
  142.0 19.5 %collective-permute-start.30 = (bf16[64,4608]{1,0:T(8,128)(2,1)S(1)}, bf16[64,4608]{1,0:T(8,128)(2,1)S(1)}, u32[]{:S(2)}, u32[]{:S(2)}) collective-permute-start(bf16[64,4608]{1,0:T(8,128)(2,1)S(1)} %get-tuple-element.42), channel_id=1, source_target_pairs={{0,3},{1,0},{2,1},{3,2},{4,7},{5,4},{6,5},{7,6},{8,11},{9,8},{10,9... | collective-permute-start | bytes 1769480 | tf_op jit(solution)/shard_map/ppermute | solution.py:34
  144.9 4.5 %copy-start.6 = (bf16[512,256]{1,0:T(8,128)(2,1)S(1)}, bf16[512,256]{1,0:T(8,128)(2,1)}, u32[]{:S(2)}) copy-start(bf16[512,256]{1,0:T(8,128)(2,1)} %get-tuple-element.38.k_ref) | copy-start | bytes 786436
  145.0 4.5 %copy-start.8 = (bf16[512,256]{1,0:T(8,128)(2,1)S(1)}, bf16[512,256]{1,0:T(8,128)(2,1)}, u32[]{:S(2)}) copy-start(bf16[512,256]{1,0:T(8,128)(2,1)} %get-tuple-element.39.v_ref) | copy-start | bytes 786436
  145.0 24.0 %collective-permute-start.34 = (bf16[64,4608]{1,0:T(8,128)(2,1)S(1)}, bf16[64,4608]{1,0:T(8,128)(2,1)S(1)}, u32[]{:S(2)}, u32[]{:S(2)}) collective-permute-start(bf16[64,4608]{1,0:T(8,128)(2,1)S(1)} %add_convert_fusion), channel_id=1, source_target_pairs={{0,3},{1,0},{2,1},{3,2},{4,7},{5,4},{6,5},{7,6},{8,11},{9,8},{10,9... | collective-permute-start | bytes 1769480 | tf_op jit(solution)/shard_map/ppermute | solution.py:34
  149.0 23.0 %copy-start.1 = (bf16[1,128,4608]{2,1,0:T(8,128)(2,1)S(1)}, bf16[1,128,4608]{2,1,0:T(8,128)(2,1)}, u32[]{:S(2)}) copy-start(bf16[1,128,4608]{2,1,0:T(8,128)(2,1)} %param.9) | copy-start | bytes 3538948
  149.0 22.9 %copy-start.9 = (f32[4608]{0:T(1024)S(1)}, f32[4608]{0:T(1024)}, u32[]{:S(2)}) copy-start(f32[4608]{0:T(1024)} %gain_ref.3) | copy-start | bytes 55300
  149.1 22.9 %collective-permute-start.32 = (bf16[64,4608]{1,0:T(8,128)(2,1)S(1)}, bf16[64,4608]{1,0:T(8,128)(2,1)S(1)}, u32[]{:S(2)}, u32[]{:S(2)}) collective-permute-start(bf16[64,4608]{1,0:T(8,128)(2,1)S(1)} %add_convert_fusion.1), channel_id=1, source_target_pairs={{0,1},{1,2},{2,3},{3,0},{4,5},{5,6},{6,7},{7,4},{8,9},{9,10},{10,1... | collective-permute-start | bytes 1769480 | tf_op jit(solution)/shard_map/ppermute | solution.py:34
  (1 other events, 0.7 us)

commit v3 on v2

--- a/solution.py
+++ b/solution.py
@@ -79,15 +79,6 @@
         store(h, jnp.dot(weights, v_ref[:, kv], preferred_element_type=F32).astype(BF16))
 
 
-def spread(att, wo, outs, width, chunk=1152):
-    for at in range(0, width, chunk):
-        partial = lax.dot_general(
-            att[...], wo[at : at + chunk, :], (((1,), (1,)), ((), ())), preferred_element_type=F32
-        )
-        for ref, first in outs:
-            ref[:, at : at + chunk] = partial[first : first + ref.shape[0]].astype(ref.dtype)
-
-
 def start(pairs, sem):
     for src, dst in pairs:
         half = src.shape[-1] // 2
@@ -184,18 +175,9 @@
         att[mine, head] = jnp.dot(weights, v_ref[:, kv], preferred_element_type=F32).astype(BF16)
 
 
-def spread(att, wbuf, outs, chunk=1152):
-    for at in range(0, wbuf.shape[0], chunk):
-        partial = lax.dot_general(
-            att[...], wbuf[at : at + chunk, 1024:1536], (((1,), (1,)), ((), ())), preferred_element_type=F32
-        )
-        for ref, first in outs:
-            ref[:, at : at + chunk] = partial[first : first + ref.shape[0]].astype(ref.dtype)
-
-
 def project_kernel(
     scal, table, cos_ref, sin_ref, up_own, down_own, up_other, down_other, xbuf, old,
-    k_ref, v_ref, far0, far1, wbuf, q, att, sem,
+    k_out, v_out, far0, far1, wbuf, q, att, k_ref, v_ref, far, sem, osem,
 ):
     c, length = scal[2], scal[4]
 
@@ -212,13 +194,25 @@
     for h in range(2):
         head = slice(h * 128, h * 128 + 128)
         k_ref[:, head] = jnp.where(live, turned(raw[:, head], cos_ref, sin_ref, 0, 512), 0.0).astype(BF16)
+    start([(k_ref, k_out)], osem.at[0])
     raw = jnp.dot(xbuf[...], wbuf[:, 768:1024], preferred_element_type=F32)
     for h in range(2):
         head = slice(h * 128, h * 128 + 128)
         v_ref[:, head] = jnp.where(live, raw[:, head], 0.0).astype(BF16)
+    start([(v_ref, v_out)], osem.at[1])
     queries(scal, 2, xbuf, wbuf, cos_ref, sin_ref, q, 0)
     attended(scal, 2, q, 0, k_ref, v_ref, att)
-    spread(att, wbuf, ((far0, 0), (far1, 64)))
+    chunk = 1152
+    for at in range(0, wbuf.shape[0], chunk):
+        cols = slice(at, at + chunk)
+        far[:, cols] = lax.dot_general(
+            att[...], wbuf[cols, 1024:1536], (((1,), (1,)), ((), ())), preferred_element_type=F32
+        ).astype(BF16)
+        for i, ref in enumerate((far0, far1)):
+            cut = pl.ds(at, chunk)
+            pltpu.make_async_copy(far.at[pl.ds(i * 64, 64), cut], ref.at[:, cut], osem.at[2 + i]).start()
+    for i, (src, dst) in enumerate(((k_ref, k_out), (v_ref, v_out), (far.at[:64], far0), (far.at[64:], far1))):
+        pltpu.make_async_copy(src, dst, osem.at[i]).wait()
 
 
 def project(scal, table, cosine, sine, arrays, xbuf, wbuf):
@@ -228,12 +222,16 @@
     return pl.pallas_call(
         project_kernel,
         in_specs=[SMEM] * 2 + [VMEM] * 2 + [ANY] * len(arrays) + [VMEM] * 2,
-        out_specs=[VMEM] * 5,
+        out_specs=[ANY] * 4 + [VMEM],
         out_shape=[jax.ShapeDtypeStruct(shape, BF16) for shape in outs] + [pltpu.VMEM(wbuf.shape, BF16)],
         scratch_shapes=[
             pltpu.VMEM((128, 512), BF16),
             pltpu.VMEM((128, 512), BF16),
+            pltpu.VMEM((512, 256), BF16),
+            pltpu.VMEM((512, 256), BF16),
+            pltpu.VMEM((128, width), BF16),
             pltpu.SemaphoreType.DMA,
+            pltpu.SemaphoreType.DMA((4,)),
         ],
         input_output_aliases={n + 1: 4},
         compiler_params=pltpu.CompilerParams(vmem_limit_bytes=SMALL_LIMIT),

time: 175 us -> 176 us (level)
  no operation moved by 1% of the time
where the time goes in v3:
time: 176 us
  waiting for transfers between devices  68 us (39%)
  starting transfers between devices  63.4 us (36%)
  Pallas kernels  30.5 us (17%)
  other arithmetic  8.84 us (5%)
  local copies, waits for them, and re-layouts  3.04 us (2%)
  between operations  1.86 us (1%)
    ppermute x10, waiting for transfers between devices, column(): return lax.ppermute(array, 'mp', [(y, (y + dy) % NY) for y in range(NY)])  37.3 us
    ppermute x15, waiting for transfers between devices, torus(): return lax.ppermute(array, 'dp', pairs)  30.7 us
    ppermute x15, starting transfers between devices, torus(): return lax.ppermute(array, 'dp', pairs)  27.5 us
    ppermute x7, starting transfers between devices, plane(): return lax.ppermute(array, 'dp', pairs)  17.9 us
    ppermute x10, starting transfers between devices, column(): return lax.ppermute(array, 'mp', [(y, (y + dy) % NY) for y in range(NY)])  14.1 us
    pallas_call x2, Pallas kernels, attend(): pl.pallas_call(functools.partial(attend_kernel, blocks, outs), in_specs=[...  12.8 us
    pallas_call x1, Pallas kernels, project(): pl.pallas_call(project_kernel, in_specs=[SMEM] * 2 + [VMEM] * 2 + [ANY] *...  8.21 us
    pallas_call x3, Pallas kernels, fill(): pl.pallas_call(functools.partial(fill_kernel, offsets, groups, len(held))...  4.29 us
  transfers between devices with their start and end apart: 35, of which 15 were waited for; matrix products, arithmetic and copies ran while one was open for 2% of the time, Pallas kernels for 11%

profile of v3, /device:TPU:1, one launch (start us, length us, event | category | flops | bytes accessed | tf_op | source)
XLA Modules:
  0.0 175.6 jit_solution(2023847106249805235)
XLA Ops:
  0.6 1.0 fusion.19
  1.6 2.1 %collective-permute-start = (bf16[72,1536]{1,0:T(8,128)(2,1)S(1)}, bf16[72,1536]{1,0:T(8,128)(2,1)S(1)}, u32[]{:S(2)}, u32[]{:S(2)}) collective-permute-start(bf16[72,1536]{1,0:T(8,128)(2,1)S(1)} %get-tuple-element.51), channel_id=1, source_target_pairs={{0,32},{4,12},{8,40},{12,20},{16,48},{20,28},{24,56},{28,4},{32,64... | collective-permute-start | bytes 663560 | tf_op jit(solution)/shard_map/ppermute | solution.py:342
  3.7 1.4 collective-permute-start.1
  5.1 3.2 %collective-permute-done = bf16[72,1536]{1,0:T(8,128)(2,1)S(1)} collective-permute-done((bf16[72,1536]{1,0:T(8,128)(2,1)S(1)}, bf16[72,1536]{1,0:T(8,128)(2,1)S(1)}, u32[]{:S(2)}, u32[]{:S(2)}) %collective-permute-start) | collective-permute-done | bytes 221216 | tf_op jit(solution)/shard_map/ppermute | solution.py:342
  8.8 5.6 %collective-permute-done.2 = bf16[72,1536]{1,0:T(8,128)(2,1)} collective-permute-done((bf16[72,1536]{1,0:T(8,128)(2,1)S(1)}, bf16[72,1536]{1,0:T(8,128)(2,1)}, u32[]{:S(2)}, u32[]{:S(2)}) %collective-permute-start.2) | collective-permute-done | bytes 221216 | tf_op jit(solution)/shard_map/ppermute | solution.py:342
  14.4 1.1 pad_maximum_fusion.refs_3_
  15.5 6.1 %collective-permute-start.3 = (bf16[4,72,1536]{2,1,0:T(8,128)(2,1)S(1)}, bf16[4,72,1536]{2,1,0:T(8,128)(2,1)S(1)}, u32[]{:S(2)}, u32[]{:S(2)}) collective-permute-start(bf16[4,72,1536]{2,1,0:T(8,128)(2,1)S(1)} %pad_maximum_fusion.refs_3_), channel_id=1, source_target_pairs={{0,24},{4,228},{8,0},{12,236},{16,8},{20,244},{24,16},{28,252},{32... | collective-permute-start | bytes 2654216 | tf_op jit(solution)/shard_map/ppermute | solution.py:342
  21.7 1.8 %fusion = (f32[512,64]{1,0:T(8,128)S(1)}, f32[512,64]{1,0:T(8,128)}, f32[512,64]{1,0:T(8,128)}) fusion(f32[64]{0:T(128)S(1)} %multiply_power_fusion, f32[512]{0:T(512)S(1)} %iota_convert_fusion), kind=kLoop, calls=%fused_computation.12 | loop fusion | flops 65536 | bytes 395520 | tf_op jit(solution)/shard_map/neg | solution.py:332
  23.8 7.1 %collective-permute-done.4 = bf16[72,1536]{1,0:T(8,128)(2,1)S(1)} collective-permute-done((bf16[72,1536]{1,0:T(8,128)(2,1)S(1)}, bf16[72,1536]{1,0:T(8,128)(2,1)S(1)}, u32[]{:S(2)}, u32[]{:S(2)}) %collective-permute-start.4) | collective-permute-done | bytes 221216 | tf_op jit(solution)/shard_map/ppermute | solution.py:342
  31.6 1.0 collective-permute-start.6
  33.1 5.7 %collective-permute-done.6 = bf16[72,1536]{1,0:T(8,128)(2,1)} collective-permute-done((bf16[72,1536]{1,0:T(8,128)(2,1)S(1)}, bf16[72,1536]{1,0:T(8,128)(2,1)}, u32[]{:S(2)}, u32[]{:S(2)}) %collective-permute-start.6) | collective-permute-done | bytes 221216 | tf_op jit(solution)/shard_map/ppermute | solution.py:342
  38.9 2.4 %collective-permute-start.7 = (bf16[72,1536]{1,0:T(8,128)(2,1)}, bf16[72,1536]{1,0:T(8,128)(2,1)}, u32[]{:S(2)}, u32[]{:S(2)}) collective-permute-start(bf16[72,1536]{1,0:T(8,128)(2,1)} %collective-permute-done.6), channel_id=1, source_target_pairs={{0,224},{4,28},{8,232},{12,4},{16,240},{20,12},{24,248},{28,20},{3... | collective-permute-start | bytes 663560 | tf_op jit(solution)/shard_map/ppermute | solution.py:342
  42.2 1.4 pad_maximum_fusion.2
  44.5 3.2 %pad_maximum_fusion.1 = (bf16[4,72,1536]{2,1,0:T(8,128)(2,1)}, bf16[4,72,1536]{2,1,0:T(8,128)(2,1)}, bf16[4,72,1536]{2,1,0:T(8,128)(2,1)}) fusion(bf16[1,72,1536]{2,1,0:T(8,128)(2,1)} %bitcast.19, bf16[1,72,1536]{2,1,0:T(8,128)(2,1)} %bitcast.18, bf16[1,72,1536]{2,1,0:T(8,128)(2,1)} %bitcast.17, bf16[1,72,1536]{2,1,0:T(8,128)(2,1)S(1)} %bitcast.53, ...), kind=kLoop, calls=%fused_computation.3 | loop fusion | flops 2211840 | bytes 5308417 | tf_op jit(solution)/shard_map/stack | solution.py:395
  47.7 1.5 collective-permute-start.12
  49.2 2.5 %norm.1.refs_0_ = bf16[128,4608]{1,0:T(8,128)(2,1)} custom-call(bf16[128,4608]{1,0:T(8,128)(2,1)} %bitcast.46, f32[4608]{0:T(1024)} %gain_ref.2), custom_call_target="tpu_custom_call" | custom-call | flops 2000000 | bytes 2400000 | tf_op jit(solution)/shard_map/norm/pallas_call | solution.py:46
  51.7 2.7 %collective-permute-start.19 = (bf16[128,4608]{1,0:T(8,128)(2,1)}, bf16[128,4608]{1,0:T(8,128)(2,1)S(1)}, u32[]{:S(2)}, u32[]{:S(2)}) collective-permute-start(bf16[128,4608]{1,0:T(8,128)(2,1)} %norm.1.refs_0_), channel_id=1, source_target_pairs={{0,3},{1,0},{2,1},{3,2},{4,7},{5,4},{6,5},{7,6},{8,11},{9,8},{10,9... | collective-permute-start | bytes 3538952 | tf_op jit(solution)/shard_map/ppermute | solution.py:34
  54.5 4.7 %collective-permute-start.25 = (bf16[4,72,1536]{2,1,0:T(8,128)(2,1)S(1)}, bf16[4,72,1536]{2,1,0:T(8,128)(2,1)S(1)}, u32[]{:S(2)}, u32[]{:S(2)}) collective-permute-start(bf16[4,72,1536]{2,1,0:T(8,128)(2,1)S(1)} %pad_maximum_fusion.refs_3_), channel_id=1, source_target_pairs={{0,4},{4,0},{8,12},{12,8},{16,20},{20,16},{24,28},{28,24},{32,36},... | collective-permute-start | bytes 2654216 | tf_op jit(solution)/shard_map/ppermute | solution.py:30
  60.2 2.6 %collective-permute-start.13 = (bf16[4,72,1536]{2,1,0:T(8,128)(2,1)S(1)}, bf16[4,72,1536]{2,1,0:T(8,128)(2,1)S(1)}, u32[]{:S(2)}, u32[]{:S(2)}) collective-permute-start(bf16[4,72,1536]{2,1,0:T(8,128)(2,1)S(1)} %broadcast_select_fusion), channel_id=1, source_target_pairs={{0,24},{4,228},{8,0},{12,236},{16,8},{20,244},{24,16},{28,252},{32... | collective-permute-start | bytes 2654216 | tf_op jit(solution)/shard_map/ppermute | solution.py:342
  62.8 12.8 %collective-permute-done.19.refs_1_ = bf16[128,4608]{1,0:T(8,128)(2,1)S(1)} collective-permute-done((bf16[128,4608]{1,0:T(8,128)(2,1)}, bf16[128,4608]{1,0:T(8,128)(2,1)S(1)}, u32[]{:S(2)}, u32[]{:S(2)}) %collective-permute-start.19) | collective-permute-done | bytes 1179680 | tf_op jit(solution)/shard_map/ppermute | solution.py:34
  75.7 3.4 %collective-permute-start.20 = (bf16[64,4608]{1,0:T(8,128)(2,1)S(1)}, bf16[64,4608]{1,0:T(8,128)(2,1)S(1)}, u32[]{:S(2)}, u32[]{:S(2)}) collective-permute-start(bf16[64,4608]{1,0:T(8,128)(2,1)S(1)} %slice.48), channel_id=1, source_target_pairs={{0,3},{1,0},{2,1},{3,2},{4,7},{5,4},{6,5},{7,6},{8,11},{9,8},{10,9... | collective-permute-start | bytes 1769480 | tf_op jit(solution)/shard_map/ppermute | solution.py:34
  79.3 2.0 %collective-permute-start.10 = (bf16[4,72,1536]{2,1,0:T(8,128)(2,1)S(1)}, bf16[4,72,1536]{2,1,0:T(8,128)(2,1)S(1)}, u32[]{:S(2)}, u32[]{:S(2)}) collective-permute-start(bf16[4,72,1536]{2,1,0:T(8,128)(2,1)S(1)} %collective-permute-done.9.refs_6_), channel_id=1, source_target_pairs={{0,8},{4,36},{8,16},{12,44},{16,24},{20,52},{24,0},{28,60},{32,40}... | collective-permute-start | bytes 2654216 | tf_op jit(solution)/shard_map/ppermute | solution.py:342
  81.3 1.3 collective-permute-start.28
  82.6 4.8 %collective-permute-done.20.refs_0_ = bf16[64,4608]{1,0:T(8,128)(2,1)S(1)} collective-permute-done((bf16[64,4608]{1,0:T(8,128)(2,1)S(1)}, bf16[64,4608]{1,0:T(8,128)(2,1)S(1)}, u32[]{:S(2)}, u32[]{:S(2)}) %collective-permute-start.20) | collective-permute-done | bytes 589856 | tf_op jit(solution)/shard_map/ppermute | solution.py:34
  87.3 6.1 %collective-permute-start.27 = (bf16[4,72,1536]{2,1,0:T(8,128)(2,1)S(1)}, bf16[4,72,1536]{2,1,0:T(8,128)(2,1)S(1)}, u32[]{:S(2)}, u32[]{:S(2)}) collective-permute-start(bf16[4,72,1536]{2,1,0:T(8,128)(2,1)S(1)} %collective-permute-done.3.refs_5_), channel_id=1, source_target_pairs={{0,4},{4,0},{8,12},{12,8},{16,20},{20,16},{24,28},{28,24},{32,36},... | collective-permute-start | bytes 2654216 | tf_op jit(solution)/shard_map/ppermute | solution.py:30
  93.5 3.4 %collective-permute-start.26 = (bf16[4,72,1536]{2,1,0:T(8,128)(2,1)S(1)}, bf16[4,72,1536]{2,1,0:T(8,128)(2,1)S(1)}, u32[]{:S(2)}, u32[]{:S(2)}) collective-permute-start(bf16[4,72,1536]{2,1,0:T(8,128)(2,1)S(1)} %copy-done.3), channel_id=1, source_target_pairs={{0,4},{4,0},{8,12},{12,8},{16,20},{20,16},{24,28},{28,24},{32,36},... | collective-permute-start | bytes 2654216 | tf_op jit(solution)/shard_map/ppermute | solution.py:30
  97.1 3.0 %collective-permute-start.24 = (bf16[4,72,1536]{2,1,0:T(8,128)(2,1)S(1)}, bf16[4,72,1536]{2,1,0:T(8,128)(2,1)S(1)}, u32[]{:S(2)}, u32[]{:S(2)}) collective-permute-start(bf16[4,72,1536]{2,1,0:T(8,128)(2,1)S(1)} %collective-permute-done.12.refs_7_), channel_id=1, source_target_pairs={{0,4},{4,0},{8,12},{12,8},{16,20},{20,16},{24,28},{28,24},{32,36},... | collective-permute-start | bytes 2654216 | tf_op jit(solution)/shard_map/ppermute | solution.py:30
  100.7 5.3 %collective-permute-start.14 = (bf16[2,72,1536]{2,1,0:T(8,128)(2,1)S(1)}, bf16[2,72,1536]{2,1,0:T(8,128)(2,1)S(1)}, u32[]{:S(2)}, u32[]{:S(2)}) collective-permute-start(bf16[2,72,1536]{2,1,0:T(8,128)(2,1)S(1)} %slice.47), channel_id=1, source_target_pairs={{4,228},{12,236},{20,244},{28,252},{36,4},{44,12},{52,20},{60,28},... | collective-permute-start | bytes 1327112 | tf_op jit(solution)/shard_map/ppermute | solution.py:342
  106.0 1.9 %collective-permute-start.11 = (bf16[2,72,1536]{2,1,0:T(8,128)(2,1)S(1)}, bf16[2,72,1536]{2,1,0:T(8,128)(2,1)S(1)}, u32[]{:S(2)}, u32[]{:S(2)}) collective-permute-start(bf16[2,72,1536]{2,1,0:T(8,128)(2,1)S(1)} %slice.46), channel_id=1, source_target_pairs={{4,36},{12,44},{20,52},{28,60},{36,68},{44,76},{52,84},{60,92},{68... | collective-permute-start | bytes 1327112 | tf_op jit(solution)/shard_map/ppermute | solution.py:342
  107.9 3.3 %collective-permute-done.14.down_own = bf16[2,72,1536]{2,1,0:T(8,128)(2,1)S(1)} collective-permute-done((bf16[2,72,1536]{2,1,0:T(8,128)(2,1)S(1)}, bf16[2,72,1536]{2,1,0:T(8,128)(2,1)S(1)}, u32[]{:S(2)}, u32[]{:S(2)}) %collective-permute-start.14) | collective-permute-done | bytes 442400 | tf_op jit(solution)/shard_map/ppermute | solution.py:342
  111.2 1.3 collective-permute-start.16
  112.5 3.7 %collective-permute-done.11.up_own = bf16[2,72,1536]{2,1,0:T(8,128)(2,1)S(1)} collective-permute-done((bf16[2,72,1536]{2,1,0:T(8,128)(2,1)S(1)}, bf16[2,72,1536]{2,1,0:T(8,128)(2,1)S(1)}, u32[]{:S(2)}, u32[]{:S(2)}) %collective-permute-start.11) | collective-permute-done | bytes 442400 | tf_op jit(solution)/shard_map/ppermute | solution.py:342
  116.3 1.3 collective-permute-start.15
  117.6 2.2 %shard_map.112 = (bf16[512,4608]{1,0:T(8,128)(2,1)S(1)}, bf16[4608,1536]{1,0:T(8,128)(2,1)S(1)}) custom-call(s32[5]{0:T(128)S(1)} %stack.59.scal, s32[64]{0:T(128)S(1)} %reshape.236.table, bf16[128,4608]{1,0:T(8,128)(2,1)S(1)} %copy-done, bf16[128,4608]{1,0:T(8,128)(2,1)S(1)} %collective-permute-done.19.refs_1_, ...), custom_call_target="tpu_custom_call" | custom-call | bytes 18000000 | tf_op jit(solution)/shard_map/pallas_call | solution.py:132
  119.8 1.2 shard_map.113
  122.0 8.2 %project.1 = (bf16[512,256]{1,0:T(8,128)(2,1)}, bf16[512,256]{1,0:T(8,128)(2,1)}, bf16[64,4608]{1,0:T(8,128)(2,1)S(1)}, bf16[64,4608]{1,0:T(8,128)(2,1)S(1)}, bf16[4608,1536]{1,0:T(8,128)(2,1)S(1)}) custom-call(s32[5]{0:T(128)S(1)} %stack.59.scal, s32[64]{0:T(128)S(1)} %reshape.236.table, ...), custom_call_target="tpu_custom_call", output_to_operand_aliasing={{4}: (9, {})} | custom-call | flops 4000000000 | bytes 10000000 | tf_op jit(solution)/shard_map/project/pallas_call | solution.py:222
  130.2 3.0 %collective-permute-start.33 = (bf16[64,4608]{1,0:T(8,128)(2,1)S(1)}, bf16[64,4608]{1,0:T(8,128)(2,1)S(1)}, u32[]{:S(2)}, u32[]{:S(2)}) collective-permute-start(bf16[64,4608]{1,0:T(8,128)(2,1)S(1)} %get-tuple-element.46), channel_id=1, source_target_pairs={{0,3},{1,0},{2,1},{3,2},{4,7},{5,4},{6,5},{7,6},{8,11},{9,8},{10,9... | collective-permute-start | bytes 1769480 | tf_op jit(solution)/shard_map/ppermute | solution.py:34
  133.1 0.9 copy-done.5
  134.1 0.9 copy-done.7
  135.0 7.7 %shard_map.116 = (bf16[64,4608]{1,0:T(8,128)(2,1)S(1)}, bf16[64,4608]{1,0:T(8,128)(2,1)S(1)}, bf16[64,4608]{1,0:T(8,128)(2,1)S(1)}, bf16[64,4608]{1,0:T(8,128)(2,1)S(1)}) custom-call(s32[5]{0:T(128)S(1)} %stack.59.scal, f32[512,128]{1,0:T(8,128)S(1)} %get-tuple-element.26.cos_ref, f32[512,128]{1,0:T(8,128)S(1)} %get-tuple-element.27.sin_ref, ...), custom_call_target="tpu_custom_call" | custom-call | flops 2800000000 | bytes 3400000 | tf_op jit(solution)/shard_map/pallas_call | solution.py:271
  142.9 2.7 %collective-permute-start.30 = (bf16[64,4608]{1,0:T(8,128)(2,1)S(1)}, bf16[64,4608]{1,0:T(8,128)(2,1)S(1)}, u32[]{:S(2)}, u32[]{:S(2)}) collective-permute-start(bf16[64,4608]{1,0:T(8,128)(2,1)S(1)} %get-tuple-element.42), channel_id=1, source_target_pairs={{0,3},{1,0},{2,1},{3,2},{4,7},{5,4},{6,5},{7,6},{8,11},{9,8},{10,9... | collective-permute-start | bytes 1769480 | tf_op jit(solution)/shard_map/ppermute | solution.py:34
  145.8 1.7 collective-permute-start.34
  147.5 2.2 %collective-permute-done.31 = bf16[64,4608]{1,0:T(8,128)(2,1)S(1)} collective-permute-done((bf16[64,4608]{1,0:T(8,128)(2,1)S(1)}, bf16[64,4608]{1,0:T(8,128)(2,1)S(1)}, u32[]{:S(2)}, u32[]{:S(2)}) %collective-permute-start.31) | collective-permute-done | bytes 589856 | tf_op jit(solution)/shard_map/ppermute | solution.py:34
  150.2 5.1 %shard_map.115.own_ref = bf16[128,4608]{1,0:T(8,128)(2,1)S(1)} custom-call(s32[5]{0:T(128)S(1)} %stack.59.scal, f32[512,128]{1,0:T(8,128)S(1)} %get-tuple-element.26.cos_ref, f32[512,128]{1,0:T(8,128)S(1)} %get-tuple-element.27.sin_ref, bf16[512,256]{1,0:T(8,128)(2,1)S(1)} %copy-done.6, bf16[512,256]{1,0:T(8,128)(2,1)S(1)} %copy-done.8, ...), custom_call_target="tpu_custom_call" | custom-call | flops 1400000000 | bytes 2200000 | tf_op jit(solution)/shard_map/pallas_call | solution.py:271
  155.3 7.0 %collective-permute-done.29.a1 = bf16[64,4608]{1,0:T(8,128)(2,1)S(1)} collective-permute-done((bf16[64,4608]{1,0:T(8,128)(2,1)S(1)}, bf16[64,4608]{1,0:T(8,128)(2,1)S(1)}, u32[]{:S(2)}, u32[]{:S(2)}) %collective-permute-start.29) | collective-permute-done | bytes 589856 | tf_op jit(solution)/shard_map/ppermute | solution.py:34
  162.3 7.4 %collective-permute-done.34.b1_hbm = bf16[64,4608]{1,0:T(8,128)(2,1)S(1)} collective-permute-done((bf16[64,4608]{1,0:T(8,128)(2,1)S(1)}, bf16[64,4608]{1,0:T(8,128)(2,1)S(1)}, u32[]{:S(2)}, u32[]{:S(2)}) %collective-permute-start.34) | collective-permute-done | bytes 589856 | tf_op jit(solution)/shard_map/ppermute | solution.py:34
  169.8 3.0 %collective-permute-done.32.a0_hbm = bf16[64,4608]{1,0:T(8,128)(2,1)S(1)} collective-permute-done((bf16[64,4608]{1,0:T(8,128)(2,1)S(1)}, bf16[64,4608]{1,0:T(8,128)(2,1)S(1)}, u32[]{:S(2)}, u32[]{:S(2)}) %collective-permute-start.32) | collective-permute-done | bytes 589856 | tf_op jit(solution)/shard_map/ppermute | solution.py:34
  172.8 2.6 %finish.1 = bf16[128,4608]{1,0:T(8,128)(2,1)} custom-call(s32[5]{0:T(128)S(1)} %stack.59.scal, bf16[128,4608]{1,0:T(8,128)(2,1)S(1)} %bitcast.47, bf16[128,4608]{1,0:T(8,128)(2,1)S(1)} %shard_map.115.own_ref, bf16[64,4608]{1,0:T(8,128)(2,1)S(1)} %collective-permute-done.29.a1, bf16[64,4608]{1,0:T(8,128)(2,1)S(1)} %collective-permute-done.30.b0, ...), custom_call_target="tpu_custom_call" | custom-call | flops 6000000 | bytes 7000000 | tf_op jit(solution)/shard_map/finish/pallas_call | solution.py:309
  (78 shorter events, 6.8 us)
Async XLA Ops:
  1.6 6.7 %collective-permute-start = (bf16[72,1536]{1,0:T(8,128)(2,1)S(1)}, bf16[72,1536]{1,0:T(8,128)(2,1)S(1)}, u32[]{:S(2)}, u32[]{:S(2)}) collective-permute-start(bf16[72,1536]{1,0:T(8,128)(2,1)S(1)} %get-tuple-element.51), channel_id=1, source_target_pairs={{0,32},{4,12},{8,40},{12,20},{16,48},{20,28},{24,56},{28,4},{32,64... | collective-permute-start | bytes 663560 | tf_op jit(solution)/shard_map/ppermute | solution.py:342
  3.7 5.1 %collective-permute-start.1 = (bf16[72,1536]{1,0:T(8,128)(2,1)S(1)}, bf16[72,1536]{1,0:T(8,128)(2,1)S(1)}, u32[]{:S(2)}, u32[]{:S(2)}) collective-permute-start(bf16[72,1536]{1,0:T(8,128)(2,1)S(1)} %get-tuple-element.51), channel_id=1, source_target_pairs={{0,224},{4,28},{8,232},{12,4},{16,240},{20,12},{24,248},{28,20},{3... | collective-permute-start | bytes 663560 | tf_op jit(solution)/shard_map/ppermute | solution.py:342
  8.3 6.1 %collective-permute-start.2 = (bf16[72,1536]{1,0:T(8,128)(2,1)S(1)}, bf16[72,1536]{1,0:T(8,128)(2,1)}, u32[]{:S(2)}, u32[]{:S(2)}) collective-permute-start(bf16[72,1536]{1,0:T(8,128)(2,1)S(1)} %collective-permute-done), channel_id=1, source_target_pairs={{0,32},{4,12},{8,40},{12,20},{16,48},{20,28},{24,56},{28,4},{32,64... | collective-permute-start | bytes 663560 | tf_op jit(solution)/shard_map/ppermute | solution.py:342
  14.4 9.4 %copy-start.12 = (s32[1,8,4,2]{1,2,3,0:T(4,128)S(1)}, s32[1,8,4,2]{1,2,3,0:T(4,128)}, u32[]{:S(2)}) copy-start(s32[1,8,4,2]{1,2,3,0:T(4,128)} %constant.108) | copy-start | bytes 772
  14.4 9.4 %copy-start.13 = (s32[1,8,4,2]{1,2,3,0:T(4,128)S(1)}, s32[1,8,4,2]{1,2,3,0:T(4,128)}, u32[]{:S(2)}) copy-start(s32[1,8,4,2]{1,2,3,0:T(4,128)} %constant.109) | copy-start | bytes 772
  15.5 28.1 %collective-permute-start.3 = (bf16[4,72,1536]{2,1,0:T(8,128)(2,1)S(1)}, bf16[4,72,1536]{2,1,0:T(8,128)(2,1)S(1)}, u32[]{:S(2)}, u32[]{:S(2)}) collective-permute-start(bf16[4,72,1536]{2,1,0:T(8,128)(2,1)S(1)} %pad_maximum_fusion.refs_3_), channel_id=1, source_target_pairs={{0,24},{4,228},{8,0},{12,236},{16,8},{20,244},{24,16},{28,252},{32... | collective-permute-start | bytes 2654216 | tf_op jit(solution)/shard_map/ppermute | solution.py:342
  21.6 22.8 %collective-permute-start.8 = (bf16[4,72,1536]{2,1,0:T(8,128)(2,1)S(1)}, bf16[4,72,1536]{2,1,0:T(8,128)(2,1)S(1)}, u32[]{:S(2)}, u32[]{:S(2)}) collective-permute-start(bf16[4,72,1536]{2,1,0:T(8,128)(2,1)S(1)} %pad_maximum_fusion.refs_3_), channel_id=1, source_target_pairs={{0,8},{4,36},{8,16},{12,44},{16,24},{20,52},{24,0},{28,60},{32,40}... | collective-permute-start | bytes 2654216 | tf_op jit(solution)/shard_map/ppermute | solution.py:342
  23.4 7.4 %collective-permute-start.4 = (bf16[72,1536]{1,0:T(8,128)(2,1)S(1)}, bf16[72,1536]{1,0:T(8,128)(2,1)S(1)}, u32[]{:S(2)}, u32[]{:S(2)}) collective-permute-start(bf16[72,1536]{1,0:T(8,128)(2,1)S(1)} %collective-permute-done.1), channel_id=1, source_target_pairs={{0,224},{4,28},{8,232},{12,4},{16,240},{20,12},{24,248},{28,20},{3... | collective-permute-start | bytes 663560 | tf_op jit(solution)/shard_map/ppermute | solution.py:342
  31.6 7.3 %collective-permute-start.6 = (bf16[72,1536]{1,0:T(8,128)(2,1)S(1)}, bf16[72,1536]{1,0:T(8,128)(2,1)}, u32[]{:S(2)}, u32[]{:S(2)}) collective-permute-start(bf16[72,1536]{1,0:T(8,128)(2,1)S(1)} %collective-permute-done.4), channel_id=1, source_target_pairs={{0,224},{4,28},{8,232},{12,4},{16,240},{20,12},{24,248},{28,20},{3... | collective-permute-start | bytes 663560 | tf_op jit(solution)/shard_map/ppermute | solution.py:342
  32.6 10.9 %collective-permute-start.5 = (bf16[72,1536]{1,0:T(8,128)(2,1)}, bf16[72,1536]{1,0:T(8,128)(2,1)}, u32[]{:S(2)}, u32[]{:S(2)}) collective-permute-start(bf16[72,1536]{1,0:T(8,128)(2,1)} %collective-permute-done.2), channel_id=1, source_target_pairs={{0,32},{4,12},{8,40},{12,20},{16,48},{20,28},{24,56},{28,4},{32,64... | collective-permute-start | bytes 663560 | tf_op jit(solution)/shard_map/ppermute | solution.py:342
  38.9 5.6 %collective-permute-start.7 = (bf16[72,1536]{1,0:T(8,128)(2,1)}, bf16[72,1536]{1,0:T(8,128)(2,1)}, u32[]{:S(2)}, u32[]{:S(2)}) collective-permute-start(bf16[72,1536]{1,0:T(8,128)(2,1)} %collective-permute-done.6), channel_id=1, source_target_pairs={{0,224},{4,28},{8,232},{12,4},{16,240},{20,12},{24,248},{28,20},{3... | collective-permute-start | bytes 663560 | tf_op jit(solution)/shard_map/ppermute | solution.py:342
  42.2 2.3 %copy-start.11 = (bf16[72,1536]{1,0:T(8,128)(2,1)S(1)}, bf16[72,1536]{1,0:T(8,128)(2,1)}, u32[]{:S(2)}) copy-start(bf16[72,1536]{1,0:T(8,128)(2,1)} %copy-done.10) | copy-start | bytes 663556
  44.5 3.2 %copy-start.2 = (bf16[4,72,1536]{2,1,0:T(8,128)(2,1)}, bf16[4,72,1536]{2,1,0:T(8,128)(2,1)S(1)}, u32[]{:S(2)}) copy-start(bf16[4,72,1536]{2,1,0:T(8,128)(2,1)S(1)} %collective-permute-done.8.refs_4_) | copy-start | bytes 2654212
  47.7 12.4 %collective-permute-start.12 = (bf16[4,72,1536]{2,1,0:T(8,128)(2,1)}, bf16[4,72,1536]{2,1,0:T(8,128)(2,1)S(1)}, u32[]{:S(2)}, u32[]{:S(2)}) collective-permute-start(bf16[4,72,1536]{2,1,0:T(8,128)(2,1)} %get-tuple-element.49), channel_id=1, source_target_pairs={{0,24},{4,228},{8,0},{12,236},{16,8},{20,244},{24,16},{28,252},{32... | collective-permute-start | bytes 2654216 | tf_op jit(solution)/shard_map/ppermute | solution.py:342
  51.7 23.9 %collective-permute-start.19 = (bf16[128,4608]{1,0:T(8,128)(2,1)}, bf16[128,4608]{1,0:T(8,128)(2,1)S(1)}, u32[]{:S(2)}, u32[]{:S(2)}) collective-permute-start(bf16[128,4608]{1,0:T(8,128)(2,1)} %norm.1.refs_0_), channel_id=1, source_target_pairs={{0,3},{1,0},{2,1},{3,2},{4,7},{5,4},{6,5},{7,6},{8,11},{9,8},{10,9... | collective-permute-start | bytes 3538952 | tf_op jit(solution)/shard_map/ppermute | solution.py:34
  54.5 24.6 %collective-permute-start.21 = (bf16[128,4608]{1,0:T(8,128)(2,1)}, bf16[128,4608]{1,0:T(8,128)(2,1)S(1)}, u32[]{:S(2)}, u32[]{:S(2)}) collective-permute-start(bf16[128,4608]{1,0:T(8,128)(2,1)} %norm.1.refs_0_), channel_id=1, source_target_pairs={{0,1},{1,2},{2,3},{3,0},{4,5},{5,6},{6,7},{7,4},{8,9},{9,10},{10,1... | collective-permute-start | bytes 3538952 | tf_op jit(solution)/shard_map/ppermute | solution.py:34
  54.5 26.8 %collective-permute-start.25 = (bf16[4,72,1536]{2,1,0:T(8,128)(2,1)S(1)}, bf16[4,72,1536]{2,1,0:T(8,128)(2,1)S(1)}, u32[]{:S(2)}, u32[]{:S(2)}) collective-permute-start(bf16[4,72,1536]{2,1,0:T(8,128)(2,1)S(1)} %pad_maximum_fusion.refs_3_), channel_id=1, source_target_pairs={{0,4},{4,0},{8,12},{12,8},{16,20},{20,16},{24,28},{28,24},{32,36},... | collective-permute-start | bytes 2654216 | tf_op jit(solution)/shard_map/ppermute | solution.py:30
  59.2 20.1 %collective-permute-start.9 = (bf16[4,72,1536]{2,1,0:T(8,128)(2,1)}, bf16[4,72,1536]{2,1,0:T(8,128)(2,1)S(1)}, u32[]{:S(2)}, u32[]{:S(2)}) collective-permute-start(bf16[4,72,1536]{2,1,0:T(8,128)(2,1)} %get-tuple-element.48), channel_id=1, source_target_pairs={{0,8},{4,36},{8,16},{12,44},{16,24},{20,52},{24,0},{28,60},{32,40}... | collective-permute-start | bytes 2654216 | tf_op jit(solution)/shard_map/ppermute | solution.py:342
  60.2 21.1 %copy-start.4 = (bf16[4,72,1536]{2,1,0:T(8,128)(2,1)S(1)}, bf16[4,72,1536]{2,1,0:T(8,128)(2,1)}, u32[]{:S(2)}) copy-start(bf16[4,72,1536]{2,1,0:T(8,128)(2,1)} %get-tuple-element.47.refs_11_) | copy-start | bytes 2654212
  60.2 33.3 %copy-start.3 = (bf16[4,72,1536]{2,1,0:T(8,128)(2,1)S(1)}, bf16[4,72,1536]{2,1,0:T(8,128)(2,1)}, u32[]{:S(2)}) copy-start(bf16[4,72,1536]{2,1,0:T(8,128)(2,1)} %copy-done.2) | copy-start | bytes 2654212
  60.2 36.7 %collective-permute-start.13 = (bf16[4,72,1536]{2,1,0:T(8,128)(2,1)S(1)}, bf16[4,72,1536]{2,1,0:T(8,128)(2,1)S(1)}, u32[]{:S(2)}, u32[]{:S(2)}) collective-permute-start(bf16[4,72,1536]{2,1,0:T(8,128)(2,1)S(1)} %broadcast_select_fusion), channel_id=1, source_target_pairs={{0,24},{4,228},{8,0},{12,236},{16,8},{20,244},{24,16},{28,252},{32... | collective-permute-start | bytes 2654216 | tf_op jit(solution)/shard_map/ppermute | solution.py:342
  75.7 11.6 %collective-permute-start.20 = (bf16[64,4608]{1,0:T(8,128)(2,1)S(1)}, bf16[64,4608]{1,0:T(8,128)(2,1)S(1)}, u32[]{:S(2)}, u32[]{:S(2)}) collective-permute-start(bf16[64,4608]{1,0:T(8,128)(2,1)S(1)} %slice.48), channel_id=1, source_target_pairs={{0,3},{1,0},{2,1},{3,2},{4,7},{5,4},{6,5},{7,6},{8,11},{9,8},{10,9... | collective-permute-start | bytes 1769480 | tf_op jit(solution)/shard_map/ppermute | solution.py:34
  79.1 38.4 %copy-start = (bf16[128,4608]{1,0:T(8,128)(2,1)S(1)}, bf16[128,4608]{1,0:T(8,128)(2,1)}, u32[]{:S(2)}) copy-start(bf16[128,4608]{1,0:T(8,128)(2,1)} %norm.1.refs_0_) | copy-start | bytes 3538948
  79.2 14.3 %collective-permute-start.22 = (bf16[64,4608]{1,0:T(8,128)(2,1)S(1)}, bf16[64,4608]{1,0:T(8,128)(2,1)S(1)}, u32[]{:S(2)}, u32[]{:S(2)}) collective-permute-start(bf16[64,4608]{1,0:T(8,128)(2,1)S(1)} %slice.49), channel_id=1, source_target_pairs={{0,1},{1,2},{2,3},{3,0},{4,5},{5,6},{6,7},{7,4},{8,9},{9,10},{10,1... | collective-permute-start | bytes 1769480 | tf_op jit(solution)/shard_map/ppermute | solution.py:34
  79.3 17.8 %collective-permute-start.10 = (bf16[4,72,1536]{2,1,0:T(8,128)(2,1)S(1)}, bf16[4,72,1536]{2,1,0:T(8,128)(2,1)S(1)}, u32[]{:S(2)}, u32[]{:S(2)}) collective-permute-start(bf16[4,72,1536]{2,1,0:T(8,128)(2,1)S(1)} %collective-permute-done.9.refs_6_), channel_id=1, source_target_pairs={{0,8},{4,36},{8,16},{12,44},{16,24},{20,52},{24,0},{28,60},{32,40}... | collective-permute-start | bytes 2654216 | tf_op jit(solution)/shard_map/ppermute | solution.py:342
  81.3 18.8 %collective-permute-start.28 = (bf16[4,72,1536]{2,1,0:T(8,128)(2,1)S(1)}, bf16[4,72,1536]{2,1,0:T(8,128)(2,1)S(1)}, u32[]{:S(2)}, u32[]{:S(2)}) collective-permute-start(bf16[4,72,1536]{2,1,0:T(8,128)(2,1)S(1)} %copy-done.4), channel_id=1, source_target_pairs={{0,4},{8,12},{16,20},{24,28},{32,36},{40,44},{48,52},{56,60},{64,6... | collective-permute-start | bytes 2654216 | tf_op jit(solution)/shard_map/ppermute | solution.py:347
  87.3 12.8 %collective-permute-start.27 = (bf16[4,72,1536]{2,1,0:T(8,128)(2,1)S(1)}, bf16[4,72,1536]{2,1,0:T(8,128)(2,1)S(1)}, u32[]{:S(2)}, u32[]{:S(2)}) collective-permute-start(bf16[4,72,1536]{2,1,0:T(8,128)(2,1)S(1)} %collective-permute-done.3.refs_5_), channel_id=1, source_target_pairs={{0,4},{4,0},{8,12},{12,8},{16,20},{20,16},{24,28},{28,24},{32,36},... | collective-permute-start | bytes 2654216 | tf_op jit(solution)/shard_map/ppermute | solution.py:30
  93.5 7.2 %collective-permute-start.26 = (bf16[4,72,1536]{2,1,0:T(8,128)(2,1)S(1)}, bf16[4,72,1536]{2,1,0:T(8,128)(2,1)S(1)}, u32[]{:S(2)}, u32[]{:S(2)}) collective-permute-start(bf16[4,72,1536]{2,1,0:T(8,128)(2,1)S(1)} %copy-done.3), channel_id=1, source_target_pairs={{0,4},{4,0},{8,12},{12,8},{16,20},{20,16},{24,28},{28,24},{32,36},... | collective-permute-start | bytes 2654216 | tf_op jit(solution)/shard_map/ppermute | solution.py:30
  96.9 9.1 %collective-permute-start.23 = (bf16[4,72,1536]{2,1,0:T(8,128)(2,1)S(1)}, bf16[4,72,1536]{2,1,0:T(8,128)(2,1)S(1)}, u32[]{:S(2)}, u32[]{:S(2)}) collective-permute-start(bf16[4,72,1536]{2,1,0:T(8,128)(2,1)S(1)} %collective-permute-done.9.refs_6_), channel_id=1, source_target_pairs={{0,4},{4,0},{8,12},{12,8},{16,20},{20,16},{24,28},{28,24},{32,36},... | collective-permute-start | bytes 2654216 | tf_op jit(solution)/shard_map/ppermute | solution.py:30
  97.1 22.7 %collective-permute-start.24 = (bf16[4,72,1536]{2,1,0:T(8,128)(2,1)S(1)}, bf16[4,72,1536]{2,1,0:T(8,128)(2,1)S(1)}, u32[]{:S(2)}, u32[]{:S(2)}) collective-permute-start(bf16[4,72,1536]{2,1,0:T(8,128)(2,1)S(1)} %collective-permute-done.12.refs_7_), channel_id=1, source_target_pairs={{0,4},{4,0},{8,12},{12,8},{16,20},{20,16},{24,28},{28,24},{32,36},... | collective-permute-start | bytes 2654216 | tf_op jit(solution)/shard_map/ppermute | solution.py:30
  100.1 21.0 %collective-permute-start.18 = (bf16[4,72,1536]{2,1,0:T(8,128)(2,1)S(1)}, bf16[4,72,1536]{2,1,0:T(8,128)(2,1)S(1)}, u32[]{:S(2)}, u32[]{:S(2)}) collective-permute-start(bf16[4,72,1536]{2,1,0:T(8,128)(2,1)S(1)} %collective-permute-done.13.refs_3_), channel_id=1, source_target_pairs={{0,4},{4,0},{8,12},{12,8},{16,20},{20,16},{24,28},{28,24},{32,36},... | collective-permute-start | bytes 2654216 | tf_op jit(solution)/shard_map/ppermute | solution.py:30
  100.2 20.9 %collective-permute-start.17 = (bf16[4,72,1536]{2,1,0:T(8,128)(2,1)S(1)}, bf16[4,72,1536]{2,1,0:T(8,128)(2,1)S(1)}, u32[]{:S(2)}, u32[]{:S(2)}) collective-permute-start(bf16[4,72,1536]{2,1,0:T(8,128)(2,1)S(1)} %collective-permute-done.10.refs_2_), channel_id=1, source_target_pairs={{0,4},{4,0},{8,12},{12,8},{16,20},{20,16},{24,28},{28,24},{32,36},... | collective-permute-start | bytes 2654216 | tf_op jit(solution)/shard_map/ppermute | solution.py:30
  100.7 10.6 %collective-permute-start.14 = (bf16[2,72,1536]{2,1,0:T(8,128)(2,1)S(1)}, bf16[2,72,1536]{2,1,0:T(8,128)(2,1)S(1)}, u32[]{:S(2)}, u32[]{:S(2)}) collective-permute-start(bf16[2,72,1536]{2,1,0:T(8,128)(2,1)S(1)} %slice.47), channel_id=1, source_target_pairs={{4,228},{12,236},{20,244},{28,252},{36,4},{44,12},{52,20},{60,28},... | collective-permute-start | bytes 1327112 | tf_op jit(solution)/shard_map/ppermute | solution.py:342
  106.0 10.3 %collective-permute-start.11 = (bf16[2,72,1536]{2,1,0:T(8,128)(2,1)S(1)}, bf16[2,72,1536]{2,1,0:T(8,128)(2,1)S(1)}, u32[]{:S(2)}, u32[]{:S(2)}) collective-permute-start(bf16[2,72,1536]{2,1,0:T(8,128)(2,1)S(1)} %slice.46), channel_id=1, source_target_pairs={{4,36},{12,44},{20,52},{28,60},{36,68},{44,76},{52,84},{60,92},{68... | collective-permute-start | bytes 1327112 | tf_op jit(solution)/shard_map/ppermute | solution.py:342
  111.2 10.7 %collective-permute-start.16 = (bf16[2,72,1536]{2,1,0:T(8,128)(2,1)S(1)}, bf16[2,72,1536]{2,1,0:T(8,128)(2,1)S(1)}, u32[]{:S(2)}, u32[]{:S(2)}) collective-permute-start(bf16[2,72,1536]{2,1,0:T(8,128)(2,1)S(1)} %collective-permute-done.14.down_own), channel_id=1, source_target_pairs={{4,0},{12,8},{20,16},{28,24},{36,32},{44,40},{52,48},{60,56},{68,6... | collective-permute-start | bytes 1327112 | tf_op jit(solution)/shard_map/ppermute | solution.py:347
  116.3 5.7 %collective-permute-start.15 = (bf16[2,72,1536]{2,1,0:T(8,128)(2,1)S(1)}, bf16[2,72,1536]{2,1,0:T(8,128)(2,1)S(1)}, u32[]{:S(2)}, u32[]{:S(2)}) collective-permute-start(bf16[2,72,1536]{2,1,0:T(8,128)(2,1)S(1)} %collective-permute-done.11.up_own), channel_id=1, source_target_pairs={{4,0},{12,8},{20,16},{28,24},{36,32},{44,40},{52,48},{60,56},{68,6... | collective-permute-start | bytes 1327112 | tf_op jit(solution)/shard_map/ppermute | solution.py:347
  130.2 15.4 %collective-permute-start.33 = (bf16[64,4608]{1,0:T(8,128)(2,1)S(1)}, bf16[64,4608]{1,0:T(8,128)(2,1)S(1)}, u32[]{:S(2)}, u32[]{:S(2)}) collective-permute-start(bf16[64,4608]{1,0:T(8,128)(2,1)S(1)} %get-tuple-element.46), channel_id=1, source_target_pairs={{0,3},{1,0},{2,1},{3,2},{4,7},{5,4},{6,5},{7,6},{8,11},{9,8},{10,9... | collective-permute-start | bytes 1769480 | tf_op jit(solution)/shard_map/ppermute | solution.py:34
  133.1 16.6 %collective-permute-start.31 = (bf16[64,4608]{1,0:T(8,128)(2,1)S(1)}, bf16[64,4608]{1,0:T(8,128)(2,1)S(1)}, u32[]{:S(2)}, u32[]{:S(2)}) collective-permute-start(bf16[64,4608]{1,0:T(8,128)(2,1)S(1)} %get-tuple-element.44), channel_id=1, source_target_pairs={{0,1},{1,2},{2,3},{3,0},{4,5},{5,6},{6,7},{7,4},{8,9},{9,10},{10,1... | collective-permute-start | bytes 1769480 | tf_op jit(solution)/shard_map/ppermute | solution.py:34
  133.1 1.0 copy-start.5
  134.1 0.9 copy-start.7
  142.8 19.6 %collective-permute-start.29 = (bf16[64,4608]{1,0:T(8,128)(2,1)S(1)}, bf16[64,4608]{1,0:T(8,128)(2,1)S(1)}, u32[]{:S(2)}, u32[]{:S(2)}) collective-permute-start(bf16[64,4608]{1,0:T(8,128)(2,1)S(1)} %get-tuple-element.41), channel_id=1, source_target_pairs={{0,1},{1,2},{2,3},{3,0},{4,5},{5,6},{6,7},{7,4},{8,9},{9,10},{10,1... | collective-permute-start | bytes 1769480 | tf_op jit(solution)/shard_map/ppermute | solution.py:34
  142.9 19.5 %collective-permute-start.30 = (bf16[64,4608]{1,0:T(8,128)(2,1)S(1)}, bf16[64,4608]{1,0:T(8,128)(2,1)S(1)}, u32[]{:S(2)}, u32[]{:S(2)}) collective-permute-start(bf16[64,4608]{1,0:T(8,128)(2,1)S(1)} %get-tuple-element.42), channel_id=1, source_target_pairs={{0,3},{1,0},{2,1},{3,2},{4,7},{5,4},{6,5},{7,6},{8,11},{9,8},{10,9... | collective-permute-start | bytes 1769480 | tf_op jit(solution)/shard_map/ppermute | solution.py:34
  145.7 4.5 %copy-start.6 = (bf16[512,256]{1,0:T(8,128)(2,1)S(1)}, bf16[512,256]{1,0:T(8,128)(2,1)}, u32[]{:S(2)}) copy-start(bf16[512,256]{1,0:T(8,128)(2,1)} %get-tuple-element.38.k_ref) | copy-start | bytes 786436
  145.8 4.5 %copy-start.8 = (bf16[512,256]{1,0:T(8,128)(2,1)S(1)}, bf16[512,256]{1,0:T(8,128)(2,1)}, u32[]{:S(2)}) copy-start(bf16[512,256]{1,0:T(8,128)(2,1)} %get-tuple-element.39.v_ref) | copy-start | bytes 786436
  145.8 24.0 %collective-permute-start.34 = (bf16[64,4608]{1,0:T(8,128)(2,1)S(1)}, bf16[64,4608]{1,0:T(8,128)(2,1)S(1)}, u32[]{:S(2)}, u32[]{:S(2)}) collective-permute-start(bf16[64,4608]{1,0:T(8,128)(2,1)S(1)} %add_convert_fusion), channel_id=1, source_target_pairs={{0,3},{1,0},{2,1},{3,2},{4,7},{5,4},{6,5},{7,6},{8,11},{9,8},{10,9... | collective-permute-start | bytes 1769480 | tf_op jit(solution)/shard_map/ppermute | solution.py:34
  149.8 23.0 %copy-start.1 = (bf16[1,128,4608]{2,1,0:T(8,128)(2,1)S(1)}, bf16[1,128,4608]{2,1,0:T(8,128)(2,1)}, u32[]{:S(2)}) copy-start(bf16[1,128,4608]{2,1,0:T(8,128)(2,1)} %param.9) | copy-start | bytes 3538948
  149.9 22.9 %copy-start.9 = (f32[4608]{0:T(1024)S(1)}, f32[4608]{0:T(1024)}, u32[]{:S(2)}) copy-start(f32[4608]{0:T(1024)} %gain_ref.3) | copy-start | bytes 55300
  149.9 22.9 %collective-permute-start.32 = (bf16[64,4608]{1,0:T(8,128)(2,1)S(1)}, bf16[64,4608]{1,0:T(8,128)(2,1)S(1)}, u32[]{:S(2)}, u32[]{:S(2)}) collective-permute-start(bf16[64,4608]{1,0:T(8,128)(2,1)S(1)} %add_convert_fusion.1), channel_id=1, source_target_pairs={{0,1},{1,2},{2,3},{3,0},{4,5},{5,6},{6,7},{7,4},{8,9},{9,10},{10,1... | collective-permute-start | bytes 1769480 | tf_op jit(solution)/shard_map/ppermute | solution.py:34
  (1 other events, 0.7 us)
